TPU v7x, 256 devices: a whole 4x4x8 slice. The times are simulated.
256 devices in a mesh: section: 4 (over x), dp: 4 (over y), chan: 16 (over z, core).
Axes of the slice: x: 4, y: 4, z: 8, core: 2. Of those that a mesh axis runs over, the one named last changes fastest.
Arguments:
- feats: bfloat16 [8, 32, 128, 2048], P('dp', None, None, 'chan'), may hold values from -6 to 6
- offsets: int32 [8], P('dp'), may hold values from 0 to 127
- widths: int32 [8], P('dp'), may hold values from 32 to 64
- labels: int32 [8, 32, 128], P('dp'), may hold values from 0 to 19
- dw_kernel: bfloat16 [4, 9, 2048], P('section', None, 'chan'), may hold values from -2 to 2
- pw_weight: bfloat16 [4, 2048, 256], P('section', 'chan'), may hold values from -0.125 to 0.125
- pw_bias: float32 [4, 256], P('section', 'chan'), may hold values from -3 to 3
- proj: bfloat16 [4, 256, 256], P('section', 'chan'), may hold values from -0.1875 to 0.1875
- proj_bias: float32 [256], P('chan'), may hold values from -3 to 3
- upstream: bfloat16 [256, 8, 32, 128], P('chan', 'dp'), may hold values from -6 to 6
Outputs:
- aspp_out: bfloat16 [256, 8, 32, 128], P('chan', 'dp')
- input_grad: bfloat16 [8, 32, 128, 2048], P('dp', 'section', None, 'chan')
- grad_dw: float32 [4, 9, 2048], P('section', None, 'chan')
- grad_pw: float32 [4, 2048, 256], P('section', 'chan')
- grad_pw_bias: float32 [4, 256], P('section', 'chan')
- grad_proj: float32 [4, 256, 256], P('section', 'chan')
- grad_proj_bias: float32 [256], P('chan')
All inputs are finite; a program needn't handle non-finite values.
Results may differ from a plain program's by a relative error of at most 0.008.
Values may be sent and summed in bfloat16 or wider, within the bound.
No kernel may reach another device: no remote copies, remote signals or barrier semaphores. Data moves between devices by JAX's collectives and lax.ppermute only.
A program may use at most 128 MiB of HBM per device.

v0:
```python
import math

import jax
import jax.numpy as jnp
from jax import lax
from jax.experimental import pallas as pl
from jax.experimental.pallas import tpu as pltpu
from jax.sharding import Mesh, PartitionSpec as P

RATE = 6
VOID = 19
BF = jnp.bfloat16
F32 = jnp.float32

WIN = (32, 48, 48, 64)
BEG = (0, -8, -8, -16)
SOFF = (0, 32, 80, 128)
NCOL = 192
PADC = 32
PADR = 9
VM = 56 * 1024 * 1024


def shift(x, axis, k):
    n = lax.axis_size(axis)
    return lax.ppermute(x, axis, [(i, (i + k) % n) for i in range(n)])


def gather_rel(x, axis):
    n = lax.axis_size(axis)
    return [x] + [shift(x, axis, k) for k in range(1, n)]


def dotf(a, b, dims=((1,), (0,))):
    return lax.dot_general(a, b, (dims, ((), ())), preferred_element_type=F32)


def back(a, k):
    return lax.rem(a - k + 4, 4)


def blocks(sc):
    for k in range(4):
        for zr in range(2):
            for cr in range(2):
                yield k, zr, cr, 4 * back(sc[2], k) + 2 * jnp.bitwise_xor(sc[3], zr) + jnp.bitwise_xor(sc[4], cr)


def perm_matrix(off, transpose=False):
    w = lax.broadcasted_iota(jnp.int32, (128, 128), 1 if transpose else 0)
    x = lax.broadcasted_iota(jnp.int32, (128, 128), 0 if transpose else 1)
    col = 2 * (jnp.bitwise_and(x, 63) - 16) + jnp.right_shift(x, 6)
    return jnp.where(jnp.bitwise_and(w - off, 127) == jnp.bitwise_and(col, 127), 1.0, 0.0).astype(BF)


def pack_kernel(sc, off, wid, pw, dw, proj, pwb, pb, out):
    rows = pl.ds(pl.multiple_of(32 * sc[5], 32), 32)
    out[0:32, :] = pw[0, rows, 0:128]
    out[32:64, :] = pw[0, rows, 128:256]
    out[64:80, :] = proj[0, :, 0:128]
    out[80:96, :] = proj[0, :, 128:256]
    i = lax.broadcasted_iota(jnp.int32, (16, 16), 0)
    j = lax.broadcasted_iota(jnp.int32, (16, 16), 1)
    lane = lax.broadcasted_iota(jnp.int32, (16, 128), 1)
    ext = jnp.zeros((16, 128), F32)
    for n, b in enumerate((pwb, pb)):
        rest = jnp.sum(jnp.where(i == j, b[...], 0.0), axis=1, keepdims=True)
        for piece in range(3):
            part = rest.astype(BF).astype(F32)
            ext = ext + jnp.where(lane == 3 * n + piece, part, 0.0)
            rest = rest - part
    out[96:112, :] = ext.astype(BF)
    taps = jnp.concatenate([dw[0].astype(F32), jnp.zeros((7, 128), F32)], axis=0)
    out[112:128, :] = taps.astype(BF)


def select_kernel(sc, off, wid, x, up, o0, o1, o2, o3, uscr):
    for f in range(2):
        res = dotf(up[f].reshape(128, 128), perm_matrix(off[f]))
        for p in range(2):
            uscr[2 * f + p] = res[:, 64 * p:64 * p + 64].reshape(8, 16, 64)
    for k, o in enumerate((o0, o1, o2, o3)):
        dest = lax.rem(sc[2] + k, 4)
        f, p = dest // 2, lax.rem(dest, 2)
        w = lax.broadcasted_iota(jnp.int32, (32, 128), 1)
        tgt = 2 * lax.broadcasted_iota(jnp.int32, (32, 128), 0) + p
        hot = jnp.where((jnp.bitwise_and(w - off[f], 127) == tgt) & (tgt < wid[f]), 1.0, 0.0).astype(BF)

        def body(t, _, o=o, hot=hot, f=f):
            o[pl.ds(pl.multiple_of(32 * t, 32), 32), :] = dotf(hot, x[f, t, 0]).astype(BF)
            return 0

        lax.fori_loop(0, 16, body, 0, unroll=8)
        for zr in range(2):
            for cr in range(2):
                t0 = 4 * jnp.bitwise_xor(sc[4], cr) + 2 * jnp.bitwise_xor(sc[3], zr)
                row = 512 + 32 * zr + 16 * cr
                o[row:row + 16, :] = jnp.concatenate([uscr[dest, t0], uscr[dest, t0 + 1]], axis=1).astype(BF)


def edge_masks(s, off, cp):
    n = WIN[s]
    u = lax.broadcasted_iota(jnp.int32, (n, 128), 0) + BEG[s]
    w = jnp.bitwise_and(off + 2 * u + cp, 127)
    return w >= RATE * s, w < 128 - RATE * s


def fill_x(xs, xscr):
    xscr[...] = jnp.zeros(xscr.shape, F32)
    for k in range(4):
        def body(t, _, k=k):
            xscr[k, PADR + t, PADC:PADC + 32, :] = xs[k][pl.ds(pl.multiple_of(32 * t, 32), 32), :].astype(F32)
            return 0
        lax.fori_loop(0, 16, body, 0, unroll=4)


def depth_kernel(sc, off, wid, x0, x1, x2, x3, a0, a1, a2, a3, depth, dws, xscr):
    hf, f, cp = sc[0], sc[2] // 2, lax.rem(sc[2], 2)
    col = off[f]
    fill_x((x0, x1, x2, x3), xscr)
    for k, a in enumerate((a0, a1, a2, a3)):
        for r in range(4):
            dws[k, back(sc[1], r)] = a[r, 112:128, :].astype(F32)

    def body(i, _):
        k = i // 8
        t = lax.rem(i, 8)
        base = 8 * hf + t + PADR
        total = jnp.sum(dws[k, 0, 0:9, :], axis=0, keepdims=True)
        depth[k, t, 0:32, :] = (xscr[k, base, PADC:PADC + 32, :] * total).astype(BF)
        for s in range(1, 4):
            n = WIN[s]
            parts = []
            for j in range(3):
                c0 = PADC + BEG[s] + 3 * s * (j - 1)
                acc = None
                for a in range(3):
                    v = xscr[k, base + 3 * s * (a - 1), c0:c0 + n, :] * dws[k, s, 3 * a + j:3 * a + j + 1, :]
                    acc = v if acc is None else acc + v
                parts.append(acc)
            left, right = edge_masks(s, col, cp)
            out = parts[1] + jnp.where(left, parts[0], 0.0) + jnp.where(right, parts[2], 0.0)
            depth[k, t, SOFF[s]:SOFF[s] + n, :] = out.astype(BF)
        return 0

    lax.fori_loop(0, 32, body, 0)


def product_kernel(sc, off, wid, depth, q0, q1, q2, q3, keep, send, wfull, pscr):
    mz, mc = sc[3], sc[4]
    for j, qj in enumerate((q0, q1, q2, q3)):
        rows = pl.ds(pl.multiple_of(32 * back(sc[5], j), 32), 32)
        for k in range(4):
            for r in range(4):
                s = back(sc[1], r)
                wfull[k, s, rows, 0:128] = qj[k, r, 0:32, :]
                wfull[k, s, rows, 128:256] = qj[k, r, 32:64, :]
    for s in range(4):
        n = WIN[s]
        acc = None
        for k in range(0, 4, 2):
            lhs = jnp.concatenate(
                [depth[k + d, :, SOFF[s]:SOFF[s] + n, :].reshape(8 * n, 128) for d in range(2)], axis=1)
            rhs = jnp.concatenate([wfull[k, s], wfull[k + 1, s]], axis=0)
            v = dotf(lhs, rhs)
            acc = v if acc is None else acc + v
        pscr[:, SOFF[s]:SOFF[s] + n, :] = acc.reshape(8, n, 256)
    for zr in range(2):
        zz = 2 * jnp.bitwise_xor(mz, zr)
        for r in range(2):
            keep[zr, r] = pscr[4 * mc + zz + r]
            send[zr, r] = pscr[4 * (1 - mc) + zz + r].astype(BF)


def middle_kernel(sc, off, wid, keep, rcore, rzl, pj, zin, cin, f0, f1, f2, f3, labels,
                  zout, res0, gkeep, gsend, pjs, upscr, gscr):
    q, zh, mz, mc = sc[1], sc[2], sc[3], sc[4]
    fs = (f0, f1, f2, f3)
    for k, zr, cr, blk in blocks(sc):
        rows = pl.ds(pl.multiple_of(16 * blk, 16), 16)
        for r in range(4):
            s = back(q, r)
            base = 48 * (4 * k + r)
            for b in range(3):
                at = base + 16 * b
                if zr == 0 and cr == 0:
                    v = pj[k, r, 16 * b:16 * b + 16, :]
                elif cr == 0:
                    v = zin[at:at + 16, :]
                else:
                    v = cin[768 * zr + at:768 * zr + at + 16, :]
                pjs[s, rows, 128 * b:128 * b + 128] = v
        if zr == 0 and cr == 0:
            u = fs[k][512:528, :]
        elif cr == 0:
            u = zin[768 + 32 * k:784 + 32 * k, :]
        else:
            u = cin[1536 + 64 * zr + 16 * k:1552 + 64 * zr + 16 * k, :]
        upscr[rows, :] = u.astype(F32)
    frame, cp = zh // 2, lax.rem(zh, 2)
    w = lax.broadcasted_iota(jnp.int32, (64, 128), 1)
    v = lax.broadcasted_iota(jnp.int32, (64, 128), 0)
    hot = jnp.bitwise_and(w - off[frame], 127) == jnp.bitwise_and(2 * (v - 16) + cp, 127)
    cols = []
    for r in range(2):
        row = 2 * (8 * sc[0] + 4 * mc + 2 * mz + r) + sc[6]
        lrow = labels[frame, pl.ds(row, 1), :]
        cols.append(jnp.sum(jnp.where(hot & (lrow != VOID), 1.0, 0.0), axis=1, keepdims=True))
    lab = jnp.concatenate(cols, axis=0)

    lane = lax.broadcasted_iota(jnp.int32, (8, 128), 1)
    pre_now = keep[0] + rcore[0].astype(F32) + rzl[...].astype(F32)
    pres, acts = [], []
    z = dotf(jnp.where((lane >= 3) & (lane < 6), 1.0, 0.0).astype(BF), pjs[0, :, 256:384], ((1,), (1,)))[0:1, :]
    for s in range(4):
        n, v0 = WIN[s], BEG[s] + 16
        bias = dotf(jnp.where(lane < 3, 1.0, 0.0).astype(BF), pjs[s, :, 256:384], ((1,), (1,)))[0:1, :]
        body = pre_now[:, SOFF[s]:SOFF[s] + n, :]
        if n < 64:
            body = jnp.concatenate(
                [jnp.zeros((2, v0, 256), F32), body, jnp.zeros((2, 64 - n - v0, 256), F32)], axis=1)
        pre = body.reshape(128, 256) + bias
        act = (pre * jax.nn.sigmoid(pre)).astype(BF)
        z = z + dotf(act, pjs[s, :, 0:256])
        pres.append(pre)
        acts.append(act)
    sig = jax.nn.sigmoid(z)
    res_t = jnp.transpose(z * sig)
    up = jnp.transpose(upscr[...])
    og = (up * (sig * (1.0 + z * (1.0 - sig))) * lab).astype(BF)
    ones = jnp.full((128, 128), 1.0, BF)
    half = lax.broadcasted_iota(jnp.int32, (256, 128), 1) < 64
    pbg = dotf(og, ones, ((0,), (0,)))
    for s in range(4):
        n, v0 = WIN[s], BEG[s] + 16
        pre = pres[s]
        sg = jax.nn.sigmoid(pre)
        ag = dotf(og, pjs[s, :, 0:256], ((1,), (1,)))
        pgs = (ag * (sg * (1.0 + pre * (1.0 - sg)))).astype(BF)
        for b in range(2):
            for r in range(2):
                at = 384 * b + 192 * r + SOFF[s]
                zout[at:at + n, :] = pgs[64 * r + v0:64 * r + v0 + n, 128 * b:128 * b + 128]
        gscr[s, :, 0:256] = dotf(acts[s], og, ((0,), (0,)))
        gscr[s, :, 256:384] = jnp.where(half, dotf(pgs, ones, ((0,), (0,))), pbg)
    upscr[...] = res_t
    for k, zr, cr, blk in blocks(sc):
        rows = pl.ds(pl.multiple_of(16 * blk, 16), 16)
        at = 64 * cr + 16 * k
        if zr == 0:
            res0[at:at + 16, :] = upscr[rows, :].astype(BF)
        else:
            zout[768 + at:784 + at, :] = upscr[rows, :].astype(BF)
        for r in range(4):
            g = gscr[lax.rem(q + r, 4), rows, :]
            if cr == 0:
                gkeep[zr, r, k] = g
            else:
                gsend[zr, r, k] = g.astype(BF)


def weight_kernel(sc, off, wid, depth, zout, zin, cin, g0, g1, g2, g3, pgs, gbuf):
    mz, mc = sc[3], sc[4]
    for zr in range(2):
        for cr in range(2):
            t0 = 4 * jnp.bitwise_xor(mc, cr) + 2 * jnp.bitwise_xor(mz, zr)
            src, at0 = (cin, 768 * zr) if cr == 1 else ((zout, 0) if zr == 0 else (zin, 0))
            for r in range(2):
                for b in range(2):
                    at = at0 + 384 * b + 192 * r
                    pgs[t0 + r, :, 128 * b:128 * b + 128] = src[at:at + 192, :]
    for s in range(4):
        n = WIN[s]
        pg = pgs[:, SOFF[s]:SOFF[s] + n, :].reshape(8 * n, 256)
        for k in range(4):
            dep = depth[k, :, SOFF[s]:SOFF[s] + n, :].reshape(8 * n, 128)
            g = dotf(dep, pg, ((0,), (0,)))
            gbuf[s, k, 0:128, :] = g[:, 0:128].astype(BF)
            gbuf[s, k, 128:256, :] = g[:, 128:256].astype(BF)
    for r, g in enumerate((g0, g1, g2, g3)):
        g[...] = gbuf[lax.rem(sc[1] + r, 4)]


def backward_kernel(sc, off, wid, x0, x1, x2, x3, wfull, dws, pgs, gpr, res0, zin, cin,
                    o0, o1, o2, o3, xscr, dgs, yscr, dwa):
    hf, q, f, cp = sc[0], sc[1], sc[2] // 2, lax.rem(sc[2], 2)
    col = off[f]
    fill_x((x0, x1, x2, x3), xscr)
    for s in range(4):
        n = WIN[s]
        pg = pgs[:, SOFF[s]:SOFF[s] + n, :].reshape(8 * n, 256)
        for k in range(4):
            dgk = dotf(pg, wfull[k, s], ((1,), (1,))).astype(BF).astype(F32)
            dgs[k, :, SOFF[s]:SOFF[s] + n, :] = dgk.reshape(8, n, 128)
    yscr[...] = jnp.zeros(yscr.shape, F32)
    dwa[...] = jnp.zeros(dwa.shape, F32)

    def fold(v):
        n = v.shape[0]
        acc = v[0:8]
        for c in range(8, n, 8):
            acc = acc + v[c:c + 8]
        return acc

    def body(i, _):
        k = i // 8
        t = lax.rem(i, 8)
        base = 8 * hf + t + PADR
        d0 = dgs[k, t, 0:32, :]
        total = jnp.sum(dws[k, 0, 0:9, :], axis=0, keepdims=True)
        dwa[k, 0, 0:8, :] += fold(d0 * xscr[k, base, PADC:PADC + 32, :])
        yscr[k, t + PADR] += d0 * total
        for s in range(1, 4):
            n = WIN[s]
            left, right = edge_masks(s, col, cp)
            d = dgs[k, t, SOFF[s]:SOFF[s] + n, :]
            ds3 = (jnp.where(left, d, 0.0), d, jnp.where(right, d, 0.0))
            for a in range(3):
                for j in range(3):
                    c0 = PADC + BEG[s] + 3 * s * (j - 1)
                    v = fold(ds3[j] * xscr[k, base + 3 * s * (a - 1), c0:c0 + n, :])
                    tap = 9 * s + 3 * a + j - 8
                    dwa[k, tap, 0:8, :] += v
            acc = [None, None, None]
            for j in range(3):
                c1 = -BEG[s] - 3 * s * (j - 1)
                dv = ds3[j][c1:c1 + 32]
                for a in range(3):
                    v = dv * dws[k, s, 3 * a + j:3 * a + j + 1, :]
                    acc[a] = v if acc[a] is None else acc[a] + v
            for a in range(3):
                yscr[k, t + PADR + 3 * s * (a - 1)] += acc[a]
        return 0

    lax.fori_loop(0, 32, body, 0)
    for k in range(4):
        for s in range(4):
            rows = []
            for tap in range(9):
                src = 0 if s == 0 else 9 * s + tap - 8
                rows.append(jnp.sum(dwa[k, src], axis=0, keepdims=True))
            rows.append(jnp.zeros((7, 128), F32))
            dws_sum = jnp.concatenate(rows, axis=0)
            dwa[k, 28 + 2 * s] = dws_sum[0:8]
            dwa[k, 29 + 2 * s] = dws_sum[8:16]
    for r, o in enumerate((o0, o1, o2, o3)):
        dest = lax.rem(q + r, 4)
        for k in range(4):
            for b in range(4):
                at = 128 * k + 32 * b
                o[at:at + 32, :] = yscr[k, PADR - 8 * hf + 4 * dest + b].astype(BF)
            o[512 + 16 * k:528 + 16 * k, :] = jnp.concatenate(
                [dwa[k, 28 + 2 * dest], dwa[k, 29 + 2 * dest]], axis=0).astype(BF)
            for b in range(3):
                at = 576 + 48 * k + 16 * b
                o[at:at + 16, :] = gpr[r, k, :, 128 * b:128 * b + 128].astype(BF)
        o[768:832, :] = res0[0:64, :]
        o[832:896, :] = cin[1536:1600, :]
        o[896:960, :] = zin[768:832, :]
        o[960:1024, :] = cin[1600:1664, :]


def combine_kernel(v0, v1, v2, v3, o0, o1, o2, o3):
    vs = (v0, v1, v2, v3)
    for k, o in enumerate((o0, o1, o2, o3)):
        ys = slice(128 * k, 128 * k + 128)
        o[0:128, :] = (v0[ys, :].astype(F32) + v2[ys, :].astype(F32)).astype(BF)
        o[128:256, :] = (v1[ys, :].astype(F32) + v3[ys, :].astype(F32)).astype(BF)
        for at, src, n in ((256, 512 + 16 * k, 16), (272, 576 + 48 * k, 48)):
            tot = v0[src:src + n, :].astype(F32)
            for v in vs[1:]:
                tot = tot + v[src:src + n, :].astype(F32)
            o[at:at + n, :] = tot.astype(BF)
        for r, v in enumerate(vs):
            for b in range(4):
                at = 320 + 64 * r + 16 * b
                o[at:at + 16, :] = v[768 + 64 * b + 16 * k:784 + 64 * b + 16 * k, :]


def restore_kernel(sc, off, wid, z0, z1, z2, z3, out, asp, small, zs, yscr, ascr):
    q, zh, mz, mc, rp = sc[1], sc[2], sc[3], sc[4], sc[6]
    tot = None
    for k, z in enumerate((z0, z1, z2, z3)):
        src = lax.rem(zh + k, 4)
        zs[src] = z[...]
        v = z[256:320, :].astype(F32)
        tot = v if tot is None else tot + v
    small[...] = tot
    for f in range(2):
        w = lax.broadcasted_iota(jnp.int32, (128, 64), 0)
        x = lax.broadcasted_iota(jnp.int32, (128, 64), 1)
        tgt = 2 * jnp.bitwise_and(x, 31) + jnp.right_shift(x, 5)
        hot = jnp.where((jnp.bitwise_and(w - off[f], 127) == tgt) & (tgt < wid[f]), 1.0, 0.0).astype(BF)
        for rho in range(2):
            par = jnp.bitwise_xor(rp, rho)
            for b in range(4):
                at = 128 * rho + 32 * b
                both = jnp.concatenate([zs[2 * f, at:at + 32, :], zs[2 * f + 1, at:at + 32, :]], axis=0)
                out[f, 2 * b + par] = dotf(hot, both).astype(BF)
        for r in range(4):
            qs = back(q, r)
            for zr in range(2):
                for cr in range(2):
                    t0 = 8 * (qs // 2) + 4 * jnp.bitwise_xor(mc, cr) + 2 * jnp.bitwise_xor(mz, zr)
                    at = 320 + 64 * r + 32 * zr + 16 * cr
                    for e in range(2):
                        h = 2 * (t0 + e) + lax.rem(qs, 2)
                        ascr[h] = jnp.concatenate(
                            [zs[2 * f, at:at + 16, 64 * e:64 * e + 64],
                             zs[2 * f + 1, at:at + 16, 64 * e:64 * e + 64]], axis=1)
        asp[f] = dotf(ascr[...].reshape(512, 128), perm_matrix(off[f], True)).astype(BF).reshape(32, 16, 128)


def call(kernel, scalars, args, outs, scratch=(), in_specs=None):
    whole = pl.BlockSpec(memory_space=pltpu.VMEM)
    specs = in_specs if in_specs is not None else [whole] * len(args)
    return pl.pallas_call(
        kernel,
        grid_spec=pltpu.PrefetchScalarGridSpec(
            num_scalar_prefetch=len(scalars), grid=(1,), in_specs=specs,
            out_specs=[pl.BlockSpec(o[0], lambda *a, n=len(o[0]): (0,) * n) for o in outs],
            scratch_shapes=[pltpu.VMEM(s, d) for s, d in scratch]),
        out_shape=[jax.ShapeDtypeStruct(s, d) for s, d in outs],
        compiler_params=pltpu.CompilerParams(vmem_limit_bytes=VM),
    )(*scalars, *args)


def local(feats, offsets, widths, labels, dw_kernel, pw_weight, pw_bias, proj, proj_bias, upstream):
    q = lax.axis_index("section")
    hf, rp = q // 2, q % 2
    scal = jnp.stack([hf, q, lax.axis_index("zh"), lax.axis_index("zl"), lax.axis_index("core"),
                      lax.axis_index("dp"), rp]).astype(jnp.int32)
    sc = (scal, offsets, widths)
    scaling = 1.0 / math.sqrt(8192.0 * lax.axis_size("dp"))

    (blk,) = call(pack_kernel, sc, [pw_weight, dw_kernel, proj, pw_bias, proj_bias[None]], [((128, 128), BF)])
    wz = gather_rel(jnp.stack(gather_rel(blk, "section")), "zh")
    quarters = gather_rel(jnp.stack([a[:, 0:64] for a in wz]), "dp")

    upx = upstream.reshape(16, 2, 2, 8, 2, 128)
    upx = lax.dynamic_slice(upx, (0, 0, hf, 0, rp, 0), (16, 2, 1, 8, 1, 128)).reshape(16, 2, 8, 128)
    upx = upx.transpose(1, 2, 0, 3)
    xs = call(
        select_kernel, sc, [feats.reshape(2, 16, 2, 128, 128), upx], [((576, 128), BF)] * 4,
        scratch=[((4, 8, 16, 64), F32)],
        in_specs=[pl.BlockSpec((2, 16, 1, 128, 128), lambda i, sc, off, wid: (0, 0, sc[6], 0, 0)),
                  pl.BlockSpec((2, 8, 16, 128), lambda i, *a: (0, 0, 0, 0))])
    xs = [xs[0]] + [shift(xs[k], "zh", k) for k in range(1, 4)]

    depth, dws = call(
        depth_kernel, sc, [*xs, *wz], [((4, 8, NCOL, 128), BF), ((4, 4, 16, 128), F32)],
        scratch=[((4, 34, 96, 128), F32)])
    keep, send, wfull = call(
        product_kernel, sc, [depth, *quarters],
        [((2, 2, NCOL, 256), F32), ((2, 2, NCOL, 256), BF), ((4, 4, 128, 256), BF)],
        scratch=[((8, NCOL, 256), F32)])

    pj = jnp.stack([a[:, 64:112] for a in wz])
    pjflat = pj.reshape(768, 128)
    uz = shift(jnp.concatenate([pjflat] + [x[544:576] for x in xs], axis=0), "zl", 1)
    uc = shift(jnp.concatenate(
        [pjflat, uz[0:768]] + [x[528:544] for x in xs] + [uz[784 + 32 * k:800 + 32 * k] for k in range(4)],
        axis=0), "core", 1)

    rcore = shift(send, "core", 1)
    rzl = shift((keep[1] + rcore[1].astype(F32)).astype(BF), "zl", 1)
    zout, res0, gkeep, gsend = call(
        middle_kernel, sc, [keep, rcore, rzl, pj, uz, uc, *xs, labels],
        [((896, 128), BF), ((128, 128), BF), ((2, 4, 4, 16, 384), F32), ((2, 4, 4, 16, 384), BF)],
        scratch=[((4, 256, 384), BF), ((256, 128), F32), ((4, 256, 384), F32)])

    zin = shift(zout, "zl", 1)
    cin = shift(jnp.concatenate([zout[0:768], zin[0:768], res0[64:128], zin[832:896]], axis=0), "core", 1)
    gz = gkeep + shift(gsend, "core", 1).astype(F32)
    gpr = gz[0] + shift(gz[1].astype(BF), "zl", 1).astype(F32)

    *gs, pgs = call(
        weight_kernel, sc, [depth, zout, zin, cin], [((4, 256, 128), BF)] * 4 + [((8, NCOL, 256), BF)],
        scratch=[((4, 4, 256, 128), BF)])
    vs = call(
        backward_kernel, sc, [*xs, wfull, dws, pgs, gpr, res0, zin, cin], [((1024, 128), BF)] * 4,
        scratch=[((4, 34, 96, 128), F32), ((4, 8, NCOL, 128), F32), ((4, 26, 32, 128), F32), ((4, 36, 8, 128), F32)])

    gsum = gs[0].astype(F32)
    for k in range(1, 4):
        gsum = gsum + shift(gs[k], "section", k).astype(F32)
    gsb = gsum.astype(BF)
    gown = gsum[0]
    for k in range(1, 4):
        gown = gown + shift(gsb[k], "zh", -k).astype(F32)

    zs = call(combine_kernel, (), [vs[0]] + [shift(vs[k], "section", k) for k in range(1, 4)],
              [((576, 128), BF)] * 4)
    input_grad, asp, small = call(
        restore_kernel, sc, [zs[0]] + [shift(zs[k], "zh", -k) for k in range(1, 4)],
        [((2, 8, 128, 128), BF), ((2, 32, 16, 128), BF), ((64, 128), F32)],
        scratch=[((4, 576, 128), BF), ((8, 128), F32), ((32, 16, 128), BF)])

    own = jnp.concatenate([gown, small], axis=0)
    ownb = own.astype(BF)
    tot = own
    for k in range(1, 4):
        tot = tot + shift(ownb, "dp", k).astype(F32)
    tot = tot * scaling
    grad_pw = jnp.concatenate([tot[0:128], tot[128:256]], axis=1)
    grad_dw = tot[256:265]
    grad_proj = jnp.concatenate([tot[272:288], tot[288:304]], axis=1)
    grad_pwb = tot[304:320, 0]
    grad_pb = tot[304:320, 64]
    aspp = asp.transpose(2, 0, 1, 3)
    return (aspp, input_grad, grad_dw[None], grad_pw[None], grad_pwb[None], grad_proj[None], grad_pb)


def solution(mesh):
    fine = Mesh(mesh.devices.reshape(4, 4, 4, 2, 2), ("section", "dp", "zh", "zl", "core"))
    chan = ("zh", "zl", "core")
    in_specs = (
        P("dp", None, None, chan),
        P("dp"),
        P("dp"),
        P("dp", None, None),
        P("section", None, chan),
        P("section", chan, None),
        P("section", chan),
        P("section", chan, None),
        P(chan),
        P(chan, "dp", None, None),
    )
    out_specs = (
        P(chan, "dp", None, None),
        P("dp", "section", None, chan),
        P("section", None, chan),
        P("section", chan, None),
        P("section", chan),
        P("section", chan, None),
        P(chan),
    )
    return jax.shard_map(local, mesh=fine, in_specs=in_specs, out_specs=out_specs, check_vma=False)
```

profile of v0, /device:TPU:8, one launch (start us, length us, event | category | flops | bytes accessed | tf_op | source)
XLA Modules:
  0.0 173.0 jit_solution(7394688077399902058)
XLA Ops:
  1.2 2.3 %shard_map.154 = bf16[128,128]{1,0:T(8,128)(2,1)} custom-call(s32[7]{0:T(128)} %stack.76.sc, s32[2]{0:T(128)} %off.15, s32[2]{0:T(128)} %wid.15, bf16[1,128,256]{2,1,0:T(8,128)(2,1)} %pw.1, bf16[1,9,128]{2,1,0:T(8,128)(2,1)} %dw.1, bf16[1,16,256]{2,1,0:T(8,128)(2,1)} %proj.1, f32[1,16]{1,0:T(1,128)} %pwb.1, f32[1,16]{1,0:T(1,128)} %bitcast.75), custom_call_target="tpu_custom_call" | custom-call | tf_op jit(solution)/shard_map/pallas_call | solution.py:417
  3.5 2.8 %collective-permute-start.5 = (bf16[128,128]{1,0:T(8,128)(2,1)}, bf16[128,128]{1,0:T(8,128)(2,1)S(1)}, u32[]{:S(2)}, u32[]{:S(2)}) collective-permute-start(bf16[128,128]{1,0:T(8,128)(2,1)} %shard_map.154), channel_id=1, source_target_pairs={{0,192},{64,0},{128,64},{192,128},{1,193},{65,1},{129,65},{193,129... | collective-permute-start | bytes 98312 | tf_op jit(solution)/shard_map/ppermute | solution.py:26
  6.3 0.8 collective-permute-start.4
  7.1 0.9 collective-permute-start.3
  8.8 4.6 %shard_map.153 = (bf16[576,128]{1,0:T(8,128)(2,1)}, bf16[576,128]{1,0:T(8,128)(2,1)}, bf16[576,128]{1,0:T(8,128)(2,1)}, bf16[576,128]{1,0:T(8,128)(2,1)}) custom-call(s32[7]{0:T(128)} %stack.76.sc, s32[2]{0:T(128)} %off.15, s32[2]{0:T(128)} %wid.15, bf16[2,16,2,128,128]{4,3,2,1,0:T(8,128)(2,1)} %bitcast.67, bf16[2,8,16,128]{3,2,1,0:T(8,128)(2,1)} %bitcast.69), custom_call_target="tpu_custom_call" | custom-call | tf_op jit(solution)/shard_map/pallas_call | solution.py:417
  13.4 3.3 %collective-permute-start = (bf16[576,128]{1,0:T(8,128)(2,1)}, bf16[576,128]{1,0:T(8,128)(2,1)S(1)}, u32[]{:S(2)}, u32[]{:S(2)}) collective-permute-start(bf16[576,128]{1,0:T(8,128)(2,1)} %get-tuple-element.37), channel_id=1, source_target_pairs={{0,4},{4,8},{8,12},{12,0},{1,5},{5,9},{9,13},{13,1},{2,6},{6,10},{... | collective-permute-start | bytes 442376 | tf_op jit(solution)/shard_map/ppermute | solution.py:26
  16.7 5.4 %collective-permute-start.1 = (bf16[576,128]{1,0:T(8,128)(2,1)}, bf16[576,128]{1,0:T(8,128)(2,1)S(1)}, u32[]{:S(2)}, u32[]{:S(2)}) collective-permute-start(bf16[576,128]{1,0:T(8,128)(2,1)} %get-tuple-element.38), channel_id=1, source_target_pairs={{0,8},{4,12},{8,0},{12,4},{1,9},{5,13},{9,1},{13,5},{2,10},{6,14},... | collective-permute-start | bytes 442376 | tf_op jit(solution)/shard_map/ppermute | solution.py:26
  22.1 2.7 %collective-permute-start.2 = (bf16[576,128]{1,0:T(8,128)(2,1)}, bf16[576,128]{1,0:T(8,128)(2,1)S(1)}, u32[]{:S(2)}, u32[]{:S(2)}) collective-permute-start(bf16[576,128]{1,0:T(8,128)(2,1)} %get-tuple-element.39), channel_id=1, source_target_pairs={{0,12},{4,0},{8,4},{12,8},{1,13},{5,1},{9,5},{13,9},{2,14},{6,2},{... | collective-permute-start | bytes 442376 | tf_op jit(solution)/shard_map/ppermute | solution.py:26
  24.9 3.8 %collective-permute-start.7 = (bf16[4,128,128]{2,1,0:T(8,128)(2,1)S(1)}, bf16[4,128,128]{2,1,0:T(8,128)(2,1)S(1)}, u32[]{:S(2)}, u32[]{:S(2)}) collective-permute-start(bf16[4,128,128]{2,1,0:T(8,128)(2,1)S(1)} %pad_maximum_fusion.4.a0), channel_id=1, source_target_pairs={{0,8},{4,12},{8,0},{12,4},{1,9},{5,13},{9,1},{13,5},{2,10},{6,14},... | collective-permute-start | bytes 393224 | tf_op jit(solution)/shard_map/ppermute | solution.py:26
  28.7 17.5 %collective-permute-done.8.a3 = bf16[4,128,128]{2,1,0:T(8,128)(2,1)S(1)} collective-permute-done((bf16[4,128,128]{2,1,0:T(8,128)(2,1)S(1)}, bf16[4,128,128]{2,1,0:T(8,128)(2,1)S(1)}, u32[]{:S(2)}, u32[]{:S(2)}) %collective-permute-start.8) | collective-permute-done | bytes 131104 | tf_op jit(solution)/shard_map/ppermute | solution.py:26
  46.2 1.8 %collective-permute-start.6 = (bf16[4,128,128]{2,1,0:T(8,128)(2,1)S(1)}, bf16[4,128,128]{2,1,0:T(8,128)(2,1)S(1)}, u32[]{:S(2)}, u32[]{:S(2)}) collective-permute-start(bf16[4,128,128]{2,1,0:T(8,128)(2,1)S(1)} %pad_maximum_fusion.4.a0), channel_id=1, source_target_pairs={{0,4},{4,8},{8,12},{12,0},{1,5},{5,9},{9,13},{13,1},{2,6},{6,10},{... | collective-permute-start | bytes 393224 | tf_op jit(solution)/shard_map/ppermute | solution.py:26
  48.0 5.2 %collective-permute-done.6.a1 = bf16[4,128,128]{2,1,0:T(8,128)(2,1)S(1)} collective-permute-done((bf16[4,128,128]{2,1,0:T(8,128)(2,1)S(1)}, bf16[4,128,128]{2,1,0:T(8,128)(2,1)S(1)}, u32[]{:S(2)}, u32[]{:S(2)}) %collective-permute-start.6) | collective-permute-done | bytes 131104 | tf_op jit(solution)/shard_map/ppermute | solution.py:26
  54.9 2.6 %collective-permute-start.10 = (bf16[4,4,64,128]{3,2,1,0:T(8,128)(2,1)S(1)}, bf16[4,4,64,128]{3,2,1,0:T(8,128)(2,1)S(1)}, u32[]{:S(2)}, u32[]{:S(2)}) collective-permute-start(bf16[4,4,64,128]{3,2,1,0:T(8,128)(2,1)S(1)} %pad_maximum_fusion.1.q0), channel_id=1, source_target_pairs={{0,32},{16,48},{32,0},{48,16},{1,33},{17,49},{33,1},{49,17},{2,34}... | collective-permute-start | bytes 786440 | tf_op jit(solution)/shard_map/ppermute | solution.py:26
  57.5 1.9 %collective-permute-start.9 = (bf16[4,4,64,128]{3,2,1,0:T(8,128)(2,1)S(1)}, bf16[4,4,64,128]{3,2,1,0:T(8,128)(2,1)S(1)}, u32[]{:S(2)}, u32[]{:S(2)}) collective-permute-start(bf16[4,4,64,128]{3,2,1,0:T(8,128)(2,1)S(1)} %pad_maximum_fusion.1.q0), channel_id=1, source_target_pairs={{0,16},{16,32},{32,48},{48,0},{1,17},{17,33},{33,49},{49,1},{2,18}... | collective-permute-start | bytes 786440 | tf_op jit(solution)/shard_map/ppermute | solution.py:26
  59.4 6.3 %shard_map.155 = (bf16[4,8,192,128]{3,2,1,0:T(8,128)(2,1)}, f32[4,4,16,128]{3,2,1,0:T(8,128)}) custom-call(s32[7]{0:T(128)} %stack.76.sc, s32[2]{0:T(128)} %off.15, s32[2]{0:T(128)} %wid.15, bf16[576,128]{1,0:T(8,128)(2,1)} %get-tuple-element.36.x0.f0, bf16[576,128]{1,0:T(8,128)(2,1)} %copy-done.4, bf16[576,128]{1,0:T(8,128)(2,1)} %copy-done.5, ...), custom_call_target="tpu_custom_call" | custom-call | tf_op jit(solution)/shard_map/pallas_call | solution.py:417
  69.4 4.5 %shard_map.156 = (f32[2,2,192,256]{3,2,1,0:T(8,128)}, bf16[2,2,192,256]{3,2,1,0:T(8,128)(2,1)}, bf16[4,4,128,256]{3,2,1,0:T(8,128)(2,1)}) custom-call(s32[7]{0:T(128)} %stack.76.sc, s32[2]{0:T(128)} %off.15, s32[2]{0:T(128)} %wid.15, bf16[4,8,192,128]{3,2,1,0:T(8,128)(2,1)} %get-tuple-element.40.depth, bf16[4,4,64,128]{3,2,1,0:T(8,128)(2,1)} %copy-done.8, ...), custom_call_target="tpu_custom_call" | custom-call | tf_op jit(solution)/shard_map/pallas_call | solution.py:417
  74.4 1.4 collective-permute-done.12.rcore
  75.8 1.2 fusion.1
  77.0 2.1 %collective-permute-start.13 = (bf16[2,192,256]{2,1,0:T(8,128)(2,1)S(1)}, bf16[2,192,256]{2,1,0:T(8,128)(2,1)S(1)}, u32[]{:S(2)}, u32[]{:S(2)}) collective-permute-start(bf16[2,192,256]{2,1,0:T(8,128)(2,1)S(1)} %fusion.1), channel_id=1, source_target_pairs={{0,2},{2,0},{1,3},{3,1},{4,6},{6,4},{5,7},{7,5},{8,10},{10,8},{9,1... | collective-permute-start | bytes 589832 | tf_op jit(solution)/shard_map/ppermute | solution.py:26
  79.1 5.2 %collective-permute-done.13.rzl = bf16[2,192,256]{2,1,0:T(8,128)(2,1)S(1)} collective-permute-done((bf16[2,192,256]{2,1,0:T(8,128)(2,1)S(1)}, bf16[2,192,256]{2,1,0:T(8,128)(2,1)S(1)}, u32[]{:S(2)}, u32[]{:S(2)}) %collective-permute-start.13) | collective-permute-done | bytes 196640 | tf_op jit(solution)/shard_map/ppermute | solution.py:26
  85.0 5.0 %shard_map.157 = (bf16[896,128]{1,0:T(8,128)(2,1)}, bf16[128,128]{1,0:T(8,128)(2,1)}, f32[2,4,4,16,384]{4,3,2,1,0:T(8,128)}, bf16[2,4,4,16,384]{4,3,2,1,0:T(8,128)(2,1)}) custom-call(s32[7]{0:T(128)} %stack.76.sc, s32[2]{0:T(128)} %off.15, s32[2]{0:T(128)} %wid.15, f32[2,2,192,256]{3,2,1,0:T(8,128)} %get-tuple-element.43.keep, ...), custom_call_target="tpu_custom_call" | custom-call | tf_op jit(solution)/shard_map/pallas_call | solution.py:417
  90.0 1.7 %collective-permute-start.16 = (bf16[896,128]{1,0:T(8,128)(2,1)}, bf16[896,128]{1,0:T(8,128)(2,1)S(1)}, u32[]{:S(2)}, u32[]{:S(2)}) collective-permute-start(bf16[896,128]{1,0:T(8,128)(2,1)} %get-tuple-element.45.zout), channel_id=1, source_target_pairs={{0,2},{2,0},{1,3},{3,1},{4,6},{6,4},{5,7},{7,5},{8,10},{10,8},{9,1... | collective-permute-start | bytes 688136 | tf_op jit(solution)/shard_map/ppermute | solution.py:26
  91.7 1.0 slice.144
  93.4 3.9 %collective-permute-done.16.zin = bf16[896,128]{1,0:T(8,128)(2,1)S(1)} collective-permute-done((bf16[896,128]{1,0:T(8,128)(2,1)}, bf16[896,128]{1,0:T(8,128)(2,1)S(1)}, u32[]{:S(2)}, u32[]{:S(2)}) %collective-permute-start.16) | collective-permute-done | bytes 229408 | tf_op jit(solution)/shard_map/ppermute | solution.py:26
  97.6 1.5 collective-permute-start.19
  100.0 4.5 %shard_map.158 = (bf16[4,256,128]{2,1,0:T(8,128)(2,1)}, bf16[4,256,128]{2,1,0:T(8,128)(2,1)}, bf16[4,256,128]{2,1,0:T(8,128)(2,1)}, bf16[4,256,128]{2,1,0:T(8,128)(2,1)}, bf16[8,192,256]{2,1,0:T(8,128)(2,1)}) custom-call(s32[7]{0:T(128)} %stack.76.sc, s32[2]{0:T(128)} %off.15, s32[2]{0:T(128)} %wid.15, bf16[4,8,192,128]{3,2,1,0:T(8,128)(2,1)} %get-tuple-element.40.depth, ...), custom_call_target="tpu_custom_call" | custom-call | tf_op jit(solution)/shard_map/pallas_call | solution.py:417
  104.4 1.8 %collective-permute-start.26 = (bf16[4,256,128]{2,1,0:T(8,128)(2,1)}, bf16[4,256,128]{2,1,0:T(8,128)(2,1)S(1)}, u32[]{:S(2)}, u32[]{:S(2)}) collective-permute-start(bf16[4,256,128]{2,1,0:T(8,128)(2,1)} %get-tuple-element.61), channel_id=1, source_target_pairs={{0,64},{64,128},{128,192},{192,0},{1,65},{65,129},{129,193},{193,1... | collective-permute-start | bytes 786440 | tf_op jit(solution)/shard_map/ppermute | solution.py:26
  106.2 2.0 %collective-permute-start.27 = (bf16[4,256,128]{2,1,0:T(8,128)(2,1)}, bf16[4,256,128]{2,1,0:T(8,128)(2,1)S(1)}, u32[]{:S(2)}, u32[]{:S(2)}) collective-permute-start(bf16[4,256,128]{2,1,0:T(8,128)(2,1)} %get-tuple-element.62), channel_id=1, source_target_pairs={{0,128},{64,192},{128,0},{192,64},{1,129},{65,193},{129,1},{193,65... | collective-permute-start | bytes 786440 | tf_op jit(solution)/shard_map/ppermute | solution.py:26
  108.2 0.9 collective-permute-start.28
  109.2 0.8 fusion.gpr
  110.0 10.1 %shard_map.159 = (bf16[1024,128]{1,0:T(8,128)(2,1)}, bf16[1024,128]{1,0:T(8,128)(2,1)}, bf16[1024,128]{1,0:T(8,128)(2,1)}, bf16[1024,128]{1,0:T(8,128)(2,1)}) custom-call(s32[7]{0:T(128)} %stack.76.sc, s32[2]{0:T(128)} %off.15, s32[2]{0:T(128)} %wid.15, bf16[576,128]{1,0:T(8,128)(2,1)} %get-tuple-element.36.x0.f0, bf16[576,128]{1,0:T(8,128)(2,1)} %copy-done.4, ...), custom_call_target="tpu_custom_call" | custom-call | tf_op jit(solution)/shard_map/pallas_call | solution.py:417
  120.1 1.1 collective-permute-start.20
  121.2 1.5 collective-permute-start.21
  122.7 1.4 collective-permute-start.22
  124.3 2.7 %collective-permute-start.29 = (bf16[256,128]{1,0:T(8,128)(2,1)S(1)}, bf16[256,128]{1,0:T(8,128)(2,1)S(1)}, u32[]{:S(2)}, u32[]{:S(2)}) collective-permute-start(bf16[256,128]{1,0:T(8,128)(2,1)S(1)} %get-tuple-element.83), channel_id=1, source_target_pairs={{0,12},{4,0},{8,4},{12,8},{1,13},{5,1},{9,5},{13,9},{2,14},{6,2},{... | collective-permute-start | bytes 196616 | tf_op jit(solution)/shard_map/ppermute | solution.py:26
  127.5 7.1 %collective-permute-done.20.v1 = bf16[1024,128]{1,0:T(8,128)(2,1)S(1)} collective-permute-done((bf16[1024,128]{1,0:T(8,128)(2,1)}, bf16[1024,128]{1,0:T(8,128)(2,1)S(1)}, u32[]{:S(2)}, u32[]{:S(2)}) %collective-permute-start.20) | collective-permute-done | bytes 262176 | tf_op jit(solution)/shard_map/ppermute | solution.py:26
  134.6 4.3 %collective-permute-start.30 = (bf16[256,128]{1,0:T(8,128)(2,1)S(1)}, bf16[256,128]{1,0:T(8,128)(2,1)S(1)}, u32[]{:S(2)}, u32[]{:S(2)}) collective-permute-start(bf16[256,128]{1,0:T(8,128)(2,1)S(1)} %get-tuple-element.85), channel_id=1, source_target_pairs={{0,8},{4,12},{8,0},{12,4},{1,9},{5,13},{9,1},{13,5},{2,10},{6,14},... | collective-permute-start | bytes 196616 | tf_op jit(solution)/shard_map/ppermute | solution.py:26
  139.7 2.0 %shard_map.160 = (bf16[576,128]{1,0:T(8,128)(2,1)}, bf16[576,128]{1,0:T(8,128)(2,1)}, bf16[576,128]{1,0:T(8,128)(2,1)}, bf16[576,128]{1,0:T(8,128)(2,1)}) custom-call(bf16[1024,128]{1,0:T(8,128)(2,1)} %get-tuple-element.50.v0, bf16[1024,128]{1,0:T(8,128)(2,1)} %copy-done.17, bf16[1024,128]{1,0:T(8,128)(2,1)} %copy-done.18, bf16[1024,128]{1,0:T(8,128)(2,1)} %copy-done.19), custom_call_target="tpu_custom_call" | custom-call | tf_op jit(solution)/shard_map/pallas_call | solution.py:417
  141.8 4.0 %collective-permute-start.24 = (bf16[576,128]{1,0:T(8,128)(2,1)}, bf16[576,128]{1,0:T(8,128)(2,1)S(1)}, u32[]{:S(2)}, u32[]{:S(2)}) collective-permute-start(bf16[576,128]{1,0:T(8,128)(2,1)} %get-tuple-element.56), channel_id=1, source_target_pairs={{0,8},{4,12},{8,0},{12,4},{1,9},{5,13},{9,1},{13,5},{2,10},{6,14},... | collective-permute-start | bytes 442376 | tf_op jit(solution)/shard_map/ppermute | solution.py:26
  146.4 8.7 %collective-permute-done.23.z1 = bf16[576,128]{1,0:T(8,128)(2,1)S(1)} collective-permute-done((bf16[576,128]{1,0:T(8,128)(2,1)}, bf16[576,128]{1,0:T(8,128)(2,1)S(1)}, u32[]{:S(2)}, u32[]{:S(2)}) %collective-permute-start.23) | collective-permute-done | bytes 147488 | tf_op jit(solution)/shard_map/ppermute | solution.py:26
  155.1 1.4 collective-permute-done.25.z3
  157.1 3.2 %shard_map.161 = (bf16[2,8,128,128]{3,2,1,0:T(8,128)(2,1)}, bf16[2,32,16,128]{3,2,1,0:T(8,128)(2,1)}, f32[64,128]{1,0:T(8,128)}) custom-call(s32[7]{0:T(128)} %stack.76.sc, s32[2]{0:T(128)} %off.15, s32[2]{0:T(128)} %wid.15, bf16[576,128]{1,0:T(8,128)(2,1)} %get-tuple-element.54.z0, bf16[576,128]{1,0:T(8,128)(2,1)} %copy-done.24, ...), custom_call_target="tpu_custom_call" | custom-call | tf_op jit(solution)/shard_map/pallas_call | solution.py:417
  160.3 0.8 fusion.3
  161.0 2.6 %collective-permute-start.34 = (bf16[320,128]{1,0:T(8,128)(2,1)S(1)}, bf16[320,128]{1,0:T(8,128)(2,1)S(1)}, u32[]{:S(2)}, u32[]{:S(2)}) collective-permute-start(bf16[320,128]{1,0:T(8,128)(2,1)S(1)} %fusion.3), channel_id=1, source_target_pairs={{0,48},{16,0},{32,16},{48,32},{1,49},{17,1},{33,17},{49,33},{2,50}... | collective-permute-start | bytes 245768 | tf_op jit(solution)/shard_map/ppermute | solution.py:26
  163.7 2.1 %collective-permute-start.32 = (bf16[320,128]{1,0:T(8,128)(2,1)S(1)}, bf16[320,128]{1,0:T(8,128)(2,1)S(1)}, u32[]{:S(2)}, u32[]{:S(2)}) collective-permute-start(bf16[320,128]{1,0:T(8,128)(2,1)S(1)} %fusion.3), channel_id=1, source_target_pairs={{0,16},{16,32},{32,48},{48,0},{1,17},{17,33},{33,49},{49,1},{2,18}... | collective-permute-start | bytes 245768 | tf_op jit(solution)/shard_map/ppermute | solution.py:26
  165.7 1.7 copy.21
  167.5 2.2 %collective-permute-done.33 = bf16[320,128]{1,0:T(8,128)(2,1)S(1)} collective-permute-done((bf16[320,128]{1,0:T(8,128)(2,1)S(1)}, bf16[320,128]{1,0:T(8,128)(2,1)S(1)}, u32[]{:S(2)}, u32[]{:S(2)}) %collective-permute-start.33) | collective-permute-done | bytes 81952 | tf_op jit(solution)/shard_map/ppermute | solution.py:26
  169.6 0.8 add_multiply_fusion
  (137 shorter events, 15.0 us)
Async XLA Ops:
  0.6 7.3 %copy-start = (bf16[16,2,32,128]{3,2,1,0:T(8,128)(2,1)S(1)}, bf16[16,2,32,128]{3,2,1,0:T(8,128)(2,1)}, u32[]{:S(2)}) copy-start(bf16[16,2,32,128]{3,2,1,0:T(8,128)(2,1)} %param.19) | copy-start | bytes 786436
  3.5 21.3 %copy-start.27 = (bf16[128,128]{1,0:T(8,128)(2,1)S(1)}, bf16[128,128]{1,0:T(8,128)(2,1)}, u32[]{:S(2)}) copy-start(bf16[128,128]{1,0:T(8,128)(2,1)} %shard_map.154) | copy-start | bytes 98308
  3.5 18.6 %collective-permute-start.5 = (bf16[128,128]{1,0:T(8,128)(2,1)}, bf16[128,128]{1,0:T(8,128)(2,1)S(1)}, u32[]{:S(2)}, u32[]{:S(2)}) collective-permute-start(bf16[128,128]{1,0:T(8,128)(2,1)} %shard_map.154), channel_id=1, source_target_pairs={{0,192},{64,0},{128,64},{192,128},{1,193},{65,1},{129,65},{193,129... | collective-permute-start | bytes 98312 | tf_op jit(solution)/shard_map/ppermute | solution.py:26
  6.3 18.5 %collective-permute-start.4 = (bf16[128,128]{1,0:T(8,128)(2,1)}, bf16[128,128]{1,0:T(8,128)(2,1)S(1)}, u32[]{:S(2)}, u32[]{:S(2)}) collective-permute-start(bf16[128,128]{1,0:T(8,128)(2,1)} %shard_map.154), channel_id=1, source_target_pairs={{0,128},{64,192},{128,0},{192,64},{1,129},{65,193},{129,1},{193,65... | collective-permute-start | bytes 98312 | tf_op jit(solution)/shard_map/ppermute | solution.py:26
  7.1 17.7 %collective-permute-start.3 = (bf16[128,128]{1,0:T(8,128)(2,1)}, bf16[128,128]{1,0:T(8,128)(2,1)S(1)}, u32[]{:S(2)}, u32[]{:S(2)}) collective-permute-start(bf16[128,128]{1,0:T(8,128)(2,1)} %shard_map.154), channel_id=1, source_target_pairs={{0,64},{64,128},{128,192},{192,0},{1,65},{65,129},{129,193},{193,1... | collective-permute-start | bytes 98312 | tf_op jit(solution)/shard_map/ppermute | solution.py:26
  13.4 40.7 %collective-permute-start = (bf16[576,128]{1,0:T(8,128)(2,1)}, bf16[576,128]{1,0:T(8,128)(2,1)S(1)}, u32[]{:S(2)}, u32[]{:S(2)}) collective-permute-start(bf16[576,128]{1,0:T(8,128)(2,1)} %get-tuple-element.37), channel_id=1, source_target_pairs={{0,4},{4,8},{8,12},{12,0},{1,5},{5,9},{9,13},{13,1},{2,6},{6,10},{... | collective-permute-start | bytes 442376 | tf_op jit(solution)/shard_map/ppermute | solution.py:26
  16.7 37.4 %collective-permute-start.1 = (bf16[576,128]{1,0:T(8,128)(2,1)}, bf16[576,128]{1,0:T(8,128)(2,1)S(1)}, u32[]{:S(2)}, u32[]{:S(2)}) collective-permute-start(bf16[576,128]{1,0:T(8,128)(2,1)} %get-tuple-element.38), channel_id=1, source_target_pairs={{0,8},{4,12},{8,0},{12,4},{1,9},{5,13},{9,1},{13,5},{2,10},{6,14},... | collective-permute-start | bytes 442376 | tf_op jit(solution)/shard_map/ppermute | solution.py:26
  22.1 32.1 %collective-permute-start.2 = (bf16[576,128]{1,0:T(8,128)(2,1)}, bf16[576,128]{1,0:T(8,128)(2,1)S(1)}, u32[]{:S(2)}, u32[]{:S(2)}) collective-permute-start(bf16[576,128]{1,0:T(8,128)(2,1)} %get-tuple-element.39), channel_id=1, source_target_pairs={{0,12},{4,0},{8,4},{12,8},{1,13},{5,1},{9,5},{13,9},{2,14},{6,2},{... | collective-permute-start | bytes 442376 | tf_op jit(solution)/shard_map/ppermute | solution.py:26
  24.8 34.6 %copy-start.7 = (bf16[4,128,128]{2,1,0:T(8,128)(2,1)}, bf16[4,128,128]{2,1,0:T(8,128)(2,1)S(1)}, u32[]{:S(2)}) copy-start(bf16[4,128,128]{2,1,0:T(8,128)(2,1)S(1)} %pad_maximum_fusion.4.a0) | copy-start | bytes 393220
  24.8 21.4 %collective-permute-start.8 = (bf16[4,128,128]{2,1,0:T(8,128)(2,1)S(1)}, bf16[4,128,128]{2,1,0:T(8,128)(2,1)S(1)}, u32[]{:S(2)}, u32[]{:S(2)}) collective-permute-start(bf16[4,128,128]{2,1,0:T(8,128)(2,1)S(1)} %pad_maximum_fusion.4.a0), channel_id=1, source_target_pairs={{0,12},{4,0},{8,4},{12,8},{1,13},{5,1},{9,5},{13,9},{2,14},{6,2},{... | collective-permute-start | bytes 393224 | tf_op jit(solution)/shard_map/ppermute | solution.py:26
  24.9 23.1 %collective-permute-start.7 = (bf16[4,128,128]{2,1,0:T(8,128)(2,1)S(1)}, bf16[4,128,128]{2,1,0:T(8,128)(2,1)S(1)}, u32[]{:S(2)}, u32[]{:S(2)}) collective-permute-start(bf16[4,128,128]{2,1,0:T(8,128)(2,1)S(1)} %pad_maximum_fusion.4.a0), channel_id=1, source_target_pairs={{0,8},{4,12},{8,0},{12,4},{1,9},{5,13},{9,1},{13,5},{2,10},{6,14},... | collective-permute-start | bytes 393224 | tf_op jit(solution)/shard_map/ppermute | solution.py:26
  46.2 13.2 %copy-start.12 = (bf16[4,128,128]{2,1,0:T(8,128)(2,1)}, bf16[4,128,128]{2,1,0:T(8,128)(2,1)S(1)}, u32[]{:S(2)}) copy-start(bf16[4,128,128]{2,1,0:T(8,128)(2,1)S(1)} %collective-permute-done.8.a3) | copy-start | bytes 393220
  46.2 7.1 %collective-permute-start.6 = (bf16[4,128,128]{2,1,0:T(8,128)(2,1)S(1)}, bf16[4,128,128]{2,1,0:T(8,128)(2,1)S(1)}, u32[]{:S(2)}, u32[]{:S(2)}) collective-permute-start(bf16[4,128,128]{2,1,0:T(8,128)(2,1)S(1)} %pad_maximum_fusion.4.a0), channel_id=1, source_target_pairs={{0,4},{4,8},{8,12},{12,0},{1,5},{5,9},{9,13},{13,1},{2,6},{6,10},{... | collective-permute-start | bytes 393224 | tf_op jit(solution)/shard_map/ppermute | solution.py:26
  48.0 11.4 %copy-start.13 = (bf16[4,128,128]{2,1,0:T(8,128)(2,1)}, bf16[4,128,128]{2,1,0:T(8,128)(2,1)S(1)}, u32[]{:S(2)}) copy-start(bf16[4,128,128]{2,1,0:T(8,128)(2,1)S(1)} %collective-permute-done.7.a2) | copy-start | bytes 393220
  53.3 6.1 %copy-start.14 = (bf16[4,128,128]{2,1,0:T(8,128)(2,1)}, bf16[4,128,128]{2,1,0:T(8,128)(2,1)S(1)}, u32[]{:S(2)}) copy-start(bf16[4,128,128]{2,1,0:T(8,128)(2,1)S(1)} %collective-permute-done.6.a1) | copy-start | bytes 393220
  53.3 20.6 %copy-start.2 = (bf16[4,4,48,128]{3,2,1,0:T(8,128)(2,1)}, bf16[4,4,48,128]{3,2,1,0:T(8,128)(2,1)S(1)}, u32[]{:S(2)}) copy-start(bf16[4,4,48,128]{3,2,1,0:T(8,128)(2,1)S(1)} %pad_maximum_fusion.2.pj) | copy-start | bytes 589828
  54.1 5.3 %copy-start.4 = (bf16[576,128]{1,0:T(8,128)(2,1)}, bf16[576,128]{1,0:T(8,128)(2,1)S(1)}, u32[]{:S(2)}) copy-start(bf16[576,128]{1,0:T(8,128)(2,1)S(1)} %collective-permute-done.x1.f1) | copy-start | bytes 442372
  54.2 11.5 %collective-permute-start.14 = (bf16[896,128]{1,0:T(8,128)(2,1)S(1)}, bf16[896,128]{1,0:T(8,128)(2,1)S(1)}, u32[]{:S(2)}, u32[]{:S(2)}) collective-permute-start(bf16[896,128]{1,0:T(8,128)(2,1)S(1)} %constant_dynamic-update-slice_fusion), channel_id=1, source_target_pairs={{0,2},{2,0},{1,3},{3,1},{4,6},{6,4},{5,7},{7,5},{8,10},{10,8},{9,1... | collective-permute-start | bytes 688136 | tf_op jit(solution)/shard_map/ppermute | solution.py:26
  54.4 14.2 %copy-start.8 = (bf16[4,4,64,128]{3,2,1,0:T(8,128)(2,1)}, bf16[4,4,64,128]{3,2,1,0:T(8,128)(2,1)S(1)}, u32[]{:S(2)}) copy-start(bf16[4,4,64,128]{3,2,1,0:T(8,128)(2,1)S(1)} %pad_maximum_fusion.1.q0) | copy-start | bytes 786436
  54.4 14.1 %collective-permute-start.11 = (bf16[4,4,64,128]{3,2,1,0:T(8,128)(2,1)S(1)}, bf16[4,4,64,128]{3,2,1,0:T(8,128)(2,1)S(1)}, u32[]{:S(2)}, u32[]{:S(2)}) collective-permute-start(bf16[4,4,64,128]{3,2,1,0:T(8,128)(2,1)S(1)} %pad_maximum_fusion.1.q0), channel_id=1, source_target_pairs={{0,48},{16,0},{32,16},{48,32},{1,49},{17,1},{33,17},{49,33},{2,50}... | collective-permute-start | bytes 786440 | tf_op jit(solution)/shard_map/ppermute | solution.py:26
  54.9 13.6 %collective-permute-start.10 = (bf16[4,4,64,128]{3,2,1,0:T(8,128)(2,1)S(1)}, bf16[4,4,64,128]{3,2,1,0:T(8,128)(2,1)S(1)}, u32[]{:S(2)}, u32[]{:S(2)}) collective-permute-start(bf16[4,4,64,128]{3,2,1,0:T(8,128)(2,1)S(1)} %pad_maximum_fusion.1.q0), channel_id=1, source_target_pairs={{0,32},{16,48},{32,0},{48,16},{1,33},{17,49},{33,1},{49,17},{2,34}... | collective-permute-start | bytes 786440 | tf_op jit(solution)/shard_map/ppermute | solution.py:26
  57.5 11.0 %collective-permute-start.9 = (bf16[4,4,64,128]{3,2,1,0:T(8,128)(2,1)S(1)}, bf16[4,4,64,128]{3,2,1,0:T(8,128)(2,1)S(1)}, u32[]{:S(2)}, u32[]{:S(2)}) collective-permute-start(bf16[4,4,64,128]{3,2,1,0:T(8,128)(2,1)S(1)} %pad_maximum_fusion.1.q0), channel_id=1, source_target_pairs={{0,16},{16,32},{32,48},{48,0},{1,17},{17,33},{33,49},{49,1},{2,18}... | collective-permute-start | bytes 786440 | tf_op jit(solution)/shard_map/ppermute | solution.py:26
  65.7 18.6 %copy-start.10 = (bf16[896,128]{1,0:T(8,128)(2,1)}, bf16[896,128]{1,0:T(8,128)(2,1)S(1)}, u32[]{:S(2)}) copy-start(bf16[896,128]{1,0:T(8,128)(2,1)S(1)} %collective-permute-done.14.zin) | copy-start | bytes 688132
  73.9 1.9 %collective-permute-start.12 = (bf16[2,2,192,256]{3,2,1,0:T(8,128)(2,1)}, bf16[2,2,192,256]{3,2,1,0:T(8,128)(2,1)S(1)}, u32[]{:S(2)}, u32[]{:S(2)}) collective-permute-start(bf16[2,2,192,256]{3,2,1,0:T(8,128)(2,1)} %get-tuple-element.44), channel_id=1, source_target_pairs={{0,1},{1,0},{2,3},{3,2},{4,5},{5,4},{6,7},{7,6},{8,9},{9,8},{10,11... | collective-permute-start | bytes 1179656 | tf_op jit(solution)/shard_map/ppermute | solution.py:26
  73.9 5.2 %collective-permute-start.15 = (bf16[1664,128]{1,0:T(8,128)(2,1)S(1)}, bf16[1664,128]{1,0:T(8,128)(2,1)S(1)}, u32[]{:S(2)}, u32[]{:S(2)}) collective-permute-start(bf16[1664,128]{1,0:T(8,128)(2,1)S(1)} %constant_dynamic-update-slice_fusion.5), channel_id=1, source_target_pairs={{0,1},{1,0},{2,3},{3,2},{4,5},{5,4},{6,7},{7,6},{8,9},{9,8},{10,11... | collective-permute-start | bytes 1277960 | tf_op jit(solution)/shard_map/ppermute | solution.py:26
  75.8 8.5 %copy-start.9 = (bf16[2,2,192,256]{3,2,1,0:T(8,128)(2,1)}, bf16[2,2,192,256]{3,2,1,0:T(8,128)(2,1)S(1)}, u32[]{:S(2)}) copy-start(bf16[2,2,192,256]{3,2,1,0:T(8,128)(2,1)S(1)} %collective-permute-done.12.rcore) | copy-start | bytes 1179652
  77.0 7.3 %collective-permute-start.13 = (bf16[2,192,256]{2,1,0:T(8,128)(2,1)S(1)}, bf16[2,192,256]{2,1,0:T(8,128)(2,1)S(1)}, u32[]{:S(2)}, u32[]{:S(2)}) collective-permute-start(bf16[2,192,256]{2,1,0:T(8,128)(2,1)S(1)} %fusion.1), channel_id=1, source_target_pairs={{0,2},{2,0},{1,3},{3,1},{4,6},{6,4},{5,7},{7,5},{8,10},{10,8},{9,1... | collective-permute-start | bytes 589832 | tf_op jit(solution)/shard_map/ppermute | solution.py:26
  90.0 7.5 %copy-start.11 = (f32[2,4,4,16,384]{4,3,2,1,0:T(8,128)S(1)}, f32[2,4,4,16,384]{4,3,2,1,0:T(8,128)}, u32[]{:S(2)}) copy-start(f32[2,4,4,16,384]{4,3,2,1,0:T(8,128)} %get-tuple-element.48) | copy-start | bytes 2359300
  90.0 7.3 %collective-permute-start.16 = (bf16[896,128]{1,0:T(8,128)(2,1)}, bf16[896,128]{1,0:T(8,128)(2,1)S(1)}, u32[]{:S(2)}, u32[]{:S(2)}) collective-permute-start(bf16[896,128]{1,0:T(8,128)(2,1)} %get-tuple-element.45.zout), channel_id=1, source_target_pairs={{0,2},{2,0},{1,3},{3,1},{4,6},{6,4},{5,7},{7,5},{8,10},{10,8},{9,1... | collective-permute-start | bytes 688136 | tf_op jit(solution)/shard_map/ppermute | solution.py:26
  91.7 5.7 %collective-permute-start.18 = (bf16[2,4,4,16,384]{4,3,2,1,0:T(8,128)(2,1)}, bf16[2,4,4,16,384]{4,3,2,1,0:T(8,128)(2,1)S(1)}, u32[]{:S(2)}, u32[]{:S(2)}) collective-permute-start(bf16[2,4,4,16,384]{4,3,2,1,0:T(8,128)(2,1)} %get-tuple-element.49), channel_id=1, source_target_pairs={{0,1},{1,0},{2,3},{3,2},{4,5},{5,4},{6,7},{7,6},{8,9},{9,8},{10,11... | collective-permute-start | bytes 1179656 | tf_op jit(solution)/shard_map/ppermute | solution.py:26
  97.3 1.9 %collective-permute-start.17 = (bf16[1664,128]{1,0:T(8,128)(2,1)S(1)}, bf16[1664,128]{1,0:T(8,128)(2,1)S(1)}, u32[]{:S(2)}, u32[]{:S(2)}) collective-permute-start(bf16[1664,128]{1,0:T(8,128)(2,1)S(1)} %pad_maximum_fusion), channel_id=1, source_target_pairs={{0,1},{1,0},{2,3},{3,2},{4,5},{5,4},{6,7},{7,6},{8,9},{9,8},{10,11... | collective-permute-start | bytes 1277960 | tf_op jit(solution)/shard_map/ppermute | solution.py:26
  97.6 11.6 %collective-permute-start.19 = (bf16[4,4,16,384]{3,2,1,0:T(8,128)(2,1)S(1)}, bf16[4,4,16,384]{3,2,1,0:T(8,128)(2,1)S(1)}, u32[]{:S(2)}, u32[]{:S(2)}) collective-permute-start(bf16[4,4,16,384]{3,2,1,0:T(8,128)(2,1)S(1)} %fusion.2), channel_id=1, source_target_pairs={{0,2},{2,0},{1,3},{3,1},{4,6},{6,4},{5,7},{7,5},{8,10},{10,8},{9,1... | collective-permute-start | bytes 589832 | tf_op jit(solution)/shard_map/ppermute | solution.py:26
  104.4 18.3 %collective-permute-start.26 = (bf16[4,256,128]{2,1,0:T(8,128)(2,1)}, bf16[4,256,128]{2,1,0:T(8,128)(2,1)S(1)}, u32[]{:S(2)}, u32[]{:S(2)}) collective-permute-start(bf16[4,256,128]{2,1,0:T(8,128)(2,1)} %get-tuple-element.61), channel_id=1, source_target_pairs={{0,64},{64,128},{128,192},{192,0},{1,65},{65,129},{129,193},{193,1... | collective-permute-start | bytes 786440 | tf_op jit(solution)/shard_map/ppermute | solution.py:26
  106.2 17.9 %collective-permute-start.27 = (bf16[4,256,128]{2,1,0:T(8,128)(2,1)}, bf16[4,256,128]{2,1,0:T(8,128)(2,1)S(1)}, u32[]{:S(2)}, u32[]{:S(2)}) collective-permute-start(bf16[4,256,128]{2,1,0:T(8,128)(2,1)} %get-tuple-element.62), channel_id=1, source_target_pairs={{0,128},{64,192},{128,0},{192,64},{1,129},{65,193},{129,1},{193,65... | collective-permute-start | bytes 786440 | tf_op jit(solution)/shard_map/ppermute | solution.py:26
  108.2 15.9 %copy-start.16 = (bf16[4,256,128]{2,1,0:T(8,128)(2,1)S(1)}, bf16[4,256,128]{2,1,0:T(8,128)(2,1)}, u32[]{:S(2)}) copy-start(bf16[4,256,128]{2,1,0:T(8,128)(2,1)} %get-tuple-element.60) | copy-start | bytes 786436
  108.2 15.9 %collective-permute-start.28 = (bf16[4,256,128]{2,1,0:T(8,128)(2,1)}, bf16[4,256,128]{2,1,0:T(8,128)(2,1)S(1)}, u32[]{:S(2)}, u32[]{:S(2)}) collective-permute-start(bf16[4,256,128]{2,1,0:T(8,128)(2,1)} %get-tuple-element.63), channel_id=1, source_target_pairs={{0,192},{64,0},{128,64},{192,128},{1,193},{65,1},{129,65},{193,129... | collective-permute-start | bytes 786440 | tf_op jit(solution)/shard_map/ppermute | solution.py:26
  120.1 14.5 %collective-permute-start.20 = (bf16[1024,128]{1,0:T(8,128)(2,1)}, bf16[1024,128]{1,0:T(8,128)(2,1)S(1)}, u32[]{:S(2)}, u32[]{:S(2)}) collective-permute-start(bf16[1024,128]{1,0:T(8,128)(2,1)} %get-tuple-element.51), channel_id=1, source_target_pairs={{0,64},{64,128},{128,192},{192,0},{1,65},{65,129},{129,193},{193,1... | collective-permute-start | bytes 786440 | tf_op jit(solution)/shard_map/ppermute | solution.py:26
  121.2 17.8 %collective-permute-start.21 = (bf16[1024,128]{1,0:T(8,128)(2,1)}, bf16[1024,128]{1,0:T(8,128)(2,1)S(1)}, u32[]{:S(2)}, u32[]{:S(2)}) collective-permute-start(bf16[1024,128]{1,0:T(8,128)(2,1)} %get-tuple-element.52), channel_id=1, source_target_pairs={{0,128},{64,192},{128,0},{192,64},{1,129},{65,193},{129,1},{193,65... | collective-permute-start | bytes 786440 | tf_op jit(solution)/shard_map/ppermute | solution.py:26
  122.7 16.3 %collective-permute-start.22 = (bf16[1024,128]{1,0:T(8,128)(2,1)}, bf16[1024,128]{1,0:T(8,128)(2,1)S(1)}, u32[]{:S(2)}, u32[]{:S(2)}) collective-permute-start(bf16[1024,128]{1,0:T(8,128)(2,1)} %get-tuple-element.53), channel_id=1, source_target_pairs={{0,192},{64,0},{128,64},{192,128},{1,193},{65,1},{129,65},{193,129... | collective-permute-start | bytes 786440 | tf_op jit(solution)/shard_map/ppermute | solution.py:26
  124.3 21.5 %collective-permute-start.29 = (bf16[256,128]{1,0:T(8,128)(2,1)S(1)}, bf16[256,128]{1,0:T(8,128)(2,1)S(1)}, u32[]{:S(2)}, u32[]{:S(2)}) collective-permute-start(bf16[256,128]{1,0:T(8,128)(2,1)S(1)} %get-tuple-element.83), channel_id=1, source_target_pairs={{0,12},{4,0},{8,4},{12,8},{1,13},{5,1},{9,5},{13,9},{2,14},{6,2},{... | collective-permute-start | bytes 196616 | tf_op jit(solution)/shard_map/ppermute | solution.py:26
  127.0 19.3 %collective-permute-start.31 = (bf16[256,128]{1,0:T(8,128)(2,1)S(1)}, bf16[256,128]{1,0:T(8,128)(2,1)S(1)}, u32[]{:S(2)}, u32[]{:S(2)}) collective-permute-start(bf16[256,128]{1,0:T(8,128)(2,1)S(1)} %get-tuple-element.84), channel_id=1, source_target_pairs={{0,4},{4,8},{8,12},{12,0},{1,5},{5,9},{9,13},{13,1},{2,6},{6,10},{... | collective-permute-start | bytes 196616 | tf_op jit(solution)/shard_map/ppermute | solution.py:26
  134.6 11.7 %collective-permute-start.30 = (bf16[256,128]{1,0:T(8,128)(2,1)S(1)}, bf16[256,128]{1,0:T(8,128)(2,1)S(1)}, u32[]{:S(2)}, u32[]{:S(2)}) collective-permute-start(bf16[256,128]{1,0:T(8,128)(2,1)S(1)} %get-tuple-element.85), channel_id=1, source_target_pairs={{0,8},{4,12},{8,0},{12,4},{1,9},{5,13},{9,1},{13,5},{2,10},{6,14},... | collective-permute-start | bytes 196616 | tf_op jit(solution)/shard_map/ppermute | solution.py:26
  141.8 13.3 %collective-permute-start.23 = (bf16[576,128]{1,0:T(8,128)(2,1)}, bf16[576,128]{1,0:T(8,128)(2,1)S(1)}, u32[]{:S(2)}, u32[]{:S(2)}) collective-permute-start(bf16[576,128]{1,0:T(8,128)(2,1)} %get-tuple-element.55), channel_id=1, source_target_pairs={{0,12},{4,0},{8,4},{12,8},{1,13},{5,1},{9,5},{13,9},{2,14},{6,2},{... | collective-permute-start | bytes 442376 | tf_op jit(solution)/shard_map/ppermute | solution.py:26
  141.8 13.3 %collective-permute-start.24 = (bf16[576,128]{1,0:T(8,128)(2,1)}, bf16[576,128]{1,0:T(8,128)(2,1)S(1)}, u32[]{:S(2)}, u32[]{:S(2)}) collective-permute-start(bf16[576,128]{1,0:T(8,128)(2,1)} %get-tuple-element.56), channel_id=1, source_target_pairs={{0,8},{4,12},{8,0},{12,4},{1,9},{5,13},{9,1},{13,5},{2,10},{6,14},... | collective-permute-start | bytes 442376 | tf_op jit(solution)/shard_map/ppermute | solution.py:26
  145.8 10.7 %collective-permute-start.25 = (bf16[576,128]{1,0:T(8,128)(2,1)}, bf16[576,128]{1,0:T(8,128)(2,1)S(1)}, u32[]{:S(2)}, u32[]{:S(2)}) collective-permute-start(bf16[576,128]{1,0:T(8,128)(2,1)} %get-tuple-element.57), channel_id=1, source_target_pairs={{0,4},{4,8},{8,12},{12,0},{1,5},{5,9},{9,13},{13,1},{2,6},{6,10},{... | collective-permute-start | bytes 442376 | tf_op jit(solution)/shard_map/ppermute | solution.py:26
  161.0 6.4 %collective-permute-start.34 = (bf16[320,128]{1,0:T(8,128)(2,1)S(1)}, bf16[320,128]{1,0:T(8,128)(2,1)S(1)}, u32[]{:S(2)}, u32[]{:S(2)}) collective-permute-start(bf16[320,128]{1,0:T(8,128)(2,1)S(1)} %fusion.3), channel_id=1, source_target_pairs={{0,48},{16,0},{32,16},{48,32},{1,49},{17,1},{33,17},{49,33},{2,50}... | collective-permute-start | bytes 245768 | tf_op jit(solution)/shard_map/ppermute | solution.py:26
  163.7 5.9 %collective-permute-start.33 = (bf16[320,128]{1,0:T(8,128)(2,1)S(1)}, bf16[320,128]{1,0:T(8,128)(2,1)S(1)}, u32[]{:S(2)}, u32[]{:S(2)}) collective-permute-start(bf16[320,128]{1,0:T(8,128)(2,1)S(1)} %fusion.3), channel_id=1, source_target_pairs={{0,32},{16,48},{32,0},{48,16},{1,33},{17,49},{33,1},{49,17},{2,34}... | collective-permute-start | bytes 245768 | tf_op jit(solution)/shard_map/ppermute | solution.py:26
  163.7 5.9 %collective-permute-start.32 = (bf16[320,128]{1,0:T(8,128)(2,1)S(1)}, bf16[320,128]{1,0:T(8,128)(2,1)S(1)}, u32[]{:S(2)}, u32[]{:S(2)}) collective-permute-start(bf16[320,128]{1,0:T(8,128)(2,1)S(1)} %fusion.3), channel_id=1, source_target_pairs={{0,16},{16,32},{32,48},{48,0},{1,17},{17,33},{33,49},{49,1},{2,18}... | collective-permute-start | bytes 245768 | tf_op jit(solution)/shard_map/ppermute | solution.py:26
  (15 other events, 30.7 us)
where the time goes:
time: 176 us; the launch traced here: 173 us
  starting transfers between devices  58.1 us (33%)
  waiting for transfers between devices  52.7 us (30%)
  Pallas kernels  42.4 us (24%)
  local copies, waits for them, and re-layouts  13.6 us (8%)
  other arithmetic  5.2 us (3%)
    ppermute x35, starting transfers between devices, shift(): return lax.ppermute(x, axis, [(i, (i + k) % n) for i in range(n)])  58.1 us
    ppermute x35, waiting for transfers between devices, shift(): return lax.ppermute(x, axis, [(i, (i + k) % n) for i in range(n)])  52.7 us
    pallas_call x9, Pallas kernels, call(): pl.pallas_call(kernel, grid_spec=pltpu.PrefetchScalarGridSpec(num_scalar_...  42.4 us
    unnamed x71, local copies, waits for them, and re-layouts  10.3 us
  transfers between devices with their start and end apart: 35, of which 10 were waited for; matrix products, arithmetic and copies ran while one was open for 6% of the time, Pallas kernels for 16%

commit v1 on v0

--- a/solution.py
+++ b/solution.py
@@ -1,3 +1,4 @@
+import functools
 import math
 
 import jax
@@ -57,8 +58,8 @@
     rows = pl.ds(pl.multiple_of(32 * sc[5], 32), 32)
     out[0:32, :] = pw[0, rows, 0:128]
     out[32:64, :] = pw[0, rows, 128:256]
-    out[64:80, :] = proj[0, :, 0:128]
-    out[80:96, :] = proj[0, :, 128:256]
+    out[80:96, :] = proj[0, :, 0:128]
+    out[96:112, :] = proj[0, :, 128:256]
     i = lax.broadcasted_iota(jnp.int32, (16, 16), 0)
     j = lax.broadcasted_iota(jnp.int32, (16, 16), 1)
     lane = lax.broadcasted_iota(jnp.int32, (16, 128), 1)
@@ -69,9 +70,33 @@
             part = rest.astype(BF).astype(F32)
             ext = ext + jnp.where(lane == 3 * n + piece, part, 0.0)
             rest = rest - part
-    out[96:112, :] = ext.astype(BF)
+    out[112:128, :] = ext.astype(BF)
     taps = jnp.concatenate([dw[0].astype(F32), jnp.zeros((7, 128), F32)], axis=0)
-    out[112:128, :] = taps.astype(BF)
+    out[64:80, :] = taps.astype(BF)
+
+
+def branch_kernel(sc, off, wid, b0, b1, b2, b3, out):
+    for r, b in enumerate((b0, b1, b2, b3)):
+        out[64 * r:64 * r + 64, :] = b[0:64, :]
+        out[304 + 16 * r:320 + 16 * r, :] = b[64:80, :]
+
+        @pl.when(sc[5] == r)
+        def _(b=b):
+            out[256:304, :] = b[80:128, :]
+
+
+def proj_kernel(sc, off, wid, q0, q1, q2, q3, own, wfull):
+    for j, qj in enumerate((q0, q1, q2, q3)):
+        d = back(sc[5], j)
+        lanes = pl.ds(pl.multiple_of(32 * d, 32), 32)
+        for k in range(4):
+            for r in range(4):
+                s = back(sc[1], r)
+                for b in range(2):
+                    at = 304 * k + 64 * r + 32 * b
+                    wfull[k, s, lanes, 128 * b:128 * b + 128] = qj[at:at + 32, :]
+            at = 304 * k + 256
+            own[pl.ds(pl.multiple_of(192 * k + 48 * d, 16), 48), :] = qj[at:at + 48, :]
 
 
 def select_kernel(sc, off, wid, x, up, o0, o1, o2, o3, uscr):
@@ -120,7 +145,7 @@
     fill_x((x0, x1, x2, x3), xscr)
     for k, a in enumerate((a0, a1, a2, a3)):
         for r in range(4):
-            dws[k, back(sc[1], r)] = a[r, 112:128, :].astype(F32)
+            dws[k, back(sc[1], r)] = a[304 + 16 * r:320 + 16 * r, :].astype(F32)
 
     def body(i, _):
         k = i // 8
@@ -146,15 +171,8 @@
     lax.fori_loop(0, 32, body, 0)
 
 
-def product_kernel(sc, off, wid, depth, q0, q1, q2, q3, keep, send, wfull, pscr):
+def product_kernel(sc, off, wid, depth, wfull, x0, x1, x2, x3, keep, send, pscr):
     mz, mc = sc[3], sc[4]
-    for j, qj in enumerate((q0, q1, q2, q3)):
-        rows = pl.ds(pl.multiple_of(32 * back(sc[5], j), 32), 32)
-        for k in range(4):
-            for r in range(4):
-                s = back(sc[1], r)
-                wfull[k, s, rows, 0:128] = qj[k, r, 0:32, :]
-                wfull[k, s, rows, 128:256] = qj[k, r, 32:64, :]
     for s in range(4):
         n = WIN[s]
         acc = None
@@ -169,10 +187,26 @@
         zz = 2 * jnp.bitwise_xor(mz, zr)
         for r in range(2):
             keep[zr, r] = pscr[4 * mc + zz + r]
-            send[zr, r] = pscr[4 * (1 - mc) + zz + r].astype(BF)
-
-
-def middle_kernel(sc, off, wid, keep, rcore, rzl, pj, zin, cin, f0, f1, f2, f3, labels,
+            for b in range(2):
+                at = 768 * zr + 384 * b + 192 * r
+                send[at:at + 192, :] = pscr[4 * (1 - mc) + zz + r, :, 128 * b:128 * b + 128].astype(BF)
+        for k, x in enumerate((x0, x1, x2, x3)):
+            at = 1536 + 64 * zr + 16 * k
+            send[at:at + 16, :] = x[528 + 32 * zr:544 + 32 * zr, :]
+
+
+def add_kernel(keep, rcore, x0, x1, x2, x3, out):
+    for r in range(2):
+        for b in range(2):
+            at = 384 * b + 192 * r
+            v = keep[1, r, :, 128 * b:128 * b + 128] + rcore[768 + at:960 + at, :].astype(F32)
+            out[at:at + 192, :] = v.astype(BF)
+    for k, x in enumerate((x0, x1, x2, x3)):
+        out[768 + 32 * k:784 + 32 * k, :] = x[544:560, :]
+        out[784 + 32 * k:800 + 32 * k, :] = rcore[1600 + 16 * k:1616 + 16 * k, :]
+
+
+def middle_kernel(sc, off, wid, keep, rcore, rzl, own, ownz, ownc, ownzc, f0, f1, f2, f3, labels,
                   zout, res0, gkeep, gsend, pjs, upscr, gscr):
     q, zh, mz, mc = sc[1], sc[2], sc[3], sc[4]
     fs = (f0, f1, f2, f3)
@@ -183,19 +217,11 @@
             base = 48 * (4 * k + r)
             for b in range(3):
                 at = base + 16 * b
-                if zr == 0 and cr == 0:
-                    v = pj[k, r, 16 * b:16 * b + 16, :]
-                elif cr == 0:
-                    v = zin[at:at + 16, :]
-                else:
-                    v = cin[768 * zr + at:768 * zr + at + 16, :]
-                pjs[s, rows, 128 * b:128 * b + 128] = v
-        if zr == 0 and cr == 0:
-            u = fs[k][512:528, :]
-        elif cr == 0:
-            u = zin[768 + 32 * k:784 + 32 * k, :]
+                pjs[s, rows, 128 * b:128 * b + 128] = ((own, ownz), (ownc, ownzc))[cr][zr][at:at + 16, :]
+        if zr == 0:
+            u = fs[k][512:528, :] if cr == 0 else rcore[1536 + 16 * k:1552 + 16 * k, :]
         else:
-            u = cin[1536 + 64 * zr + 16 * k:1552 + 64 * zr + 16 * k, :]
+            u = rzl[768 + 32 * k + 16 * cr:784 + 32 * k + 16 * cr, :]
         upscr[rows, :] = u.astype(F32)
     frame, cp = zh // 2, lax.rem(zh, 2)
     w = lax.broadcasted_iota(jnp.int32, (64, 128), 1)
@@ -209,7 +235,12 @@
     lab = jnp.concatenate(cols, axis=0)
 
     lane = lax.broadcasted_iota(jnp.int32, (8, 128), 1)
-    pre_now = keep[0] + rcore[0].astype(F32) + rzl[...].astype(F32)
+    sums = []
+    for r in range(2):
+        got = [rcore[384 * b + 192 * r:384 * b + 192 * r + 192, :].astype(F32)
+               + rzl[384 * b + 192 * r:384 * b + 192 * r + 192, :].astype(F32) for b in range(2)]
+        sums.append(keep[0, r] + jnp.concatenate(got, axis=1))
+    pre_now = jnp.stack(sums)
     pres, acts = [], []
     z = dotf(jnp.where((lane >= 3) & (lane < 6), 1.0, 0.0).astype(BF), pjs[0, :, 256:384], ((1,), (1,)))[0:1, :]
     for s in range(4):
@@ -259,7 +290,7 @@
                 gsend[zr, r, k] = g.astype(BF)
 
 
-def weight_kernel(sc, off, wid, depth, zout, zin, cin, g0, g1, g2, g3, pgs, gbuf):
+def weight_kernel(sc, off, wid, depth, zout, zin, cin, res0, g0, g1, g2, g3, pgs, gbuf):
     mz, mc = sc[3], sc[4]
     for zr in range(2):
         for cr in range(2):
@@ -275,13 +306,15 @@
         for k in range(4):
             dep = depth[k, :, SOFF[s]:SOFF[s] + n, :].reshape(8 * n, 128)
             g = dotf(dep, pg, ((0,), (0,)))
-            gbuf[s, k, 0:128, :] = g[:, 0:128].astype(BF)
-            gbuf[s, k, 128:256, :] = g[:, 128:256].astype(BF)
+            gbuf[s, 256 * k:256 * k + 128, :] = g[:, 0:128].astype(BF)
+            gbuf[s, 256 * k + 128:256 * k + 256, :] = g[:, 128:256].astype(BF)
     for r, g in enumerate((g0, g1, g2, g3)):
-        g[...] = gbuf[lax.rem(sc[1] + r, 4)]
-
-
-def backward_kernel(sc, off, wid, x0, x1, x2, x3, wfull, dws, pgs, gpr, res0, zin, cin,
+        g[0:1024, :] = gbuf[lax.rem(sc[1] + r, 4)]
+        for b, (src, at) in enumerate(((res0, 0), (cin, 1536), (zin, 768), (cin, 1600))):
+            g[1024 + 64 * b:1088 + 64 * b, :] = src[at:at + 64, :]
+
+
+def backward_kernel(sc, off, wid, x0, x1, x2, x3, wfull, dws, pgs, gpr,
                     o0, o1, o2, o3, xscr, dgs, yscr, dwa):
     hf, q, f, cp = sc[0], sc[1], sc[2] // 2, lax.rem(sc[2], 2)
     col = off[f]
@@ -354,38 +387,54 @@
             for b in range(3):
                 at = 576 + 48 * k + 16 * b
                 o[at:at + 16, :] = gpr[r, k, :, 128 * b:128 * b + 128].astype(BF)
-        o[768:832, :] = res0[0:64, :]
-        o[832:896, :] = cin[1536:1600, :]
-        o[896:960, :] = zin[768:832, :]
-        o[960:1024, :] = cin[1600:1664, :]
 
 
 def combine_kernel(v0, v1, v2, v3, o0, o1, o2, o3):
-    vs = (v0, v1, v2, v3)
     for k, o in enumerate((o0, o1, o2, o3)):
         ys = slice(128 * k, 128 * k + 128)
         o[0:128, :] = (v0[ys, :].astype(F32) + v2[ys, :].astype(F32)).astype(BF)
         o[128:256, :] = (v1[ys, :].astype(F32) + v3[ys, :].astype(F32)).astype(BF)
         for at, src, n in ((256, 512 + 16 * k, 16), (272, 576 + 48 * k, 48)):
             tot = v0[src:src + n, :].astype(F32)
-            for v in vs[1:]:
+            for v in (v1, v2, v3):
                 tot = tot + v[src:src + n, :].astype(F32)
             o[at:at + n, :] = tot.astype(BF)
-        for r, v in enumerate(vs):
+
+
+def gather_kernel(g0, g1, g2, g3, own, o0, o1, o2, o3):
+    gs = (g0, g1, g2, g3)
+    for k, o in enumerate((o0, o1, o2, o3)):
+        tot = g0[256 * k:256 * k + 256, :].astype(F32)
+        for g in gs[1:]:
+            tot = tot + g[256 * k:256 * k + 256, :].astype(F32)
+        if k == 0:
+            own[...] = tot
+        o[0:256, :] = tot.astype(BF)
+        for r, g in enumerate(gs):
             for b in range(4):
-                at = 320 + 64 * r + 16 * b
-                o[at:at + 16, :] = v[768 + 64 * b + 16 * k:784 + 64 * b + 16 * k, :]
-
-
-def restore_kernel(sc, off, wid, z0, z1, z2, z3, out, asp, small, zs, yscr, ascr):
+                at = 256 + 64 * r + 16 * b
+                o[at:at + 16, :] = g[1024 + 64 * b + 16 * k:1040 + 64 * b + 16 * k, :]
+
+
+def sum_kernel(z0, z1, z2, z3, gown, h1, h2, h3, own, ownb):
+    tot = gown[...]
+    for h in (h1, h2, h3):
+        tot = tot + h[0:256, :].astype(F32)
+    own[0:256, :] = tot
+    ownb[0:256, :] = tot.astype(BF)
+    tot = z0[256:320, :].astype(F32)
+    for z in (z1, z2, z3):
+        tot = tot + z[256:320, :].astype(F32)
+    own[256:320, :] = tot
+    ownb[256:320, :] = tot.astype(BF)
+
+
+def restore_kernel(sc, off, wid, z0, z1, z2, z3, h0, h1, h2, h3, out, asp, zs, rs, ascr):
     q, zh, mz, mc, rp = sc[1], sc[2], sc[3], sc[4], sc[6]
-    tot = None
-    for k, z in enumerate((z0, z1, z2, z3)):
+    for k, (z, h) in enumerate(((z0, h0), (z1, h1), (z2, h2), (z3, h3))):
         src = lax.rem(zh + k, 4)
         zs[src] = z[...]
-        v = z[256:320, :].astype(F32)
-        tot = v if tot is None else tot + v
-    small[...] = tot
+        rs[src] = h[256:512, :]
     for f in range(2):
         w = lax.broadcasted_iota(jnp.int32, (128, 64), 0)
         x = lax.broadcasted_iota(jnp.int32, (128, 64), 1)
@@ -402,16 +451,32 @@
             for zr in range(2):
                 for cr in range(2):
                     t0 = 8 * (qs // 2) + 4 * jnp.bitwise_xor(mc, cr) + 2 * jnp.bitwise_xor(mz, zr)
-                    at = 320 + 64 * r + 32 * zr + 16 * cr
+                    at = 64 * r + 32 * zr + 16 * cr
                     for e in range(2):
                         h = 2 * (t0 + e) + lax.rem(qs, 2)
                         ascr[h] = jnp.concatenate(
-                            [zs[2 * f, at:at + 16, 64 * e:64 * e + 64],
-                             zs[2 * f + 1, at:at + 16, 64 * e:64 * e + 64]], axis=1)
+                            [rs[2 * f, at:at + 16, 64 * e:64 * e + 64],
+                             rs[2 * f + 1, at:at + 16, 64 * e:64 * e + 64]], axis=1)
         asp[f] = dotf(ascr[...].reshape(512, 128), perm_matrix(off[f], True)).astype(BF).reshape(32, 16, 128)
 
 
-def call(kernel, scalars, args, outs, scratch=(), in_specs=None):
+def final_kernel(own, d1, d2, d3, dw, pw, pwb, proj, pb, *, scaling):
+    tot = (own[...] + d1[...].astype(F32) + d2[...].astype(F32) + d3[...].astype(F32)) * scaling
+    pw[0, :, 0:128] = tot[0:128]
+    pw[0, :, 128:256] = tot[128:256]
+    for t in range(9):
+        dw[t] = tot[256 + t:257 + t]
+    proj[0, :, 0:128] = tot[272:288]
+    proj[0, :, 128:256] = tot[288:304]
+    ext = tot[304:320]
+    i = lax.broadcasted_iota(jnp.int32, (16, 16), 0)
+    j = lax.broadcasted_iota(jnp.int32, (16, 16), 1)
+    for o, lane in ((pwb, 0), (pb, 64)):
+        col = jnp.broadcast_to(ext[:, lane:lane + 1], (16, 16))
+        o[...] = jnp.sum(jnp.where(i == j, col, 0.0), axis=0, keepdims=True)
+
+
+def call(kernel, scalars, args, outs, scratch=(), in_specs=None, us=1):
     whole = pl.BlockSpec(memory_space=pltpu.VMEM)
     specs = in_specs if in_specs is not None else [whole] * len(args)
     return pl.pallas_call(
@@ -422,6 +487,7 @@
             scratch_shapes=[pltpu.VMEM(s, d) for s, d in scratch]),
         out_shape=[jax.ShapeDtypeStruct(s, d) for s, d in outs],
         compiler_params=pltpu.CompilerParams(vmem_limit_bytes=VM),
+        cost_estimate=pl.CostEstimate(flops=us * 10 ** 9, bytes_accessed=us * 3 * 10 ** 6, transcendentals=0),
     )(*scalars, *args)
 
 
@@ -434,81 +500,75 @@
     scaling = 1.0 / math.sqrt(8192.0 * lax.axis_size("dp"))
 
     (blk,) = call(pack_kernel, sc, [pw_weight, dw_kernel, proj, pw_bias, proj_bias[None]], [((128, 128), BF)])
-    wz = gather_rel(jnp.stack(gather_rel(blk, "section")), "zh")
-    quarters = gather_rel(jnp.stack([a[:, 0:64] for a in wz]), "dp")
+    wb = gather_rel(blk, "section")
 
     upx = upstream.reshape(16, 2, 2, 8, 2, 128)
     upx = lax.dynamic_slice(upx, (0, 0, hf, 0, rp, 0), (16, 2, 1, 8, 1, 128)).reshape(16, 2, 8, 128)
     upx = upx.transpose(1, 2, 0, 3)
     xs = call(
         select_kernel, sc, [feats.reshape(2, 16, 2, 128, 128), upx], [((576, 128), BF)] * 4,
-        scratch=[((4, 8, 16, 64), F32)],
+        scratch=[((4, 8, 16, 64), F32)], us=5,
         in_specs=[pl.BlockSpec((2, 16, 1, 128, 128), lambda i, sc, off, wid: (0, 0, sc[6], 0, 0)),
                   pl.BlockSpec((2, 8, 16, 128), lambda i, *a: (0, 0, 0, 0))])
+
+    wb, xs = lax.optimization_barrier((wb, xs))
+    (wown,) = call(branch_kernel, sc, wb, [((368, 128), BF)])
+    wown, xs = lax.optimization_barrier((wown, xs))
+    wz = gather_rel(wown, "zh")
+    quart = jnp.concatenate([a[0:304] for a in wz], axis=0)
     xs = [xs[0]] + [shift(xs[k], "zh", k) for k in range(1, 4)]
-
+    quarters = gather_rel(quart, "dp")
+    own, wfull = call(proj_kernel, sc, quarters, [((768, 128), BF), ((4, 4, 128, 256), BF)])
+    xs, own, wfull = lax.optimization_barrier((xs, own, wfull))
     depth, dws = call(
         depth_kernel, sc, [*xs, *wz], [((4, 8, NCOL, 128), BF), ((4, 4, 16, 128), F32)],
-        scratch=[((4, 34, 96, 128), F32)])
-    keep, send, wfull = call(
-        product_kernel, sc, [depth, *quarters],
-        [((2, 2, NCOL, 256), F32), ((2, 2, NCOL, 256), BF), ((4, 4, 128, 256), BF)],
-        scratch=[((8, NCOL, 256), F32)])
-
-    pj = jnp.stack([a[:, 64:112] for a in wz])
-    pjflat = pj.reshape(768, 128)
-    uz = shift(jnp.concatenate([pjflat] + [x[544:576] for x in xs], axis=0), "zl", 1)
-    uc = shift(jnp.concatenate(
-        [pjflat, uz[0:768]] + [x[528:544] for x in xs] + [uz[784 + 32 * k:800 + 32 * k] for k in range(4)],
-        axis=0), "core", 1)
-
+        scratch=[((4, 34, 96, 128), F32)], us=6)
+    ownz = shift(own, "zl", 1)
+    ownc = shift(own, "core", 1)
+    ownzc = shift(ownz, "core", 1)
+    keep, send = call(
+        product_kernel, sc, [depth, wfull, *xs], [((2, 2, NCOL, 256), F32), ((1664, 128), BF)],
+        scratch=[((8, NCOL, 256), F32)], us=4)
     rcore = shift(send, "core", 1)
-    rzl = shift((keep[1] + rcore[1].astype(F32)).astype(BF), "zl", 1)
+    (zsend,) = call(add_kernel, (), [keep, rcore, *xs], [((896, 128), BF)])
+    rzl = shift(zsend, "zl", 1)
     zout, res0, gkeep, gsend = call(
-        middle_kernel, sc, [keep, rcore, rzl, pj, uz, uc, *xs, labels],
+        middle_kernel, sc, [keep, rcore, rzl, own, ownz, ownc, ownzc, *xs, labels],
         [((896, 128), BF), ((128, 128), BF), ((2, 4, 4, 16, 384), F32), ((2, 4, 4, 16, 384), BF)],
-        scratch=[((4, 256, 384), BF), ((256, 128), F32), ((4, 256, 384), F32)])
+        scratch=[((4, 256, 384), BF), ((256, 128), F32), ((4, 256, 384), F32)], us=5)
 
     zin = shift(zout, "zl", 1)
     cin = shift(jnp.concatenate([zout[0:768], zin[0:768], res0[64:128], zin[832:896]], axis=0), "core", 1)
     gz = gkeep + shift(gsend, "core", 1).astype(F32)
+
+    *gs, pgs = call(
+        weight_kernel, sc, [depth, zout, zin, cin, res0],
+        [((1280, 128), BF)] * 4 + [((8, NCOL, 256), BF)], scratch=[((4, 1024, 128), BF)], us=4)
+    gs = [gs[0]] + [shift(gs[k], "section", k) for k in range(1, 4)]
+    gz, pgs = lax.optimization_barrier((gz, pgs))
     gpr = gz[0] + shift(gz[1].astype(BF), "zl", 1).astype(F32)
-
-    *gs, pgs = call(
-        weight_kernel, sc, [depth, zout, zin, cin], [((4, 256, 128), BF)] * 4 + [((8, NCOL, 256), BF)],
-        scratch=[((4, 4, 256, 128), BF)])
     vs = call(
-        backward_kernel, sc, [*xs, wfull, dws, pgs, gpr, res0, zin, cin], [((1024, 128), BF)] * 4,
-        scratch=[((4, 34, 96, 128), F32), ((4, 8, NCOL, 128), F32), ((4, 26, 32, 128), F32), ((4, 36, 8, 128), F32)])
-
-    gsum = gs[0].astype(F32)
-    for k in range(1, 4):
-        gsum = gsum + shift(gs[k], "section", k).astype(F32)
-    gsb = gsum.astype(BF)
-    gown = gsum[0]
-    for k in range(1, 4):
-        gown = gown + shift(gsb[k], "zh", -k).astype(F32)
-
-    zs = call(combine_kernel, (), [vs[0]] + [shift(vs[k], "section", k) for k in range(1, 4)],
-              [((576, 128), BF)] * 4)
-    input_grad, asp, small = call(
-        restore_kernel, sc, [zs[0]] + [shift(zs[k], "zh", -k) for k in range(1, 4)],
-        [((2, 8, 128, 128), BF), ((2, 32, 16, 128), BF), ((64, 128), F32)],
-        scratch=[((4, 576, 128), BF), ((8, 128), F32), ((32, 16, 128), BF)])
-
-    own = jnp.concatenate([gown, small], axis=0)
-    ownb = own.astype(BF)
-    tot = own
-    for k in range(1, 4):
-        tot = tot + shift(ownb, "dp", k).astype(F32)
-    tot = tot * scaling
-    grad_pw = jnp.concatenate([tot[0:128], tot[128:256]], axis=1)
-    grad_dw = tot[256:265]
-    grad_proj = jnp.concatenate([tot[272:288], tot[288:304]], axis=1)
-    grad_pwb = tot[304:320, 0]
-    grad_pb = tot[304:320, 64]
+        backward_kernel, sc, [*xs, wfull, dws, pgs, gpr], [((768, 128), BF)] * 4,
+        scratch=[((4, 34, 96, 128), F32), ((4, 8, NCOL, 128), F32), ((4, 26, 32, 128), F32), ((4, 36, 8, 128), F32)],
+        us=10)
+    vs = [vs[0]] + [shift(vs[k], "section", k) for k in range(1, 4)]
+
+    gown, *hs = call(gather_kernel, (), gs, [((256, 128), F32)] + [((512, 128), BF)] * 4)
+    hs = [hs[0]] + [shift(hs[k], "zh", -k) for k in range(1, 4)]
+
+    zs = call(combine_kernel, (), vs, [((320, 128), BF)] * 4)
+    zs = [zs[0]] + [shift(zs[k], "zh", -k) for k in range(1, 4)]
+    own, ownb = call(sum_kernel, (), [*zs, gown, *hs[1:]], [((320, 128), F32), ((320, 128), BF)])
+    input_grad, asp = call(
+        restore_kernel, sc, [*zs, *hs],
+        [((2, 8, 128, 128), BF), ((2, 32, 16, 128), BF)],
+        scratch=[((4, 320, 128), BF), ((4, 256, 128), BF), ((32, 16, 128), BF)], us=3)
+    outs = call(
+        functools.partial(final_kernel, scaling=scaling), (), [own] + [shift(ownb, "dp", k) for k in range(1, 4)],
+        [((9, 1, 128), F32), ((1, 128, 256), F32), ((1, 16), F32), ((1, 16, 256), F32), ((1, 16), F32)])
+    grad_dw, grad_pw, grad_pwb, grad_proj, grad_pb = outs
     aspp = asp.transpose(2, 0, 1, 3)
-    return (aspp, input_grad, grad_dw[None], grad_pw[None], grad_pwb[None], grad_proj[None], grad_pb)
+    return (aspp, input_grad, grad_dw.reshape(1, 9, 128), grad_pw, grad_pwb, grad_proj, grad_pb[0])
 
 
 def solution(mesh):

time: 176 us -> 167 us (0.949); the launches traced: 173 us -> 166 us
  waiting for transfers between devices: 52.7 us -> 38.5 us
  Pallas kernels: 42.4 us -> 55.5 us
  other arithmetic: 5.2 us -> 0.93 us
    ppermute x35 -> x36, waiting for transfers between devices: 52.7 us -> 38.5 us  [shift(): return lax.ppermute(x, axis, [(i, (i + k) % n) for i in range(n)])]
    pallas_call x9 -> x15, Pallas kernels: 42.4 us -> 55.5 us  [call(): pl.pallas_call(kernel, grid_spec=pltpu.PrefetchScalarGridSpec(num_scalar_...]
    convert_element_type x3 -> x0, other arithmetic: 2.09 us -> none  [the longest x1 1.18 us: local(): rzl = shift((keep[1] + rcore[1].astype(F32)).astype(BF), 'zl', 1)]
    unnamed x71 -> x84, local copies, waits for them, and re-layouts: 10.3 us -> 9.52 us
    ppermute x35 -> x36, starting transfers between devices: 58.1 us -> 57.6 us  [shift(): return lax.ppermute(x, axis, [(i, (i + k) % n) for i in range(n)])]
  transfers between devices with their start and end apart: 35 -> 36, of which waited for: 10 -> 17; matrix products, arithmetic and copies ran while one was open for 6% -> 4% of each run, Pallas kernels for 16% -> 16%
where the time goes in v1:
time: 167 us; the launch traced here: 166 us
  starting transfers between devices  57.6 us (34%)
  Pallas kernels  55.5 us (33%)
  waiting for transfers between devices  38.5 us (23%)
  local copies, waits for them, and re-layouts  12.9 us (8%)
    ppermute x36, starting transfers between devices, shift(): return lax.ppermute(x, axis, [(i, (i + k) % n) for i in range(n)])  57.6 us
    pallas_call x15, Pallas kernels, call(): pl.pallas_call(kernel, grid_spec=pltpu.PrefetchScalarGridSpec(num_scalar_...  55.5 us
    ppermute x36, waiting for transfers between devices, shift(): return lax.ppermute(x, axis, [(i, (i + k) % n) for i in range(n)])  38.5 us
    unnamed x84, local copies, waits for them, and re-layouts  9.52 us
  transfers between devices with their start and end apart: 36, of which 17 were waited for; matrix products, arithmetic and copies ran while one was open for 4% of the time, Pallas kernels for 16%

profile of v1, /device:TPU:8, one launch (start us, length us, event | category | flops | bytes accessed | tf_op | source)
XLA Modules:
  0.0 166.4 jit_solution(16662502943424780106)
XLA Ops:
  1.3 2.3 %shard_map.153.b0 = bf16[128,128]{1,0:T(8,128)(2,1)} custom-call(s32[7]{0:T(128)} %stack.31.sc, s32[2]{0:T(128)} %off.19, s32[2]{0:T(128)} %wid.19, bf16[1,128,256]{2,1,0:T(8,128)(2,1)} %pw.1, bf16[1,9,128]{2,1,0:T(8,128)(2,1)} %dw.1, bf16[1,16,256]{2,1,0:T(8,128)(2,1)} %proj.1, f32[1,16]{1,0:T(1,128)} %pwb.1, f32[1,16]{1,0:T(1,128)} %bitcast.26), custom_call_target="tpu_custom_call" | custom-call | flops 1000000000 | bytes 3000000 | tf_op jit(solution)/shard_map/pallas_call | solution.py:482
  3.5 2.8 %collective-permute-start.2 = (bf16[128,128]{1,0:T(8,128)(2,1)}, bf16[128,128]{1,0:T(8,128)(2,1)S(1)}, u32[]{:S(2)}, u32[]{:S(2)}) collective-permute-start(bf16[128,128]{1,0:T(8,128)(2,1)} %shard_map.153.b0), channel_id=1, source_target_pairs={{0,192},{64,0},{128,64},{192,128},{1,193},{65,1},{129,65},{193,129... | collective-permute-start | bytes 98312 | tf_op jit(solution)/shard_map/ppermute | solution.py:27
  8.8 4.6 %shard_map.154 = (bf16[576,128]{1,0:T(8,128)(2,1)}, bf16[576,128]{1,0:T(8,128)(2,1)}, bf16[576,128]{1,0:T(8,128)(2,1)}, bf16[576,128]{1,0:T(8,128)(2,1)}) custom-call(s32[7]{0:T(128)} %stack.31.sc, s32[2]{0:T(128)} %off.19, s32[2]{0:T(128)} %wid.19, bf16[2,16,2,128,128]{4,3,2,1,0:T(8,128)(2,1)} %bitcast.25, bf16[2,8,16,128]{3,2,1,0:T(8,128)(2,1)} %bitcast.24), custom_call_target="tpu_custom_call" | custom-call | flops 5000000000 | bytes 15000000 | tf_op jit(solution)/shard_map/pallas_call | solution.py:482
  14.1 2.3 %shard_map.155.a0 = bf16[368,128]{1,0:T(8,128)(2,1)} custom-call(s32[7]{0:T(128)} %stack.31.sc, s32[2]{0:T(128)} %off.19, s32[2]{0:T(128)} %wid.19, bf16[128,128]{1,0:T(8,128)(2,1)} %shard_map.153.b0, bf16[128,128]{1,0:T(8,128)(2,1)} %copy-done.40, bf16[128,128]{1,0:T(8,128)(2,1)} %copy-done.39, bf16[128,128]{1,0:T(8,128)(2,1)} %copy-done.38), custom_call_target="tpu_custom_call" | custom-call | flops 1000000000 | bytes 3000000 | tf_op jit(solution)/shard_map/pallas_call | solution.py:482
  16.4 6.3 %collective-permute-start.8 = (bf16[368,128]{1,0:T(8,128)(2,1)}, bf16[368,128]{1,0:T(8,128)(2,1)S(1)}, u32[]{:S(2)}, u32[]{:S(2)}) collective-permute-start(bf16[368,128]{1,0:T(8,128)(2,1)} %shard_map.155.a0), channel_id=1, source_target_pairs={{0,12},{4,0},{8,4},{12,8},{1,13},{5,1},{9,5},{13,9},{2,14},{6,2},{... | collective-permute-start | bytes 282632 | tf_op jit(solution)/shard_map/ppermute | solution.py:27
  23.6 2.9 %collective-permute-start.6 = (bf16[368,128]{1,0:T(8,128)(2,1)}, bf16[368,128]{1,0:T(8,128)(2,1)S(1)}, u32[]{:S(2)}, u32[]{:S(2)}) collective-permute-start(bf16[368,128]{1,0:T(8,128)(2,1)} %shard_map.155.a0), channel_id=1, source_target_pairs={{0,4},{4,8},{8,12},{12,0},{1,5},{5,9},{9,13},{13,1},{2,6},{6,10},{... | collective-permute-start | bytes 282632 | tf_op jit(solution)/shard_map/ppermute | solution.py:27
  27.4 2.8 %collective-permute-done.8.a3 = bf16[368,128]{1,0:T(8,128)(2,1)S(1)} collective-permute-done((bf16[368,128]{1,0:T(8,128)(2,1)}, bf16[368,128]{1,0:T(8,128)(2,1)S(1)}, u32[]{:S(2)}, u32[]{:S(2)}) %collective-permute-start.8) | collective-permute-done | bytes 94240 | tf_op jit(solution)/shard_map/ppermute | solution.py:27
  30.2 3.5 %collective-permute-done.7.a2 = bf16[368,128]{1,0:T(8,128)(2,1)S(1)} collective-permute-done((bf16[368,128]{1,0:T(8,128)(2,1)}, bf16[368,128]{1,0:T(8,128)(2,1)S(1)}, u32[]{:S(2)}, u32[]{:S(2)}) %collective-permute-start.7) | collective-permute-done | bytes 94240 | tf_op jit(solution)/shard_map/ppermute | solution.py:27
  34.3 2.6 %collective-permute-start.10 = (bf16[1216,128]{1,0:T(8,128)(2,1)S(1)}, bf16[1216,128]{1,0:T(8,128)(2,1)S(1)}, u32[]{:S(2)}, u32[]{:S(2)}) collective-permute-start(bf16[1216,128]{1,0:T(8,128)(2,1)S(1)} %pad_maximum_fusion.1.q0), channel_id=1, source_target_pairs={{0,32},{16,48},{32,0},{48,16},{1,33},{17,49},{33,1},{49,17},{2,34}... | collective-permute-start | bytes 933896 | tf_op jit(solution)/shard_map/ppermute | solution.py:27
  36.9 1.9 %collective-permute-start.9 = (bf16[1216,128]{1,0:T(8,128)(2,1)S(1)}, bf16[1216,128]{1,0:T(8,128)(2,1)S(1)}, u32[]{:S(2)}, u32[]{:S(2)}) collective-permute-start(bf16[1216,128]{1,0:T(8,128)(2,1)S(1)} %pad_maximum_fusion.1.q0), channel_id=1, source_target_pairs={{0,16},{16,32},{32,48},{48,0},{1,17},{17,33},{33,49},{49,1},{2,18}... | collective-permute-start | bytes 933896 | tf_op jit(solution)/shard_map/ppermute | solution.py:27
  38.9 4.1 %collective-permute-start.4 = (bf16[576,128]{1,0:T(8,128)(2,1)S(1)}, bf16[576,128]{1,0:T(8,128)(2,1)S(1)}, u32[]{:S(2)}, u32[]{:S(2)}) collective-permute-start(bf16[576,128]{1,0:T(8,128)(2,1)S(1)} %copy-done.27), channel_id=1, source_target_pairs={{0,8},{4,12},{8,0},{12,4},{1,9},{5,13},{9,1},{13,5},{2,10},{6,14},... | collective-permute-start | bytes 442376 | tf_op jit(solution)/shard_map/ppermute | solution.py:27
  43.9 3.1 %collective-permute-start.5 = (bf16[576,128]{1,0:T(8,128)(2,1)S(1)}, bf16[576,128]{1,0:T(8,128)(2,1)S(1)}, u32[]{:S(2)}, u32[]{:S(2)}) collective-permute-start(bf16[576,128]{1,0:T(8,128)(2,1)S(1)} %copy-done.26), channel_id=1, source_target_pairs={{0,12},{4,0},{8,4},{12,8},{1,13},{5,1},{9,5},{13,9},{2,14},{6,2},{... | collective-permute-start | bytes 442376 | tf_op jit(solution)/shard_map/ppermute | solution.py:27
  48.8 3.2 %shard_map.156 = (bf16[768,128]{1,0:T(8,128)(2,1)}, bf16[4,4,128,256]{3,2,1,0:T(8,128)(2,1)}) custom-call(s32[7]{0:T(128)} %stack.31.sc, s32[2]{0:T(128)} %off.19, s32[2]{0:T(128)} %wid.19, bf16[1216,128]{1,0:T(8,128)(2,1)} %copy-done.2, bf16[1216,128]{1,0:T(8,128)(2,1)} %copy-done.14, bf16[1216,128]{1,0:T(8,128)(2,1)} %copy-done.13, ...), custom_call_target="tpu_custom_call" | custom-call | flops 1000000000 | bytes 3000000 | tf_op jit(solution)/shard_map/pallas_call | solution.py:482
  52.1 4.6 %collective-permute-done.5.x3.f3 = bf16[576,128]{1,0:T(8,128)(2,1)S(1)} collective-permute-done((bf16[576,128]{1,0:T(8,128)(2,1)S(1)}, bf16[576,128]{1,0:T(8,128)(2,1)S(1)}, u32[]{:S(2)}, u32[]{:S(2)}) %collective-permute-start.5) | collective-permute-done | bytes 147488 | tf_op jit(solution)/shard_map/ppermute | solution.py:27
  57.4 6.1 %shard_map.157 = (bf16[4,8,192,128]{3,2,1,0:T(8,128)(2,1)}, f32[4,4,16,128]{3,2,1,0:T(8,128)}) custom-call(s32[7]{0:T(128)} %stack.31.sc, s32[2]{0:T(128)} %off.19, s32[2]{0:T(128)} %wid.19, bf16[576,128]{1,0:T(8,128)(2,1)} %get-tuple-element.88.x0.f0, bf16[576,128]{1,0:T(8,128)(2,1)} %copy-done.23, bf16[576,128]{1,0:T(8,128)(2,1)} %copy-done.24, ...), custom_call_target="tpu_custom_call" | custom-call | flops 6000000000 | bytes 18000000 | tf_op jit(solution)/shard_map/pallas_call | solution.py:482
  63.5 4.3 %shard_map.158 = (f32[2,2,192,256]{3,2,1,0:T(8,128)}, bf16[1664,128]{1,0:T(8,128)(2,1)}) custom-call(s32[7]{0:T(128)} %stack.31.sc, s32[2]{0:T(128)} %off.19, s32[2]{0:T(128)} %wid.19, bf16[4,8,192,128]{3,2,1,0:T(8,128)(2,1)} %get-tuple-element.94.depth, bf16[4,4,128,256]{3,2,1,0:T(8,128)(2,1)} %get-tuple-element.92.wfull, ...), custom_call_target="tpu_custom_call" | custom-call | flops 4000000000 | bytes 12000000 | tf_op jit(solution)/shard_map/pallas_call | solution.py:482
  68.0 1.9 %collective-permute-done.12.rcore = bf16[1664,128]{1,0:T(8,128)(2,1)S(1)} collective-permute-done((bf16[1664,128]{1,0:T(8,128)(2,1)}, bf16[1664,128]{1,0:T(8,128)(2,1)S(1)}, u32[]{:S(2)}, u32[]{:S(2)}) %collective-permute-start.12) | collective-permute-done | bytes 426016 | tf_op jit(solution)/shard_map/ppermute | solution.py:27
  70.6 2.2 %shard_map.159 = bf16[896,128]{1,0:T(8,128)(2,1)} custom-call(f32[2,2,192,256]{3,2,1,0:T(8,128)} %get-tuple-element.95.keep, bf16[1664,128]{1,0:T(8,128)(2,1)} %copy-done.7, bf16[576,128]{1,0:T(8,128)(2,1)} %get-tuple-element.88.x0.f0, bf16[576,128]{1,0:T(8,128)(2,1)} %copy-done.23, bf16[576,128]{1,0:T(8,128)(2,1)} %copy-done.24, bf16[576,128]{1,0:T(8,128)(2,1)} %copy-done.25), custom_call_target="tpu_custom_call" | custom-call | flops 1000000000 | bytes 3000000 | tf_op jit(solution)/shard_map/pallas_call | solution.py:482
  72.9 2.3 %collective-permute-done.14.ownz = bf16[768,128]{1,0:T(8,128)(2,1)S(1)} collective-permute-done((bf16[768,128]{1,0:T(8,128)(2,1)S(1)}, bf16[768,128]{1,0:T(8,128)(2,1)S(1)}, u32[]{:S(2)}, u32[]{:S(2)}) %collective-permute-start.14) | collective-permute-done | bytes 196640 | tf_op jit(solution)/shard_map/ppermute | solution.py:27
  75.2 1.4 collective-permute-done.16.ownzc
  76.6 4.0 %collective-permute-done.13.rzl = bf16[896,128]{1,0:T(8,128)(2,1)S(1)} collective-permute-done((bf16[896,128]{1,0:T(8,128)(2,1)}, bf16[896,128]{1,0:T(8,128)(2,1)S(1)}, u32[]{:S(2)}, u32[]{:S(2)}) %collective-permute-start.13) | collective-permute-done | bytes 229408 | tf_op jit(solution)/shard_map/ppermute | solution.py:27
  81.3 5.1 %shard_map.160 = (bf16[896,128]{1,0:T(8,128)(2,1)}, bf16[128,128]{1,0:T(8,128)(2,1)}, f32[2,4,4,16,384]{4,3,2,1,0:T(8,128)}, bf16[2,4,4,16,384]{4,3,2,1,0:T(8,128)(2,1)}) custom-call(s32[7]{0:T(128)} %stack.31.sc, s32[2]{0:T(128)} %off.19, s32[2]{0:T(128)} %wid.19, f32[2,2,192,256]{3,2,1,0:T(8,128)} %get-tuple-element.95.keep, bf16[1664,128]{1,0:T(8,128)(2,1)} %copy-done.7, ...), custom_call_target="tpu_custom_call" | custom-call | flops 5000000000 | bytes 15000000 | tf_op jit(solution)/shard_map/pallas_call | solution.py:482
  86.7 1.0 slice.35
  88.4 5.0 %collective-permute-done.18.zin = bf16[896,128]{1,0:T(8,128)(2,1)S(1)} collective-permute-done((bf16[896,128]{1,0:T(8,128)(2,1)}, bf16[896,128]{1,0:T(8,128)(2,1)S(1)}, u32[]{:S(2)}, u32[]{:S(2)}) %collective-permute-start.18) | collective-permute-done | bytes 229408 | tf_op jit(solution)/shard_map/ppermute | solution.py:27
  93.7 1.6 collective-permute-done.19.cin
  96.1 4.5 %shard_map.161 = (bf16[1280,128]{1,0:T(8,128)(2,1)}, bf16[1280,128]{1,0:T(8,128)(2,1)}, bf16[1280,128]{1,0:T(8,128)(2,1)}, bf16[1280,128]{1,0:T(8,128)(2,1)}, bf16[8,192,256]{2,1,0:T(8,128)(2,1)}) custom-call(s32[7]{0:T(128)} %stack.31.sc, s32[2]{0:T(128)} %off.19, s32[2]{0:T(128)} %wid.19, bf16[4,8,192,128]{3,2,1,0:T(8,128)(2,1)} %get-tuple-element.94.depth, ...), custom_call_target="tpu_custom_call" | custom-call | flops 4000000000 | bytes 12000000 | tf_op jit(solution)/shard_map/pallas_call | solution.py:482
  101.2 1.7 %collective-permute-start.27 = (bf16[1280,128]{1,0:T(8,128)(2,1)}, bf16[1280,128]{1,0:T(8,128)(2,1)S(1)}, u32[]{:S(2)}, u32[]{:S(2)}) collective-permute-start(bf16[1280,128]{1,0:T(8,128)(2,1)} %get-tuple-element.114), channel_id=1, source_target_pairs={{0,64},{64,128},{128,192},{192,0},{1,65},{65,129},{129,193},{193,1... | collective-permute-start | bytes 983048 | tf_op jit(solution)/shard_map/ppermute | solution.py:27
  102.9 2.0 %collective-permute-start.28 = (bf16[1280,128]{1,0:T(8,128)(2,1)}, bf16[1280,128]{1,0:T(8,128)(2,1)S(1)}, u32[]{:S(2)}, u32[]{:S(2)}) collective-permute-start(bf16[1280,128]{1,0:T(8,128)(2,1)} %get-tuple-element.115), channel_id=1, source_target_pairs={{0,128},{64,192},{128,0},{192,64},{1,129},{65,193},{129,1},{193,65... | collective-permute-start | bytes 983048 | tf_op jit(solution)/shard_map/ppermute | solution.py:27
  105.9 1.8 %collective-permute-done.20 = bf16[4,4,16,384]{3,2,1,0:T(8,128)(2,1)S(1)} collective-permute-done((bf16[4,4,16,384]{3,2,1,0:T(8,128)(2,1)S(1)}, bf16[4,4,16,384]{3,2,1,0:T(8,128)(2,1)S(1)}, u32[]{:S(2)}, u32[]{:S(2)}) %collective-permute-start.20) | collective-permute-done | bytes 196640 | tf_op jit(solution)/shard_map/ppermute | solution.py:27
  108.5 9.8 %shard_map.162 = (bf16[768,128]{1,0:T(8,128)(2,1)}, bf16[768,128]{1,0:T(8,128)(2,1)}, bf16[768,128]{1,0:T(8,128)(2,1)}, bf16[768,128]{1,0:T(8,128)(2,1)}) custom-call(s32[7]{0:T(128)} %stack.31.sc, s32[2]{0:T(128)} %off.19, s32[2]{0:T(128)} %wid.19, bf16[576,128]{1,0:T(8,128)(2,1)} %get-tuple-element.88.x0.f0, bf16[576,128]{1,0:T(8,128)(2,1)} %copy-done.23, ...), custom_call_target="tpu_custom_call" | custom-call | flops 10000000000 | bytes 30000000 | tf_op jit(solution)/shard_map/pallas_call | solution.py:482
  118.3 1.7 %collective-permute-start.21 = (bf16[768,128]{1,0:T(8,128)(2,1)}, bf16[768,128]{1,0:T(8,128)(2,1)S(1)}, u32[]{:S(2)}, u32[]{:S(2)}) collective-permute-start(bf16[768,128]{1,0:T(8,128)(2,1)} %get-tuple-element.106), channel_id=1, source_target_pairs={{0,64},{64,128},{128,192},{192,0},{1,65},{65,129},{129,193},{193,1... | collective-permute-start | bytes 589832 | tf_op jit(solution)/shard_map/ppermute | solution.py:27
  120.0 2.0 %collective-permute-start.22 = (bf16[768,128]{1,0:T(8,128)(2,1)}, bf16[768,128]{1,0:T(8,128)(2,1)S(1)}, u32[]{:S(2)}, u32[]{:S(2)}) collective-permute-start(bf16[768,128]{1,0:T(8,128)(2,1)} %get-tuple-element.107), channel_id=1, source_target_pairs={{0,128},{64,192},{128,0},{192,64},{1,129},{65,193},{129,1},{193,65... | collective-permute-start | bytes 589832 | tf_op jit(solution)/shard_map/ppermute | solution.py:27
  123.9 2.1 %shard_map.164 = (f32[256,128]{1,0:T(8,128)}, bf16[512,128]{1,0:T(8,128)(2,1)}, bf16[512,128]{1,0:T(8,128)(2,1)}, bf16[512,128]{1,0:T(8,128)(2,1)}, bf16[512,128]{1,0:T(8,128)(2,1)}) custom-call(bf16[1280,128]{1,0:T(8,128)(2,1)} %get-tuple-element.113.g0, bf16[1280,128]{1,0:T(8,128)(2,1)} %copy-done.9, bf16[1280,128]{1,0:T(8,128)(2,1)} %copy-done.10, ...), custom_call_target="tpu_custom_call" | custom-call | flops 1000000000 | bytes 3000000 | tf_op jit(solution)/shard_map/pallas_call | solution.py:482
  126.0 3.7 %collective-permute-start.30 = (bf16[512,128]{1,0:T(8,128)(2,1)}, bf16[512,128]{1,0:T(8,128)(2,1)S(1)}, u32[]{:S(2)}, u32[]{:S(2)}) collective-permute-start(bf16[512,128]{1,0:T(8,128)(2,1)} %get-tuple-element.118), channel_id=1, source_target_pairs={{0,12},{4,0},{8,4},{12,8},{1,13},{5,1},{9,5},{13,9},{2,14},{6,2},{... | collective-permute-start | bytes 393224 | tf_op jit(solution)/shard_map/ppermute | solution.py:27
  129.7 1.7 %collective-permute-start.31 = (bf16[512,128]{1,0:T(8,128)(2,1)}, bf16[512,128]{1,0:T(8,128)(2,1)S(1)}, u32[]{:S(2)}, u32[]{:S(2)}) collective-permute-start(bf16[512,128]{1,0:T(8,128)(2,1)} %get-tuple-element.119), channel_id=1, source_target_pairs={{0,8},{4,12},{8,0},{12,4},{1,9},{5,13},{9,1},{13,5},{2,10},{6,14},... | collective-permute-start | bytes 393224 | tf_op jit(solution)/shard_map/ppermute | solution.py:27
  131.5 1.3 collective-permute-start.32
  133.5 2.0 %shard_map.163 = (bf16[320,128]{1,0:T(8,128)(2,1)}, bf16[320,128]{1,0:T(8,128)(2,1)}, bf16[320,128]{1,0:T(8,128)(2,1)}, bf16[320,128]{1,0:T(8,128)(2,1)}) custom-call(bf16[768,128]{1,0:T(8,128)(2,1)} %get-tuple-element.105.v0, bf16[768,128]{1,0:T(8,128)(2,1)} %copy-done.17, bf16[768,128]{1,0:T(8,128)(2,1)} %copy-done.18, bf16[768,128]{1,0:T(8,128)(2,1)} %copy-done.19), custom_call_target="tpu_custom_call" | custom-call | flops 1000000000 | bytes 3000000 | tf_op jit(solution)/shard_map/pallas_call | solution.py:482
  135.5 2.8 %collective-permute-start.24 = (bf16[320,128]{1,0:T(8,128)(2,1)}, bf16[320,128]{1,0:T(8,128)(2,1)S(1)}, u32[]{:S(2)}, u32[]{:S(2)}) collective-permute-start(bf16[320,128]{1,0:T(8,128)(2,1)} %get-tuple-element.110), channel_id=1, source_target_pairs={{0,12},{4,0},{8,4},{12,8},{1,13},{5,1},{9,5},{13,9},{2,14},{6,2},{... | collective-permute-start | bytes 245768 | tf_op jit(solution)/shard_map/ppermute | solution.py:27
  138.4 4.2 %collective-permute-start.25 = (bf16[320,128]{1,0:T(8,128)(2,1)}, bf16[320,128]{1,0:T(8,128)(2,1)S(1)}, u32[]{:S(2)}, u32[]{:S(2)}) collective-permute-start(bf16[320,128]{1,0:T(8,128)(2,1)} %get-tuple-element.111), channel_id=1, source_target_pairs={{0,8},{4,12},{8,0},{12,4},{1,9},{5,13},{9,1},{13,5},{2,10},{6,14},... | collective-permute-start | bytes 245768 | tf_op jit(solution)/shard_map/ppermute | solution.py:27
  142.7 3.5 %collective-permute-done.32.h3 = bf16[512,128]{1,0:T(8,128)(2,1)S(1)} collective-permute-done((bf16[512,128]{1,0:T(8,128)(2,1)}, bf16[512,128]{1,0:T(8,128)(2,1)S(1)}, u32[]{:S(2)}, u32[]{:S(2)}) %collective-permute-start.32) | collective-permute-done | bytes 131104 | tf_op jit(solution)/shard_map/ppermute | solution.py:27
  146.2 3.8 %collective-permute-done.25.z2 = bf16[320,128]{1,0:T(8,128)(2,1)S(1)} collective-permute-done((bf16[320,128]{1,0:T(8,128)(2,1)}, bf16[320,128]{1,0:T(8,128)(2,1)S(1)}, u32[]{:S(2)}, u32[]{:S(2)}) %collective-permute-start.25) | collective-permute-done | bytes 81952 | tf_op jit(solution)/shard_map/ppermute | solution.py:27
  150.7 2.0 %shard_map.166 = (f32[320,128]{1,0:T(8,128)}, bf16[320,128]{1,0:T(8,128)(2,1)}) custom-call(bf16[320,128]{1,0:T(8,128)(2,1)} %get-tuple-element.109.z0, bf16[320,128]{1,0:T(8,128)(2,1)} %copy-done.32, bf16[320,128]{1,0:T(8,128)(2,1)} %copy-done.33, bf16[320,128]{1,0:T(8,128)(2,1)} %copy-done.34, f32[256,128]{1,0:T(8,128)} %get-tuple-element.123.gown, ...), custom_call_target="tpu_custom_call" | custom-call | flops 1000000000 | bytes 3000000 | tf_op jit(solution)/shard_map/pallas_call | solution.py:482
  152.7 1.3 collective-permute-start.35
  154.0 2.4 %collective-permute-start.34 = (bf16[320,128]{1,0:T(8,128)(2,1)}, bf16[320,128]{1,0:T(8,128)(2,1)S(1)}, u32[]{:S(2)}, u32[]{:S(2)}) collective-permute-start(bf16[320,128]{1,0:T(8,128)(2,1)} %get-tuple-element.125), channel_id=1, source_target_pairs={{0,32},{16,48},{32,0},{48,16},{1,33},{17,49},{33,1},{49,17},{2,34}... | collective-permute-start | bytes 245768 | tf_op jit(solution)/shard_map/ppermute | solution.py:27
  156.4 2.6 %collective-permute-start.33 = (bf16[320,128]{1,0:T(8,128)(2,1)}, bf16[320,128]{1,0:T(8,128)(2,1)S(1)}, u32[]{:S(2)}, u32[]{:S(2)}) collective-permute-start(bf16[320,128]{1,0:T(8,128)(2,1)} %get-tuple-element.125), channel_id=1, source_target_pairs={{0,16},{16,32},{32,48},{48,0},{1,17},{17,33},{33,49},{49,1},{2,18}... | collective-permute-start | bytes 245768 | tf_op jit(solution)/shard_map/ppermute | solution.py:27
  159.0 3.2 %shard_map.165 = (bf16[2,8,128,128]{3,2,1,0:T(8,128)(2,1)}, bf16[2,32,16,128]{3,2,1,0:T(8,128)(2,1)}) custom-call(s32[7]{0:T(128)} %stack.31.sc, s32[2]{0:T(128)} %off.19, s32[2]{0:T(128)} %wid.19, bf16[320,128]{1,0:T(8,128)(2,1)} %get-tuple-element.109.z0, bf16[320,128]{1,0:T(8,128)(2,1)} %copy-done.32, bf16[320,128]{1,0:T(8,128)(2,1)} %copy-done.33, ...), custom_call_target="tpu_custom_call" | custom-call | flops 3000000000 | bytes 9000000 | tf_op jit(solution)/shard_map/pallas_call | solution.py:482
  162.3 1.7 %copy.18 = bf16[16,2,32,128]{3,2,1,0:T(8,128)(2,1)} copy(bf16[16,2,32,128]{3,0,2,1:T(8,128)(2,1)} %bitcast.23) | data formatting | bytes 524288
  164.7 1.7 %shard_map.167 = (f32[9,1,128]{2,1,0:T(1,128)}, f32[1,128,256]{2,1,0:T(8,128)}, f32[1,16]{1,0:T(1,128)}, f32[1,16,256]{2,1,0:T(8,128)}, f32[1,16]{1,0:T(1,128)}) custom-call(f32[320,128]{1,0:T(8,128)} %get-tuple-element.124.own, bf16[320,128]{1,0:T(8,128)(2,1)} %copy-done.37, bf16[320,128]{1,0:T(8,128)(2,1)} %copy-done.36, bf16[320,128]{1,0:T(8,128)(2,1)} %copy-done.35), custom_call_target="tpu_custom_call" | custom-call | flops 1000000000 | bytes 3000000 | tf_op jit(solution)/shard_map/pallas_call | solution.py:482
  (138 shorter events, 19.7 us)
Async XLA Ops:
  0.6 7.4 %copy-start = (bf16[16,2,32,128]{3,2,1,0:T(8,128)(2,1)S(1)}, bf16[16,2,32,128]{3,2,1,0:T(8,128)(2,1)}, u32[]{:S(2)}) copy-start(bf16[16,2,32,128]{3,2,1,0:T(8,128)(2,1)} %param.19) | copy-start | bytes 786436
  3.5 9.9 %collective-permute-start.2 = (bf16[128,128]{1,0:T(8,128)(2,1)}, bf16[128,128]{1,0:T(8,128)(2,1)S(1)}, u32[]{:S(2)}, u32[]{:S(2)}) collective-permute-start(bf16[128,128]{1,0:T(8,128)(2,1)} %shard_map.153.b0), channel_id=1, source_target_pairs={{0,192},{64,0},{128,64},{192,128},{1,193},{65,1},{129,65},{193,129... | collective-permute-start | bytes 98312 | tf_op jit(solution)/shard_map/ppermute | solution.py:27
  6.3 7.2 %collective-permute-start.1 = (bf16[128,128]{1,0:T(8,128)(2,1)}, bf16[128,128]{1,0:T(8,128)(2,1)S(1)}, u32[]{:S(2)}, u32[]{:S(2)}) collective-permute-start(bf16[128,128]{1,0:T(8,128)(2,1)} %shard_map.153.b0), channel_id=1, source_target_pairs={{0,128},{64,192},{128,0},{192,64},{1,129},{65,193},{129,1},{193,65... | collective-permute-start | bytes 98312 | tf_op jit(solution)/shard_map/ppermute | solution.py:27
  7.1 6.4 %collective-permute-start = (bf16[128,128]{1,0:T(8,128)(2,1)}, bf16[128,128]{1,0:T(8,128)(2,1)S(1)}, u32[]{:S(2)}, u32[]{:S(2)}) collective-permute-start(bf16[128,128]{1,0:T(8,128)(2,1)} %shard_map.153.b0), channel_id=1, source_target_pairs={{0,64},{64,128},{128,192},{192,0},{1,65},{65,129},{129,193},{193,1... | collective-permute-start | bytes 98312 | tf_op jit(solution)/shard_map/ppermute | solution.py:27
  14.1 24.7 %copy-start.28 = (bf16[576,128]{1,0:T(8,128)(2,1)S(1)}, bf16[576,128]{1,0:T(8,128)(2,1)}, u32[]{:S(2)}) copy-start(bf16[576,128]{1,0:T(8,128)(2,1)} %get-tuple-element.82) | copy-start | bytes 442372
  14.1 24.8 %copy-start.27 = (bf16[576,128]{1,0:T(8,128)(2,1)S(1)}, bf16[576,128]{1,0:T(8,128)(2,1)}, u32[]{:S(2)}) copy-start(bf16[576,128]{1,0:T(8,128)(2,1)} %get-tuple-element.83) | copy-start | bytes 442372
  14.1 29.8 %copy-start.26 = (bf16[576,128]{1,0:T(8,128)(2,1)S(1)}, bf16[576,128]{1,0:T(8,128)(2,1)}, u32[]{:S(2)}) copy-start(bf16[576,128]{1,0:T(8,128)(2,1)} %get-tuple-element.84) | copy-start | bytes 442372
  16.4 13.8 %collective-permute-start.8 = (bf16[368,128]{1,0:T(8,128)(2,1)}, bf16[368,128]{1,0:T(8,128)(2,1)S(1)}, u32[]{:S(2)}, u32[]{:S(2)}) collective-permute-start(bf16[368,128]{1,0:T(8,128)(2,1)} %shard_map.155.a0), channel_id=1, source_target_pairs={{0,12},{4,0},{8,4},{12,8},{1,13},{5,1},{9,5},{13,9},{2,14},{6,2},{... | collective-permute-start | bytes 282632 | tf_op jit(solution)/shard_map/ppermute | solution.py:27
  22.7 11.0 %collective-permute-start.7 = (bf16[368,128]{1,0:T(8,128)(2,1)}, bf16[368,128]{1,0:T(8,128)(2,1)S(1)}, u32[]{:S(2)}, u32[]{:S(2)}) collective-permute-start(bf16[368,128]{1,0:T(8,128)(2,1)} %shard_map.155.a0), channel_id=1, source_target_pairs={{0,8},{4,12},{8,0},{12,4},{1,9},{5,13},{9,1},{13,5},{2,10},{6,14},... | collective-permute-start | bytes 282632 | tf_op jit(solution)/shard_map/ppermute | solution.py:27
  23.6 10.2 %collective-permute-start.6 = (bf16[368,128]{1,0:T(8,128)(2,1)}, bf16[368,128]{1,0:T(8,128)(2,1)S(1)}, u32[]{:S(2)}, u32[]{:S(2)}) collective-permute-start(bf16[368,128]{1,0:T(8,128)(2,1)} %shard_map.155.a0), channel_id=1, source_target_pairs={{0,4},{4,8},{8,12},{12,0},{1,5},{5,9},{9,13},{13,1},{2,6},{6,10},{... | collective-permute-start | bytes 282632 | tf_op jit(solution)/shard_map/ppermute | solution.py:27
  30.2 21.8 %copy-start.4 = (bf16[368,128]{1,0:T(8,128)(2,1)}, bf16[368,128]{1,0:T(8,128)(2,1)S(1)}, u32[]{:S(2)}) copy-start(bf16[368,128]{1,0:T(8,128)(2,1)S(1)} %collective-permute-done.8.a3) | copy-start | bytes 282628
  33.7 18.3 %copy-start.5 = (bf16[368,128]{1,0:T(8,128)(2,1)}, bf16[368,128]{1,0:T(8,128)(2,1)S(1)}, u32[]{:S(2)}) copy-start(bf16[368,128]{1,0:T(8,128)(2,1)S(1)} %collective-permute-done.7.a2) | copy-start | bytes 282628
  33.7 18.3 %copy-start.6 = (bf16[368,128]{1,0:T(8,128)(2,1)}, bf16[368,128]{1,0:T(8,128)(2,1)S(1)}, u32[]{:S(2)}) copy-start(bf16[368,128]{1,0:T(8,128)(2,1)S(1)} %collective-permute-done.6.a1) | copy-start | bytes 282628
  33.8 14.3 %copy-start.2 = (bf16[1216,128]{1,0:T(8,128)(2,1)}, bf16[1216,128]{1,0:T(8,128)(2,1)S(1)}, u32[]{:S(2)}) copy-start(bf16[1216,128]{1,0:T(8,128)(2,1)S(1)} %pad_maximum_fusion.1.q0) | copy-start | bytes 933892
  33.8 10.1 %collective-permute-start.11 = (bf16[1216,128]{1,0:T(8,128)(2,1)S(1)}, bf16[1216,128]{1,0:T(8,128)(2,1)S(1)}, u32[]{:S(2)}, u32[]{:S(2)}) collective-permute-start(bf16[1216,128]{1,0:T(8,128)(2,1)S(1)} %pad_maximum_fusion.1.q0), channel_id=1, source_target_pairs={{0,48},{16,0},{32,16},{48,32},{1,49},{17,1},{33,17},{49,33},{2,50}... | collective-permute-start | bytes 933896 | tf_op jit(solution)/shard_map/ppermute | solution.py:27
  34.3 12.9 %collective-permute-start.10 = (bf16[1216,128]{1,0:T(8,128)(2,1)S(1)}, bf16[1216,128]{1,0:T(8,128)(2,1)S(1)}, u32[]{:S(2)}, u32[]{:S(2)}) collective-permute-start(bf16[1216,128]{1,0:T(8,128)(2,1)S(1)} %pad_maximum_fusion.1.q0), channel_id=1, source_target_pairs={{0,32},{16,48},{32,0},{48,16},{1,33},{17,49},{33,1},{49,17},{2,34}... | collective-permute-start | bytes 933896 | tf_op jit(solution)/shard_map/ppermute | solution.py:27
  36.9 11.2 %collective-permute-start.9 = (bf16[1216,128]{1,0:T(8,128)(2,1)S(1)}, bf16[1216,128]{1,0:T(8,128)(2,1)S(1)}, u32[]{:S(2)}, u32[]{:S(2)}) collective-permute-start(bf16[1216,128]{1,0:T(8,128)(2,1)S(1)} %pad_maximum_fusion.1.q0), channel_id=1, source_target_pairs={{0,16},{16,32},{32,48},{48,0},{1,17},{17,33},{33,49},{49,1},{2,18}... | collective-permute-start | bytes 933896 | tf_op jit(solution)/shard_map/ppermute | solution.py:27
  38.8 13.3 %collective-permute-start.3 = (bf16[576,128]{1,0:T(8,128)(2,1)S(1)}, bf16[576,128]{1,0:T(8,128)(2,1)S(1)}, u32[]{:S(2)}, u32[]{:S(2)}) collective-permute-start(bf16[576,128]{1,0:T(8,128)(2,1)S(1)} %copy-done.28), channel_id=1, source_target_pairs={{0,4},{4,8},{8,12},{12,0},{1,5},{5,9},{9,13},{13,1},{2,6},{6,10},{... | collective-permute-start | bytes 442376 | tf_op jit(solution)/shard_map/ppermute | solution.py:27
  38.9 13.2 %collective-permute-start.4 = (bf16[576,128]{1,0:T(8,128)(2,1)S(1)}, bf16[576,128]{1,0:T(8,128)(2,1)S(1)}, u32[]{:S(2)}, u32[]{:S(2)}) collective-permute-start(bf16[576,128]{1,0:T(8,128)(2,1)S(1)} %copy-done.27), channel_id=1, source_target_pairs={{0,8},{4,12},{8,0},{12,4},{1,9},{5,13},{9,1},{13,5},{2,10},{6,14},... | collective-permute-start | bytes 442376 | tf_op jit(solution)/shard_map/ppermute | solution.py:27
  43.9 12.8 %collective-permute-start.5 = (bf16[576,128]{1,0:T(8,128)(2,1)S(1)}, bf16[576,128]{1,0:T(8,128)(2,1)S(1)}, u32[]{:S(2)}, u32[]{:S(2)}) collective-permute-start(bf16[576,128]{1,0:T(8,128)(2,1)S(1)} %copy-done.26), channel_id=1, source_target_pairs={{0,12},{4,0},{8,4},{12,8},{1,13},{5,1},{9,5},{13,9},{2,14},{6,2},{... | collective-permute-start | bytes 442376 | tf_op jit(solution)/shard_map/ppermute | solution.py:27
  67.8 2.0 %collective-permute-start.12 = (bf16[1664,128]{1,0:T(8,128)(2,1)}, bf16[1664,128]{1,0:T(8,128)(2,1)S(1)}, u32[]{:S(2)}, u32[]{:S(2)}) collective-permute-start(bf16[1664,128]{1,0:T(8,128)(2,1)} %get-tuple-element.96), channel_id=1, source_target_pairs={{0,1},{1,0},{2,3},{3,2},{4,5},{5,4},{6,7},{7,6},{8,9},{9,8},{10,11... | collective-permute-start | bytes 1277960 | tf_op jit(solution)/shard_map/ppermute | solution.py:27
  67.9 7.3 %collective-permute-start.14 = (bf16[768,128]{1,0:T(8,128)(2,1)S(1)}, bf16[768,128]{1,0:T(8,128)(2,1)S(1)}, u32[]{:S(2)}, u32[]{:S(2)}) collective-permute-start(bf16[768,128]{1,0:T(8,128)(2,1)S(1)} %copy-done.16), channel_id=1, source_target_pairs={{0,2},{2,0},{1,3},{3,1},{4,6},{6,4},{5,7},{7,5},{8,10},{10,8},{9,1... | collective-permute-start | bytes 589832 | tf_op jit(solution)/shard_map/ppermute | solution.py:27
  72.7 7.9 %collective-permute-start.13 = (bf16[896,128]{1,0:T(8,128)(2,1)}, bf16[896,128]{1,0:T(8,128)(2,1)S(1)}, u32[]{:S(2)}, u32[]{:S(2)}) collective-permute-start(bf16[896,128]{1,0:T(8,128)(2,1)} %shard_map.159), channel_id=1, source_target_pairs={{0,2},{2,0},{1,3},{3,1},{4,6},{6,4},{5,7},{7,5},{8,10},{10,8},{9,1... | collective-permute-start | bytes 688136 | tf_op jit(solution)/shard_map/ppermute | solution.py:27
  72.9 2.3 %collective-permute-start.15 = (bf16[768,128]{1,0:T(8,128)(2,1)S(1)}, bf16[768,128]{1,0:T(8,128)(2,1)S(1)}, u32[]{:S(2)}, u32[]{:S(2)}) collective-permute-start(bf16[768,128]{1,0:T(8,128)(2,1)S(1)} %copy-done.16), channel_id=1, source_target_pairs={{0,1},{1,0},{2,3},{3,2},{4,5},{5,4},{6,7},{7,6},{8,9},{9,8},{10,11... | collective-permute-start | bytes 589832 | tf_op jit(solution)/shard_map/ppermute | solution.py:27
  75.2 5.4 %copy-start.20 = (bf16[768,128]{1,0:T(8,128)(2,1)}, bf16[768,128]{1,0:T(8,128)(2,1)S(1)}, u32[]{:S(2)}) copy-start(bf16[768,128]{1,0:T(8,128)(2,1)S(1)} %collective-permute-done.14.ownz) | copy-start | bytes 589828
  75.2 1.4 collective-permute-start.16
  86.4 7.2 %copy-start.1 = (f32[2,4,4,16,384]{4,3,2,1,0:T(8,128)S(1)}, f32[2,4,4,16,384]{4,3,2,1,0:T(8,128)}, u32[]{:S(2)}) copy-start(f32[2,4,4,16,384]{4,3,2,1,0:T(8,128)} %get-tuple-element.98) | copy-start | bytes 2359300
  86.4 7.0 %collective-permute-start.18 = (bf16[896,128]{1,0:T(8,128)(2,1)}, bf16[896,128]{1,0:T(8,128)(2,1)S(1)}, u32[]{:S(2)}, u32[]{:S(2)}) collective-permute-start(bf16[896,128]{1,0:T(8,128)(2,1)} %get-tuple-element.100.zout), channel_id=1, source_target_pairs={{0,2},{2,0},{1,3},{3,1},{4,6},{6,4},{5,7},{7,5},{8,10},{10,8},{9,1... | collective-permute-start | bytes 688136 | tf_op jit(solution)/shard_map/ppermute | solution.py:27
  86.7 6.9 %collective-permute-start.17 = (bf16[2,4,4,16,384]{4,3,2,1,0:T(8,128)(2,1)}, bf16[2,4,4,16,384]{4,3,2,1,0:T(8,128)(2,1)S(1)}, u32[]{:S(2)}, u32[]{:S(2)}) collective-permute-start(bf16[2,4,4,16,384]{4,3,2,1,0:T(8,128)(2,1)} %get-tuple-element.99), channel_id=1, source_target_pairs={{0,1},{1,0},{2,3},{3,2},{4,5},{5,4},{6,7},{7,6},{8,9},{9,8},{10,11... | collective-permute-start | bytes 1179656 | tf_op jit(solution)/shard_map/ppermute | solution.py:27
  93.5 1.9 %collective-permute-start.19 = (bf16[1664,128]{1,0:T(8,128)(2,1)S(1)}, bf16[1664,128]{1,0:T(8,128)(2,1)S(1)}, u32[]{:S(2)}, u32[]{:S(2)}) collective-permute-start(bf16[1664,128]{1,0:T(8,128)(2,1)S(1)} %pad_maximum_fusion), channel_id=1, source_target_pairs={{0,1},{1,0},{2,3},{3,2},{4,5},{5,4},{6,7},{7,6},{8,9},{9,8},{10,11... | collective-permute-start | bytes 1277960 | tf_op jit(solution)/shard_map/ppermute | solution.py:27
  100.7 7.0 %collective-permute-start.20 = (bf16[4,4,16,384]{3,2,1,0:T(8,128)(2,1)S(1)}, bf16[4,4,16,384]{3,2,1,0:T(8,128)(2,1)S(1)}, u32[]{:S(2)}, u32[]{:S(2)}) collective-permute-start(bf16[4,4,16,384]{3,2,1,0:T(8,128)(2,1)S(1)} %fusion), channel_id=1, source_target_pairs={{0,2},{2,0},{1,3},{3,1},{4,6},{6,4},{5,7},{7,5},{8,10},{10,8},{9,1... | collective-permute-start | bytes 589832 | tf_op jit(solution)/shard_map/ppermute | solution.py:27
  101.2 20.9 %collective-permute-start.27 = (bf16[1280,128]{1,0:T(8,128)(2,1)}, bf16[1280,128]{1,0:T(8,128)(2,1)S(1)}, u32[]{:S(2)}, u32[]{:S(2)}) collective-permute-start(bf16[1280,128]{1,0:T(8,128)(2,1)} %get-tuple-element.114), channel_id=1, source_target_pairs={{0,64},{64,128},{128,192},{192,0},{1,65},{65,129},{129,193},{193,1... | collective-permute-start | bytes 983048 | tf_op jit(solution)/shard_map/ppermute | solution.py:27
  102.9 20.1 %collective-permute-start.28 = (bf16[1280,128]{1,0:T(8,128)(2,1)}, bf16[1280,128]{1,0:T(8,128)(2,1)S(1)}, u32[]{:S(2)}, u32[]{:S(2)}) collective-permute-start(bf16[1280,128]{1,0:T(8,128)(2,1)} %get-tuple-element.115), channel_id=1, source_target_pairs={{0,128},{64,192},{128,0},{192,64},{1,129},{65,193},{129,1},{193,65... | collective-permute-start | bytes 983048 | tf_op jit(solution)/shard_map/ppermute | solution.py:27
  104.9 18.1 %collective-permute-start.29 = (bf16[1280,128]{1,0:T(8,128)(2,1)}, bf16[1280,128]{1,0:T(8,128)(2,1)S(1)}, u32[]{:S(2)}, u32[]{:S(2)}) collective-permute-start(bf16[1280,128]{1,0:T(8,128)(2,1)} %get-tuple-element.116), channel_id=1, source_target_pairs={{0,192},{64,0},{128,64},{192,128},{1,193},{65,1},{129,65},{193,129... | collective-permute-start | bytes 983048 | tf_op jit(solution)/shard_map/ppermute | solution.py:27
  118.3 13.2 %collective-permute-start.21 = (bf16[768,128]{1,0:T(8,128)(2,1)}, bf16[768,128]{1,0:T(8,128)(2,1)S(1)}, u32[]{:S(2)}, u32[]{:S(2)}) collective-permute-start(bf16[768,128]{1,0:T(8,128)(2,1)} %get-tuple-element.106), channel_id=1, source_target_pairs={{0,64},{64,128},{128,192},{192,0},{1,65},{65,129},{129,193},{193,1... | collective-permute-start | bytes 589832 | tf_op jit(solution)/shard_map/ppermute | solution.py:27
  120.0 12.7 %collective-permute-start.22 = (bf16[768,128]{1,0:T(8,128)(2,1)}, bf16[768,128]{1,0:T(8,128)(2,1)S(1)}, u32[]{:S(2)}, u32[]{:S(2)}) collective-permute-start(bf16[768,128]{1,0:T(8,128)(2,1)} %get-tuple-element.107), channel_id=1, source_target_pairs={{0,128},{64,192},{128,0},{192,64},{1,129},{65,193},{129,1},{193,65... | collective-permute-start | bytes 589832 | tf_op jit(solution)/shard_map/ppermute | solution.py:27
  122.1 10.7 %collective-permute-start.23 = (bf16[768,128]{1,0:T(8,128)(2,1)}, bf16[768,128]{1,0:T(8,128)(2,1)S(1)}, u32[]{:S(2)}, u32[]{:S(2)}) collective-permute-start(bf16[768,128]{1,0:T(8,128)(2,1)} %get-tuple-element.108), channel_id=1, source_target_pairs={{0,192},{64,0},{128,64},{192,128},{1,193},{65,1},{129,65},{193,129... | collective-permute-start | bytes 589832 | tf_op jit(solution)/shard_map/ppermute | solution.py:27
  126.0 16.5 %collective-permute-start.30 = (bf16[512,128]{1,0:T(8,128)(2,1)}, bf16[512,128]{1,0:T(8,128)(2,1)S(1)}, u32[]{:S(2)}, u32[]{:S(2)}) collective-permute-start(bf16[512,128]{1,0:T(8,128)(2,1)} %get-tuple-element.118), channel_id=1, source_target_pairs={{0,12},{4,0},{8,4},{12,8},{1,13},{5,1},{9,5},{13,9},{2,14},{6,2},{... | collective-permute-start | bytes 393224 | tf_op jit(solution)/shard_map/ppermute | solution.py:27
  129.7 13.0 %collective-permute-start.31 = (bf16[512,128]{1,0:T(8,128)(2,1)}, bf16[512,128]{1,0:T(8,128)(2,1)S(1)}, u32[]{:S(2)}, u32[]{:S(2)}) collective-permute-start(bf16[512,128]{1,0:T(8,128)(2,1)} %get-tuple-element.119), channel_id=1, source_target_pairs={{0,8},{4,12},{8,0},{12,4},{1,9},{5,13},{9,1},{13,5},{2,10},{6,14},... | collective-permute-start | bytes 393224 | tf_op jit(solution)/shard_map/ppermute | solution.py:27
  131.5 14.8 %collective-permute-start.32 = (bf16[512,128]{1,0:T(8,128)(2,1)}, bf16[512,128]{1,0:T(8,128)(2,1)S(1)}, u32[]{:S(2)}, u32[]{:S(2)}) collective-permute-start(bf16[512,128]{1,0:T(8,128)(2,1)} %get-tuple-element.120), channel_id=1, source_target_pairs={{0,4},{4,8},{8,12},{12,0},{1,5},{5,9},{9,13},{13,1},{2,6},{6,10},{... | collective-permute-start | bytes 393224 | tf_op jit(solution)/shard_map/ppermute | solution.py:27
  135.5 10.7 %collective-permute-start.24 = (bf16[320,128]{1,0:T(8,128)(2,1)}, bf16[320,128]{1,0:T(8,128)(2,1)S(1)}, u32[]{:S(2)}, u32[]{:S(2)}) collective-permute-start(bf16[320,128]{1,0:T(8,128)(2,1)} %get-tuple-element.110), channel_id=1, source_target_pairs={{0,12},{4,0},{8,4},{12,8},{1,13},{5,1},{9,5},{13,9},{2,14},{6,2},{... | collective-permute-start | bytes 245768 | tf_op jit(solution)/shard_map/ppermute | solution.py:27
  138.4 11.7 %collective-permute-start.25 = (bf16[320,128]{1,0:T(8,128)(2,1)}, bf16[320,128]{1,0:T(8,128)(2,1)S(1)}, u32[]{:S(2)}, u32[]{:S(2)}) collective-permute-start(bf16[320,128]{1,0:T(8,128)(2,1)} %get-tuple-element.111), channel_id=1, source_target_pairs={{0,8},{4,12},{8,0},{12,4},{1,9},{5,13},{9,1},{13,5},{2,10},{6,14},... | collective-permute-start | bytes 245768 | tf_op jit(solution)/shard_map/ppermute | solution.py:27
  142.6 7.5 %copy-start.29 = (bf16[512,128]{1,0:T(8,128)(2,1)}, bf16[512,128]{1,0:T(8,128)(2,1)S(1)}, u32[]{:S(2)}) copy-start(bf16[512,128]{1,0:T(8,128)(2,1)S(1)} %collective-permute-done.30.h1) | copy-start | bytes 393220
  142.6 7.5 %collective-permute-start.26 = (bf16[320,128]{1,0:T(8,128)(2,1)}, bf16[320,128]{1,0:T(8,128)(2,1)S(1)}, u32[]{:S(2)}, u32[]{:S(2)}) collective-permute-start(bf16[320,128]{1,0:T(8,128)(2,1)} %get-tuple-element.112), channel_id=1, source_target_pairs={{0,4},{4,8},{8,12},{12,0},{1,5},{5,9},{9,13},{13,1},{2,6},{6,10},{... | collective-permute-start | bytes 245768 | tf_op jit(solution)/shard_map/ppermute | solution.py:27
  142.7 7.4 %copy-start.30 = (bf16[512,128]{1,0:T(8,128)(2,1)}, bf16[512,128]{1,0:T(8,128)(2,1)S(1)}, u32[]{:S(2)}) copy-start(bf16[512,128]{1,0:T(8,128)(2,1)S(1)} %collective-permute-done.31.h2) | copy-start | bytes 393220
  152.7 11.3 %collective-permute-start.35 = (bf16[320,128]{1,0:T(8,128)(2,1)}, bf16[320,128]{1,0:T(8,128)(2,1)S(1)}, u32[]{:S(2)}, u32[]{:S(2)}) collective-permute-start(bf16[320,128]{1,0:T(8,128)(2,1)} %get-tuple-element.125), channel_id=1, source_target_pairs={{0,48},{16,0},{32,16},{48,32},{1,49},{17,1},{33,17},{49,33},{2,50}... | collective-permute-start | bytes 245768 | tf_op jit(solution)/shard_map/ppermute | solution.py:27
  154.0 10.0 %collective-permute-start.34 = (bf16[320,128]{1,0:T(8,128)(2,1)}, bf16[320,128]{1,0:T(8,128)(2,1)S(1)}, u32[]{:S(2)}, u32[]{:S(2)}) collective-permute-start(bf16[320,128]{1,0:T(8,128)(2,1)} %get-tuple-element.125), channel_id=1, source_target_pairs={{0,32},{16,48},{32,0},{48,16},{1,33},{17,49},{33,1},{49,17},{2,34}... | collective-permute-start | bytes 245768 | tf_op jit(solution)/shard_map/ppermute | solution.py:27
  156.4 7.6 %collective-permute-start.33 = (bf16[320,128]{1,0:T(8,128)(2,1)}, bf16[320,128]{1,0:T(8,128)(2,1)S(1)}, u32[]{:S(2)}, u32[]{:S(2)}) collective-permute-start(bf16[320,128]{1,0:T(8,128)(2,1)} %get-tuple-element.125), channel_id=1, source_target_pairs={{0,16},{16,32},{32,48},{48,0},{1,17},{17,33},{33,49},{49,1},{2,18}... | collective-permute-start | bytes 245768 | tf_op jit(solution)/shard_map/ppermute | solution.py:27
  (29 other events, 51.7 us)

commit v2 on v1

--- a/solution.py
+++ b/solution.py
@@ -454,10 +454,10 @@
                     at = 64 * r + 32 * zr + 16 * cr
                     for e in range(2):
                         h = 2 * (t0 + e) + lax.rem(qs, 2)
-                        ascr[h] = jnp.concatenate(
+                        ascr[f, h] = jnp.concatenate(
                             [rs[2 * f, at:at + 16, 64 * e:64 * e + 64],
                              rs[2 * f + 1, at:at + 16, 64 * e:64 * e + 64]], axis=1)
-        asp[f] = dotf(ascr[...].reshape(512, 128), perm_matrix(off[f], True)).astype(BF).reshape(32, 16, 128)
+        asp[f] = dotf(ascr[f].reshape(512, 128), perm_matrix(off[f], True)).astype(BF).reshape(32, 16, 128)
 
 
 def final_kernel(own, d1, d2, d3, dw, pw, pwb, proj, pb, *, scaling):
@@ -562,7 +562,7 @@
     input_grad, asp = call(
         restore_kernel, sc, [*zs, *hs],
         [((2, 8, 128, 128), BF), ((2, 32, 16, 128), BF)],
-        scratch=[((4, 320, 128), BF), ((4, 256, 128), BF), ((32, 16, 128), BF)], us=3)
+        scratch=[((4, 320, 128), BF), ((4, 256, 128), BF), ((2, 32, 16, 128), BF)], us=3)
     outs = call(
         functools.partial(final_kernel, scaling=scaling), (), [own] + [shift(ownb, "dp", k) for k in range(1, 4)],
         [((9, 1, 128), F32), ((1, 128, 256), F32), ((1, 16), F32), ((1, 16, 256), F32), ((1, 16), F32)])

time: 167 us -> 167 us (level)
  no operation moved by 1% of the time
where the time goes in v2:
time: 167 us; the launch traced here: 166 us
  starting transfers between devices  57.6 us (34%)
  Pallas kernels  55.5 us (33%)
  waiting for transfers between devices  38.5 us (23%)
  local copies, waits for them, and re-layouts  12.9 us (8%)
    ppermute x36, starting transfers between devices, shift(): return lax.ppermute(x, axis, [(i, (i + k) % n) for i in range(n)])  57.6 us
    pallas_call x15, Pallas kernels, call(): pl.pallas_call(kernel, grid_spec=pltpu.PrefetchScalarGridSpec(num_scalar_...  55.5 us
    ppermute x36, waiting for transfers between devices, shift(): return lax.ppermute(x, axis, [(i, (i + k) % n) for i in range(n)])  38.5 us
    unnamed x84, local copies, waits for them, and re-layouts  9.52 us
  transfers between devices with their start and end apart: 36, of which 17 were waited for; matrix products, arithmetic and copies ran while one was open for 4% of the time, Pallas kernels for 16%

profile of v2, /device:TPU:8, one launch (start us, length us, event | category | flops | bytes accessed | tf_op | source)
XLA Modules:
  0.0 166.4 jit_solution(3173452519603264013)
XLA Ops:
  1.3 2.3 %shard_map.153.b0 = bf16[128,128]{1,0:T(8,128)(2,1)} custom-call(s32[7]{0:T(128)} %stack.31.sc, s32[2]{0:T(128)} %off.19, s32[2]{0:T(128)} %wid.19, bf16[1,128,256]{2,1,0:T(8,128)(2,1)} %pw.1, bf16[1,9,128]{2,1,0:T(8,128)(2,1)} %dw.1, bf16[1,16,256]{2,1,0:T(8,128)(2,1)} %proj.1, f32[1,16]{1,0:T(1,128)} %pwb.1, f32[1,16]{1,0:T(1,128)} %bitcast.26), custom_call_target="tpu_custom_call" | custom-call | flops 1000000000 | bytes 3000000 | tf_op jit(solution)/shard_map/pallas_call | solution.py:482
  3.5 2.8 %collective-permute-start.2 = (bf16[128,128]{1,0:T(8,128)(2,1)}, bf16[128,128]{1,0:T(8,128)(2,1)S(1)}, u32[]{:S(2)}, u32[]{:S(2)}) collective-permute-start(bf16[128,128]{1,0:T(8,128)(2,1)} %shard_map.153.b0), channel_id=1, source_target_pairs={{0,192},{64,0},{128,64},{192,128},{1,193},{65,1},{129,65},{193,129... | collective-permute-start | bytes 98312 | tf_op jit(solution)/shard_map/ppermute | solution.py:27
  8.8 4.6 %shard_map.154 = (bf16[576,128]{1,0:T(8,128)(2,1)}, bf16[576,128]{1,0:T(8,128)(2,1)}, bf16[576,128]{1,0:T(8,128)(2,1)}, bf16[576,128]{1,0:T(8,128)(2,1)}) custom-call(s32[7]{0:T(128)} %stack.31.sc, s32[2]{0:T(128)} %off.19, s32[2]{0:T(128)} %wid.19, bf16[2,16,2,128,128]{4,3,2,1,0:T(8,128)(2,1)} %bitcast.25, bf16[2,8,16,128]{3,2,1,0:T(8,128)(2,1)} %bitcast.24), custom_call_target="tpu_custom_call" | custom-call | flops 5000000000 | bytes 15000000 | tf_op jit(solution)/shard_map/pallas_call | solution.py:482
  14.1 2.3 %shard_map.155.a0 = bf16[368,128]{1,0:T(8,128)(2,1)} custom-call(s32[7]{0:T(128)} %stack.31.sc, s32[2]{0:T(128)} %off.19, s32[2]{0:T(128)} %wid.19, bf16[128,128]{1,0:T(8,128)(2,1)} %shard_map.153.b0, bf16[128,128]{1,0:T(8,128)(2,1)} %copy-done.40, bf16[128,128]{1,0:T(8,128)(2,1)} %copy-done.39, bf16[128,128]{1,0:T(8,128)(2,1)} %copy-done.38), custom_call_target="tpu_custom_call" | custom-call | flops 1000000000 | bytes 3000000 | tf_op jit(solution)/shard_map/pallas_call | solution.py:482
  16.4 6.3 %collective-permute-start.8 = (bf16[368,128]{1,0:T(8,128)(2,1)}, bf16[368,128]{1,0:T(8,128)(2,1)S(1)}, u32[]{:S(2)}, u32[]{:S(2)}) collective-permute-start(bf16[368,128]{1,0:T(8,128)(2,1)} %shard_map.155.a0), channel_id=1, source_target_pairs={{0,12},{4,0},{8,4},{12,8},{1,13},{5,1},{9,5},{13,9},{2,14},{6,2},{... | collective-permute-start | bytes 282632 | tf_op jit(solution)/shard_map/ppermute | solution.py:27
  23.6 2.9 %collective-permute-start.6 = (bf16[368,128]{1,0:T(8,128)(2,1)}, bf16[368,128]{1,0:T(8,128)(2,1)S(1)}, u32[]{:S(2)}, u32[]{:S(2)}) collective-permute-start(bf16[368,128]{1,0:T(8,128)(2,1)} %shard_map.155.a0), channel_id=1, source_target_pairs={{0,4},{4,8},{8,12},{12,0},{1,5},{5,9},{9,13},{13,1},{2,6},{6,10},{... | collective-permute-start | bytes 282632 | tf_op jit(solution)/shard_map/ppermute | solution.py:27
  27.4 2.8 %collective-permute-done.8.a3 = bf16[368,128]{1,0:T(8,128)(2,1)S(1)} collective-permute-done((bf16[368,128]{1,0:T(8,128)(2,1)}, bf16[368,128]{1,0:T(8,128)(2,1)S(1)}, u32[]{:S(2)}, u32[]{:S(2)}) %collective-permute-start.8) | collective-permute-done | bytes 94240 | tf_op jit(solution)/shard_map/ppermute | solution.py:27
  30.2 3.5 %collective-permute-done.7.a2 = bf16[368,128]{1,0:T(8,128)(2,1)S(1)} collective-permute-done((bf16[368,128]{1,0:T(8,128)(2,1)}, bf16[368,128]{1,0:T(8,128)(2,1)S(1)}, u32[]{:S(2)}, u32[]{:S(2)}) %collective-permute-start.7) | collective-permute-done | bytes 94240 | tf_op jit(solution)/shard_map/ppermute | solution.py:27
  34.3 2.6 %collective-permute-start.10 = (bf16[1216,128]{1,0:T(8,128)(2,1)S(1)}, bf16[1216,128]{1,0:T(8,128)(2,1)S(1)}, u32[]{:S(2)}, u32[]{:S(2)}) collective-permute-start(bf16[1216,128]{1,0:T(8,128)(2,1)S(1)} %pad_maximum_fusion.1.q0), channel_id=1, source_target_pairs={{0,32},{16,48},{32,0},{48,16},{1,33},{17,49},{33,1},{49,17},{2,34}... | collective-permute-start | bytes 933896 | tf_op jit(solution)/shard_map/ppermute | solution.py:27
  36.9 1.9 %collective-permute-start.9 = (bf16[1216,128]{1,0:T(8,128)(2,1)S(1)}, bf16[1216,128]{1,0:T(8,128)(2,1)S(1)}, u32[]{:S(2)}, u32[]{:S(2)}) collective-permute-start(bf16[1216,128]{1,0:T(8,128)(2,1)S(1)} %pad_maximum_fusion.1.q0), channel_id=1, source_target_pairs={{0,16},{16,32},{32,48},{48,0},{1,17},{17,33},{33,49},{49,1},{2,18}... | collective-permute-start | bytes 933896 | tf_op jit(solution)/shard_map/ppermute | solution.py:27
  38.9 4.1 %collective-permute-start.4 = (bf16[576,128]{1,0:T(8,128)(2,1)S(1)}, bf16[576,128]{1,0:T(8,128)(2,1)S(1)}, u32[]{:S(2)}, u32[]{:S(2)}) collective-permute-start(bf16[576,128]{1,0:T(8,128)(2,1)S(1)} %copy-done.27), channel_id=1, source_target_pairs={{0,8},{4,12},{8,0},{12,4},{1,9},{5,13},{9,1},{13,5},{2,10},{6,14},... | collective-permute-start | bytes 442376 | tf_op jit(solution)/shard_map/ppermute | solution.py:27
  43.9 3.1 %collective-permute-start.5 = (bf16[576,128]{1,0:T(8,128)(2,1)S(1)}, bf16[576,128]{1,0:T(8,128)(2,1)S(1)}, u32[]{:S(2)}, u32[]{:S(2)}) collective-permute-start(bf16[576,128]{1,0:T(8,128)(2,1)S(1)} %copy-done.26), channel_id=1, source_target_pairs={{0,12},{4,0},{8,4},{12,8},{1,13},{5,1},{9,5},{13,9},{2,14},{6,2},{... | collective-permute-start | bytes 442376 | tf_op jit(solution)/shard_map/ppermute | solution.py:27
  48.8 3.2 %shard_map.156 = (bf16[768,128]{1,0:T(8,128)(2,1)}, bf16[4,4,128,256]{3,2,1,0:T(8,128)(2,1)}) custom-call(s32[7]{0:T(128)} %stack.31.sc, s32[2]{0:T(128)} %off.19, s32[2]{0:T(128)} %wid.19, bf16[1216,128]{1,0:T(8,128)(2,1)} %copy-done.2, bf16[1216,128]{1,0:T(8,128)(2,1)} %copy-done.14, bf16[1216,128]{1,0:T(8,128)(2,1)} %copy-done.13, ...), custom_call_target="tpu_custom_call" | custom-call | flops 1000000000 | bytes 3000000 | tf_op jit(solution)/shard_map/pallas_call | solution.py:482
  52.1 4.6 %collective-permute-done.5.x3.f3 = bf16[576,128]{1,0:T(8,128)(2,1)S(1)} collective-permute-done((bf16[576,128]{1,0:T(8,128)(2,1)S(1)}, bf16[576,128]{1,0:T(8,128)(2,1)S(1)}, u32[]{:S(2)}, u32[]{:S(2)}) %collective-permute-start.5) | collective-permute-done | bytes 147488 | tf_op jit(solution)/shard_map/ppermute | solution.py:27
  57.4 6.1 %shard_map.157 = (bf16[4,8,192,128]{3,2,1,0:T(8,128)(2,1)}, f32[4,4,16,128]{3,2,1,0:T(8,128)}) custom-call(s32[7]{0:T(128)} %stack.31.sc, s32[2]{0:T(128)} %off.19, s32[2]{0:T(128)} %wid.19, bf16[576,128]{1,0:T(8,128)(2,1)} %get-tuple-element.88.x0.f0, bf16[576,128]{1,0:T(8,128)(2,1)} %copy-done.23, bf16[576,128]{1,0:T(8,128)(2,1)} %copy-done.24, ...), custom_call_target="tpu_custom_call" | custom-call | flops 6000000000 | bytes 18000000 | tf_op jit(solution)/shard_map/pallas_call | solution.py:482
  63.5 4.3 %shard_map.158 = (f32[2,2,192,256]{3,2,1,0:T(8,128)}, bf16[1664,128]{1,0:T(8,128)(2,1)}) custom-call(s32[7]{0:T(128)} %stack.31.sc, s32[2]{0:T(128)} %off.19, s32[2]{0:T(128)} %wid.19, bf16[4,8,192,128]{3,2,1,0:T(8,128)(2,1)} %get-tuple-element.94.depth, bf16[4,4,128,256]{3,2,1,0:T(8,128)(2,1)} %get-tuple-element.92.wfull, ...), custom_call_target="tpu_custom_call" | custom-call | flops 4000000000 | bytes 12000000 | tf_op jit(solution)/shard_map/pallas_call | solution.py:482
  68.0 1.9 %collective-permute-done.12.rcore = bf16[1664,128]{1,0:T(8,128)(2,1)S(1)} collective-permute-done((bf16[1664,128]{1,0:T(8,128)(2,1)}, bf16[1664,128]{1,0:T(8,128)(2,1)S(1)}, u32[]{:S(2)}, u32[]{:S(2)}) %collective-permute-start.12) | collective-permute-done | bytes 426016 | tf_op jit(solution)/shard_map/ppermute | solution.py:27
  70.6 2.2 %shard_map.159 = bf16[896,128]{1,0:T(8,128)(2,1)} custom-call(f32[2,2,192,256]{3,2,1,0:T(8,128)} %get-tuple-element.95.keep, bf16[1664,128]{1,0:T(8,128)(2,1)} %copy-done.7, bf16[576,128]{1,0:T(8,128)(2,1)} %get-tuple-element.88.x0.f0, bf16[576,128]{1,0:T(8,128)(2,1)} %copy-done.23, bf16[576,128]{1,0:T(8,128)(2,1)} %copy-done.24, bf16[576,128]{1,0:T(8,128)(2,1)} %copy-done.25), custom_call_target="tpu_custom_call" | custom-call | flops 1000000000 | bytes 3000000 | tf_op jit(solution)/shard_map/pallas_call | solution.py:482
  72.9 2.3 %collective-permute-done.14.ownz = bf16[768,128]{1,0:T(8,128)(2,1)S(1)} collective-permute-done((bf16[768,128]{1,0:T(8,128)(2,1)S(1)}, bf16[768,128]{1,0:T(8,128)(2,1)S(1)}, u32[]{:S(2)}, u32[]{:S(2)}) %collective-permute-start.14) | collective-permute-done | bytes 196640 | tf_op jit(solution)/shard_map/ppermute | solution.py:27
  75.2 1.4 collective-permute-done.16.ownzc
  76.6 4.0 %collective-permute-done.13.rzl = bf16[896,128]{1,0:T(8,128)(2,1)S(1)} collective-permute-done((bf16[896,128]{1,0:T(8,128)(2,1)}, bf16[896,128]{1,0:T(8,128)(2,1)S(1)}, u32[]{:S(2)}, u32[]{:S(2)}) %collective-permute-start.13) | collective-permute-done | bytes 229408 | tf_op jit(solution)/shard_map/ppermute | solution.py:27
  81.3 5.1 %shard_map.160 = (bf16[896,128]{1,0:T(8,128)(2,1)}, bf16[128,128]{1,0:T(8,128)(2,1)}, f32[2,4,4,16,384]{4,3,2,1,0:T(8,128)}, bf16[2,4,4,16,384]{4,3,2,1,0:T(8,128)(2,1)}) custom-call(s32[7]{0:T(128)} %stack.31.sc, s32[2]{0:T(128)} %off.19, s32[2]{0:T(128)} %wid.19, f32[2,2,192,256]{3,2,1,0:T(8,128)} %get-tuple-element.95.keep, bf16[1664,128]{1,0:T(8,128)(2,1)} %copy-done.7, ...), custom_call_target="tpu_custom_call" | custom-call | flops 5000000000 | bytes 15000000 | tf_op jit(solution)/shard_map/pallas_call | solution.py:482
  86.7 1.0 slice.35
  88.4 5.0 %collective-permute-done.18.zin = bf16[896,128]{1,0:T(8,128)(2,1)S(1)} collective-permute-done((bf16[896,128]{1,0:T(8,128)(2,1)}, bf16[896,128]{1,0:T(8,128)(2,1)S(1)}, u32[]{:S(2)}, u32[]{:S(2)}) %collective-permute-start.18) | collective-permute-done | bytes 229408 | tf_op jit(solution)/shard_map/ppermute | solution.py:27
  93.7 1.6 collective-permute-done.19.cin
  96.1 4.5 %shard_map.161 = (bf16[1280,128]{1,0:T(8,128)(2,1)}, bf16[1280,128]{1,0:T(8,128)(2,1)}, bf16[1280,128]{1,0:T(8,128)(2,1)}, bf16[1280,128]{1,0:T(8,128)(2,1)}, bf16[8,192,256]{2,1,0:T(8,128)(2,1)}) custom-call(s32[7]{0:T(128)} %stack.31.sc, s32[2]{0:T(128)} %off.19, s32[2]{0:T(128)} %wid.19, bf16[4,8,192,128]{3,2,1,0:T(8,128)(2,1)} %get-tuple-element.94.depth, ...), custom_call_target="tpu_custom_call" | custom-call | flops 4000000000 | bytes 12000000 | tf_op jit(solution)/shard_map/pallas_call | solution.py:482
  101.2 1.7 %collective-permute-start.27 = (bf16[1280,128]{1,0:T(8,128)(2,1)}, bf16[1280,128]{1,0:T(8,128)(2,1)S(1)}, u32[]{:S(2)}, u32[]{:S(2)}) collective-permute-start(bf16[1280,128]{1,0:T(8,128)(2,1)} %get-tuple-element.114), channel_id=1, source_target_pairs={{0,64},{64,128},{128,192},{192,0},{1,65},{65,129},{129,193},{193,1... | collective-permute-start | bytes 983048 | tf_op jit(solution)/shard_map/ppermute | solution.py:27
  102.9 2.0 %collective-permute-start.28 = (bf16[1280,128]{1,0:T(8,128)(2,1)}, bf16[1280,128]{1,0:T(8,128)(2,1)S(1)}, u32[]{:S(2)}, u32[]{:S(2)}) collective-permute-start(bf16[1280,128]{1,0:T(8,128)(2,1)} %get-tuple-element.115), channel_id=1, source_target_pairs={{0,128},{64,192},{128,0},{192,64},{1,129},{65,193},{129,1},{193,65... | collective-permute-start | bytes 983048 | tf_op jit(solution)/shard_map/ppermute | solution.py:27
  105.9 1.8 %collective-permute-done.20 = bf16[4,4,16,384]{3,2,1,0:T(8,128)(2,1)S(1)} collective-permute-done((bf16[4,4,16,384]{3,2,1,0:T(8,128)(2,1)S(1)}, bf16[4,4,16,384]{3,2,1,0:T(8,128)(2,1)S(1)}, u32[]{:S(2)}, u32[]{:S(2)}) %collective-permute-start.20) | collective-permute-done | bytes 196640 | tf_op jit(solution)/shard_map/ppermute | solution.py:27
  108.5 9.8 %shard_map.162 = (bf16[768,128]{1,0:T(8,128)(2,1)}, bf16[768,128]{1,0:T(8,128)(2,1)}, bf16[768,128]{1,0:T(8,128)(2,1)}, bf16[768,128]{1,0:T(8,128)(2,1)}) custom-call(s32[7]{0:T(128)} %stack.31.sc, s32[2]{0:T(128)} %off.19, s32[2]{0:T(128)} %wid.19, bf16[576,128]{1,0:T(8,128)(2,1)} %get-tuple-element.88.x0.f0, bf16[576,128]{1,0:T(8,128)(2,1)} %copy-done.23, ...), custom_call_target="tpu_custom_call" | custom-call | flops 10000000000 | bytes 30000000 | tf_op jit(solution)/shard_map/pallas_call | solution.py:482
  118.3 1.7 %collective-permute-start.21 = (bf16[768,128]{1,0:T(8,128)(2,1)}, bf16[768,128]{1,0:T(8,128)(2,1)S(1)}, u32[]{:S(2)}, u32[]{:S(2)}) collective-permute-start(bf16[768,128]{1,0:T(8,128)(2,1)} %get-tuple-element.106), channel_id=1, source_target_pairs={{0,64},{64,128},{128,192},{192,0},{1,65},{65,129},{129,193},{193,1... | collective-permute-start | bytes 589832 | tf_op jit(solution)/shard_map/ppermute | solution.py:27
  120.0 2.0 %collective-permute-start.22 = (bf16[768,128]{1,0:T(8,128)(2,1)}, bf16[768,128]{1,0:T(8,128)(2,1)S(1)}, u32[]{:S(2)}, u32[]{:S(2)}) collective-permute-start(bf16[768,128]{1,0:T(8,128)(2,1)} %get-tuple-element.107), channel_id=1, source_target_pairs={{0,128},{64,192},{128,0},{192,64},{1,129},{65,193},{129,1},{193,65... | collective-permute-start | bytes 589832 | tf_op jit(solution)/shard_map/ppermute | solution.py:27
  123.9 2.1 %shard_map.164 = (f32[256,128]{1,0:T(8,128)}, bf16[512,128]{1,0:T(8,128)(2,1)}, bf16[512,128]{1,0:T(8,128)(2,1)}, bf16[512,128]{1,0:T(8,128)(2,1)}, bf16[512,128]{1,0:T(8,128)(2,1)}) custom-call(bf16[1280,128]{1,0:T(8,128)(2,1)} %get-tuple-element.113.g0, bf16[1280,128]{1,0:T(8,128)(2,1)} %copy-done.9, bf16[1280,128]{1,0:T(8,128)(2,1)} %copy-done.10, ...), custom_call_target="tpu_custom_call" | custom-call | flops 1000000000 | bytes 3000000 | tf_op jit(solution)/shard_map/pallas_call | solution.py:482
  126.0 3.7 %collective-permute-start.30 = (bf16[512,128]{1,0:T(8,128)(2,1)}, bf16[512,128]{1,0:T(8,128)(2,1)S(1)}, u32[]{:S(2)}, u32[]{:S(2)}) collective-permute-start(bf16[512,128]{1,0:T(8,128)(2,1)} %get-tuple-element.118), channel_id=1, source_target_pairs={{0,12},{4,0},{8,4},{12,8},{1,13},{5,1},{9,5},{13,9},{2,14},{6,2},{... | collective-permute-start | bytes 393224 | tf_op jit(solution)/shard_map/ppermute | solution.py:27
  129.7 1.7 %collective-permute-start.31 = (bf16[512,128]{1,0:T(8,128)(2,1)}, bf16[512,128]{1,0:T(8,128)(2,1)S(1)}, u32[]{:S(2)}, u32[]{:S(2)}) collective-permute-start(bf16[512,128]{1,0:T(8,128)(2,1)} %get-tuple-element.119), channel_id=1, source_target_pairs={{0,8},{4,12},{8,0},{12,4},{1,9},{5,13},{9,1},{13,5},{2,10},{6,14},... | collective-permute-start | bytes 393224 | tf_op jit(solution)/shard_map/ppermute | solution.py:27
  131.5 1.3 collective-permute-start.32
  133.5 2.0 %shard_map.163 = (bf16[320,128]{1,0:T(8,128)(2,1)}, bf16[320,128]{1,0:T(8,128)(2,1)}, bf16[320,128]{1,0:T(8,128)(2,1)}, bf16[320,128]{1,0:T(8,128)(2,1)}) custom-call(bf16[768,128]{1,0:T(8,128)(2,1)} %get-tuple-element.105.v0, bf16[768,128]{1,0:T(8,128)(2,1)} %copy-done.17, bf16[768,128]{1,0:T(8,128)(2,1)} %copy-done.18, bf16[768,128]{1,0:T(8,128)(2,1)} %copy-done.19), custom_call_target="tpu_custom_call" | custom-call | flops 1000000000 | bytes 3000000 | tf_op jit(solution)/shard_map/pallas_call | solution.py:482
  135.5 2.8 %collective-permute-start.24 = (bf16[320,128]{1,0:T(8,128)(2,1)}, bf16[320,128]{1,0:T(8,128)(2,1)S(1)}, u32[]{:S(2)}, u32[]{:S(2)}) collective-permute-start(bf16[320,128]{1,0:T(8,128)(2,1)} %get-tuple-element.110), channel_id=1, source_target_pairs={{0,12},{4,0},{8,4},{12,8},{1,13},{5,1},{9,5},{13,9},{2,14},{6,2},{... | collective-permute-start | bytes 245768 | tf_op jit(solution)/shard_map/ppermute | solution.py:27
  138.4 4.2 %collective-permute-start.25 = (bf16[320,128]{1,0:T(8,128)(2,1)}, bf16[320,128]{1,0:T(8,128)(2,1)S(1)}, u32[]{:S(2)}, u32[]{:S(2)}) collective-permute-start(bf16[320,128]{1,0:T(8,128)(2,1)} %get-tuple-element.111), channel_id=1, source_target_pairs={{0,8},{4,12},{8,0},{12,4},{1,9},{5,13},{9,1},{13,5},{2,10},{6,14},... | collective-permute-start | bytes 245768 | tf_op jit(solution)/shard_map/ppermute | solution.py:27
  142.7 3.5 %collective-permute-done.32.h3 = bf16[512,128]{1,0:T(8,128)(2,1)S(1)} collective-permute-done((bf16[512,128]{1,0:T(8,128)(2,1)}, bf16[512,128]{1,0:T(8,128)(2,1)S(1)}, u32[]{:S(2)}, u32[]{:S(2)}) %collective-permute-start.32) | collective-permute-done | bytes 131104 | tf_op jit(solution)/shard_map/ppermute | solution.py:27
  146.2 3.8 %collective-permute-done.25.z2 = bf16[320,128]{1,0:T(8,128)(2,1)S(1)} collective-permute-done((bf16[320,128]{1,0:T(8,128)(2,1)}, bf16[320,128]{1,0:T(8,128)(2,1)S(1)}, u32[]{:S(2)}, u32[]{:S(2)}) %collective-permute-start.25) | collective-permute-done | bytes 81952 | tf_op jit(solution)/shard_map/ppermute | solution.py:27
  150.7 2.0 %shard_map.166 = (f32[320,128]{1,0:T(8,128)}, bf16[320,128]{1,0:T(8,128)(2,1)}) custom-call(bf16[320,128]{1,0:T(8,128)(2,1)} %get-tuple-element.109.z0, bf16[320,128]{1,0:T(8,128)(2,1)} %copy-done.32, bf16[320,128]{1,0:T(8,128)(2,1)} %copy-done.33, bf16[320,128]{1,0:T(8,128)(2,1)} %copy-done.34, f32[256,128]{1,0:T(8,128)} %get-tuple-element.123.gown, ...), custom_call_target="tpu_custom_call" | custom-call | flops 1000000000 | bytes 3000000 | tf_op jit(solution)/shard_map/pallas_call | solution.py:482
  152.7 1.3 collective-permute-start.35
  154.0 2.4 %collective-permute-start.34 = (bf16[320,128]{1,0:T(8,128)(2,1)}, bf16[320,128]{1,0:T(8,128)(2,1)S(1)}, u32[]{:S(2)}, u32[]{:S(2)}) collective-permute-start(bf16[320,128]{1,0:T(8,128)(2,1)} %get-tuple-element.125), channel_id=1, source_target_pairs={{0,32},{16,48},{32,0},{48,16},{1,33},{17,49},{33,1},{49,17},{2,34}... | collective-permute-start | bytes 245768 | tf_op jit(solution)/shard_map/ppermute | solution.py:27
  156.4 2.6 %collective-permute-start.33 = (bf16[320,128]{1,0:T(8,128)(2,1)}, bf16[320,128]{1,0:T(8,128)(2,1)S(1)}, u32[]{:S(2)}, u32[]{:S(2)}) collective-permute-start(bf16[320,128]{1,0:T(8,128)(2,1)} %get-tuple-element.125), channel_id=1, source_target_pairs={{0,16},{16,32},{32,48},{48,0},{1,17},{17,33},{33,49},{49,1},{2,18}... | collective-permute-start | bytes 245768 | tf_op jit(solution)/shard_map/ppermute | solution.py:27
  159.0 3.2 %shard_map.165 = (bf16[2,8,128,128]{3,2,1,0:T(8,128)(2,1)}, bf16[2,32,16,128]{3,2,1,0:T(8,128)(2,1)}) custom-call(s32[7]{0:T(128)} %stack.31.sc, s32[2]{0:T(128)} %off.19, s32[2]{0:T(128)} %wid.19, bf16[320,128]{1,0:T(8,128)(2,1)} %get-tuple-element.109.z0, bf16[320,128]{1,0:T(8,128)(2,1)} %copy-done.32, bf16[320,128]{1,0:T(8,128)(2,1)} %copy-done.33, ...), custom_call_target="tpu_custom_call" | custom-call | flops 3000000000 | bytes 9000000 | tf_op jit(solution)/shard_map/pallas_call | solution.py:482
  162.3 1.7 %copy.18 = bf16[16,2,32,128]{3,2,1,0:T(8,128)(2,1)} copy(bf16[16,2,32,128]{3,0,2,1:T(8,128)(2,1)} %bitcast.23) | data formatting | bytes 524288
  164.7 1.7 %shard_map.167 = (f32[9,1,128]{2,1,0:T(1,128)}, f32[1,128,256]{2,1,0:T(8,128)}, f32[1,16]{1,0:T(1,128)}, f32[1,16,256]{2,1,0:T(8,128)}, f32[1,16]{1,0:T(1,128)}) custom-call(f32[320,128]{1,0:T(8,128)} %get-tuple-element.124.own, bf16[320,128]{1,0:T(8,128)(2,1)} %copy-done.37, bf16[320,128]{1,0:T(8,128)(2,1)} %copy-done.36, bf16[320,128]{1,0:T(8,128)(2,1)} %copy-done.35), custom_call_target="tpu_custom_call" | custom-call | flops 1000000000 | bytes 3000000 | tf_op jit(solution)/shard_map/pallas_call | solution.py:482
  (138 shorter events, 19.7 us)
Async XLA Ops:
  0.6 7.4 %copy-start = (bf16[16,2,32,128]{3,2,1,0:T(8,128)(2,1)S(1)}, bf16[16,2,32,128]{3,2,1,0:T(8,128)(2,1)}, u32[]{:S(2)}) copy-start(bf16[16,2,32,128]{3,2,1,0:T(8,128)(2,1)} %param.19) | copy-start | bytes 786436
  3.5 9.9 %collective-permute-start.2 = (bf16[128,128]{1,0:T(8,128)(2,1)}, bf16[128,128]{1,0:T(8,128)(2,1)S(1)}, u32[]{:S(2)}, u32[]{:S(2)}) collective-permute-start(bf16[128,128]{1,0:T(8,128)(2,1)} %shard_map.153.b0), channel_id=1, source_target_pairs={{0,192},{64,0},{128,64},{192,128},{1,193},{65,1},{129,65},{193,129... | collective-permute-start | bytes 98312 | tf_op jit(solution)/shard_map/ppermute | solution.py:27
  6.3 7.2 %collective-permute-start.1 = (bf16[128,128]{1,0:T(8,128)(2,1)}, bf16[128,128]{1,0:T(8,128)(2,1)S(1)}, u32[]{:S(2)}, u32[]{:S(2)}) collective-permute-start(bf16[128,128]{1,0:T(8,128)(2,1)} %shard_map.153.b0), channel_id=1, source_target_pairs={{0,128},{64,192},{128,0},{192,64},{1,129},{65,193},{129,1},{193,65... | collective-permute-start | bytes 98312 | tf_op jit(solution)/shard_map/ppermute | solution.py:27
  7.1 6.4 %collective-permute-start = (bf16[128,128]{1,0:T(8,128)(2,1)}, bf16[128,128]{1,0:T(8,128)(2,1)S(1)}, u32[]{:S(2)}, u32[]{:S(2)}) collective-permute-start(bf16[128,128]{1,0:T(8,128)(2,1)} %shard_map.153.b0), channel_id=1, source_target_pairs={{0,64},{64,128},{128,192},{192,0},{1,65},{65,129},{129,193},{193,1... | collective-permute-start | bytes 98312 | tf_op jit(solution)/shard_map/ppermute | solution.py:27
  14.1 24.7 %copy-start.28 = (bf16[576,128]{1,0:T(8,128)(2,1)S(1)}, bf16[576,128]{1,0:T(8,128)(2,1)}, u32[]{:S(2)}) copy-start(bf16[576,128]{1,0:T(8,128)(2,1)} %get-tuple-element.82) | copy-start | bytes 442372
  14.1 24.8 %copy-start.27 = (bf16[576,128]{1,0:T(8,128)(2,1)S(1)}, bf16[576,128]{1,0:T(8,128)(2,1)}, u32[]{:S(2)}) copy-start(bf16[576,128]{1,0:T(8,128)(2,1)} %get-tuple-element.83) | copy-start | bytes 442372
  14.1 29.8 %copy-start.26 = (bf16[576,128]{1,0:T(8,128)(2,1)S(1)}, bf16[576,128]{1,0:T(8,128)(2,1)}, u32[]{:S(2)}) copy-start(bf16[576,128]{1,0:T(8,128)(2,1)} %get-tuple-element.84) | copy-start | bytes 442372
  16.4 13.8 %collective-permute-start.8 = (bf16[368,128]{1,0:T(8,128)(2,1)}, bf16[368,128]{1,0:T(8,128)(2,1)S(1)}, u32[]{:S(2)}, u32[]{:S(2)}) collective-permute-start(bf16[368,128]{1,0:T(8,128)(2,1)} %shard_map.155.a0), channel_id=1, source_target_pairs={{0,12},{4,0},{8,4},{12,8},{1,13},{5,1},{9,5},{13,9},{2,14},{6,2},{... | collective-permute-start | bytes 282632 | tf_op jit(solution)/shard_map/ppermute | solution.py:27
  22.7 11.0 %collective-permute-start.7 = (bf16[368,128]{1,0:T(8,128)(2,1)}, bf16[368,128]{1,0:T(8,128)(2,1)S(1)}, u32[]{:S(2)}, u32[]{:S(2)}) collective-permute-start(bf16[368,128]{1,0:T(8,128)(2,1)} %shard_map.155.a0), channel_id=1, source_target_pairs={{0,8},{4,12},{8,0},{12,4},{1,9},{5,13},{9,1},{13,5},{2,10},{6,14},... | collective-permute-start | bytes 282632 | tf_op jit(solution)/shard_map/ppermute | solution.py:27
  23.6 10.2 %collective-permute-start.6 = (bf16[368,128]{1,0:T(8,128)(2,1)}, bf16[368,128]{1,0:T(8,128)(2,1)S(1)}, u32[]{:S(2)}, u32[]{:S(2)}) collective-permute-start(bf16[368,128]{1,0:T(8,128)(2,1)} %shard_map.155.a0), channel_id=1, source_target_pairs={{0,4},{4,8},{8,12},{12,0},{1,5},{5,9},{9,13},{13,1},{2,6},{6,10},{... | collective-permute-start | bytes 282632 | tf_op jit(solution)/shard_map/ppermute | solution.py:27
  30.2 21.8 %copy-start.4 = (bf16[368,128]{1,0:T(8,128)(2,1)}, bf16[368,128]{1,0:T(8,128)(2,1)S(1)}, u32[]{:S(2)}) copy-start(bf16[368,128]{1,0:T(8,128)(2,1)S(1)} %collective-permute-done.8.a3) | copy-start | bytes 282628
  33.7 18.3 %copy-start.5 = (bf16[368,128]{1,0:T(8,128)(2,1)}, bf16[368,128]{1,0:T(8,128)(2,1)S(1)}, u32[]{:S(2)}) copy-start(bf16[368,128]{1,0:T(8,128)(2,1)S(1)} %collective-permute-done.7.a2) | copy-start | bytes 282628
  33.7 18.3 %copy-start.6 = (bf16[368,128]{1,0:T(8,128)(2,1)}, bf16[368,128]{1,0:T(8,128)(2,1)S(1)}, u32[]{:S(2)}) copy-start(bf16[368,128]{1,0:T(8,128)(2,1)S(1)} %collective-permute-done.6.a1) | copy-start | bytes 282628
  33.8 14.3 %copy-start.2 = (bf16[1216,128]{1,0:T(8,128)(2,1)}, bf16[1216,128]{1,0:T(8,128)(2,1)S(1)}, u32[]{:S(2)}) copy-start(bf16[1216,128]{1,0:T(8,128)(2,1)S(1)} %pad_maximum_fusion.1.q0) | copy-start | bytes 933892
  33.8 10.1 %collective-permute-start.11 = (bf16[1216,128]{1,0:T(8,128)(2,1)S(1)}, bf16[1216,128]{1,0:T(8,128)(2,1)S(1)}, u32[]{:S(2)}, u32[]{:S(2)}) collective-permute-start(bf16[1216,128]{1,0:T(8,128)(2,1)S(1)} %pad_maximum_fusion.1.q0), channel_id=1, source_target_pairs={{0,48},{16,0},{32,16},{48,32},{1,49},{17,1},{33,17},{49,33},{2,50}... | collective-permute-start | bytes 933896 | tf_op jit(solution)/shard_map/ppermute | solution.py:27
  34.3 12.9 %collective-permute-start.10 = (bf16[1216,128]{1,0:T(8,128)(2,1)S(1)}, bf16[1216,128]{1,0:T(8,128)(2,1)S(1)}, u32[]{:S(2)}, u32[]{:S(2)}) collective-permute-start(bf16[1216,128]{1,0:T(8,128)(2,1)S(1)} %pad_maximum_fusion.1.q0), channel_id=1, source_target_pairs={{0,32},{16,48},{32,0},{48,16},{1,33},{17,49},{33,1},{49,17},{2,34}... | collective-permute-start | bytes 933896 | tf_op jit(solution)/shard_map/ppermute | solution.py:27
  36.9 11.2 %collective-permute-start.9 = (bf16[1216,128]{1,0:T(8,128)(2,1)S(1)}, bf16[1216,128]{1,0:T(8,128)(2,1)S(1)}, u32[]{:S(2)}, u32[]{:S(2)}) collective-permute-start(bf16[1216,128]{1,0:T(8,128)(2,1)S(1)} %pad_maximum_fusion.1.q0), channel_id=1, source_target_pairs={{0,16},{16,32},{32,48},{48,0},{1,17},{17,33},{33,49},{49,1},{2,18}... | collective-permute-start | bytes 933896 | tf_op jit(solution)/shard_map/ppermute | solution.py:27
  38.8 13.3 %collective-permute-start.3 = (bf16[576,128]{1,0:T(8,128)(2,1)S(1)}, bf16[576,128]{1,0:T(8,128)(2,1)S(1)}, u32[]{:S(2)}, u32[]{:S(2)}) collective-permute-start(bf16[576,128]{1,0:T(8,128)(2,1)S(1)} %copy-done.28), channel_id=1, source_target_pairs={{0,4},{4,8},{8,12},{12,0},{1,5},{5,9},{9,13},{13,1},{2,6},{6,10},{... | collective-permute-start | bytes 442376 | tf_op jit(solution)/shard_map/ppermute | solution.py:27
  38.9 13.2 %collective-permute-start.4 = (bf16[576,128]{1,0:T(8,128)(2,1)S(1)}, bf16[576,128]{1,0:T(8,128)(2,1)S(1)}, u32[]{:S(2)}, u32[]{:S(2)}) collective-permute-start(bf16[576,128]{1,0:T(8,128)(2,1)S(1)} %copy-done.27), channel_id=1, source_target_pairs={{0,8},{4,12},{8,0},{12,4},{1,9},{5,13},{9,1},{13,5},{2,10},{6,14},... | collective-permute-start | bytes 442376 | tf_op jit(solution)/shard_map/ppermute | solution.py:27
  43.9 12.8 %collective-permute-start.5 = (bf16[576,128]{1,0:T(8,128)(2,1)S(1)}, bf16[576,128]{1,0:T(8,128)(2,1)S(1)}, u32[]{:S(2)}, u32[]{:S(2)}) collective-permute-start(bf16[576,128]{1,0:T(8,128)(2,1)S(1)} %copy-done.26), channel_id=1, source_target_pairs={{0,12},{4,0},{8,4},{12,8},{1,13},{5,1},{9,5},{13,9},{2,14},{6,2},{... | collective-permute-start | bytes 442376 | tf_op jit(solution)/shard_map/ppermute | solution.py:27
  67.8 2.0 %collective-permute-start.12 = (bf16[1664,128]{1,0:T(8,128)(2,1)}, bf16[1664,128]{1,0:T(8,128)(2,1)S(1)}, u32[]{:S(2)}, u32[]{:S(2)}) collective-permute-start(bf16[1664,128]{1,0:T(8,128)(2,1)} %get-tuple-element.96), channel_id=1, source_target_pairs={{0,1},{1,0},{2,3},{3,2},{4,5},{5,4},{6,7},{7,6},{8,9},{9,8},{10,11... | collective-permute-start | bytes 1277960 | tf_op jit(solution)/shard_map/ppermute | solution.py:27
  67.9 7.3 %collective-permute-start.14 = (bf16[768,128]{1,0:T(8,128)(2,1)S(1)}, bf16[768,128]{1,0:T(8,128)(2,1)S(1)}, u32[]{:S(2)}, u32[]{:S(2)}) collective-permute-start(bf16[768,128]{1,0:T(8,128)(2,1)S(1)} %copy-done.16), channel_id=1, source_target_pairs={{0,2},{2,0},{1,3},{3,1},{4,6},{6,4},{5,7},{7,5},{8,10},{10,8},{9,1... | collective-permute-start | bytes 589832 | tf_op jit(solution)/shard_map/ppermute | solution.py:27
  72.7 7.9 %collective-permute-start.13 = (bf16[896,128]{1,0:T(8,128)(2,1)}, bf16[896,128]{1,0:T(8,128)(2,1)S(1)}, u32[]{:S(2)}, u32[]{:S(2)}) collective-permute-start(bf16[896,128]{1,0:T(8,128)(2,1)} %shard_map.159), channel_id=1, source_target_pairs={{0,2},{2,0},{1,3},{3,1},{4,6},{6,4},{5,7},{7,5},{8,10},{10,8},{9,1... | collective-permute-start | bytes 688136 | tf_op jit(solution)/shard_map/ppermute | solution.py:27
  72.9 2.3 %collective-permute-start.15 = (bf16[768,128]{1,0:T(8,128)(2,1)S(1)}, bf16[768,128]{1,0:T(8,128)(2,1)S(1)}, u32[]{:S(2)}, u32[]{:S(2)}) collective-permute-start(bf16[768,128]{1,0:T(8,128)(2,1)S(1)} %copy-done.16), channel_id=1, source_target_pairs={{0,1},{1,0},{2,3},{3,2},{4,5},{5,4},{6,7},{7,6},{8,9},{9,8},{10,11... | collective-permute-start | bytes 589832 | tf_op jit(solution)/shard_map/ppermute | solution.py:27
  75.2 5.4 %copy-start.20 = (bf16[768,128]{1,0:T(8,128)(2,1)}, bf16[768,128]{1,0:T(8,128)(2,1)S(1)}, u32[]{:S(2)}) copy-start(bf16[768,128]{1,0:T(8,128)(2,1)S(1)} %collective-permute-done.14.ownz) | copy-start | bytes 589828
  75.2 1.4 collective-permute-start.16
  86.4 7.2 %copy-start.1 = (f32[2,4,4,16,384]{4,3,2,1,0:T(8,128)S(1)}, f32[2,4,4,16,384]{4,3,2,1,0:T(8,128)}, u32[]{:S(2)}) copy-start(f32[2,4,4,16,384]{4,3,2,1,0:T(8,128)} %get-tuple-element.98) | copy-start | bytes 2359300
  86.4 7.0 %collective-permute-start.18 = (bf16[896,128]{1,0:T(8,128)(2,1)}, bf16[896,128]{1,0:T(8,128)(2,1)S(1)}, u32[]{:S(2)}, u32[]{:S(2)}) collective-permute-start(bf16[896,128]{1,0:T(8,128)(2,1)} %get-tuple-element.100.zout), channel_id=1, source_target_pairs={{0,2},{2,0},{1,3},{3,1},{4,6},{6,4},{5,7},{7,5},{8,10},{10,8},{9,1... | collective-permute-start | bytes 688136 | tf_op jit(solution)/shard_map/ppermute | solution.py:27
  86.7 6.9 %collective-permute-start.17 = (bf16[2,4,4,16,384]{4,3,2,1,0:T(8,128)(2,1)}, bf16[2,4,4,16,384]{4,3,2,1,0:T(8,128)(2,1)S(1)}, u32[]{:S(2)}, u32[]{:S(2)}) collective-permute-start(bf16[2,4,4,16,384]{4,3,2,1,0:T(8,128)(2,1)} %get-tuple-element.99), channel_id=1, source_target_pairs={{0,1},{1,0},{2,3},{3,2},{4,5},{5,4},{6,7},{7,6},{8,9},{9,8},{10,11... | collective-permute-start | bytes 1179656 | tf_op jit(solution)/shard_map/ppermute | solution.py:27
  93.5 1.9 %collective-permute-start.19 = (bf16[1664,128]{1,0:T(8,128)(2,1)S(1)}, bf16[1664,128]{1,0:T(8,128)(2,1)S(1)}, u32[]{:S(2)}, u32[]{:S(2)}) collective-permute-start(bf16[1664,128]{1,0:T(8,128)(2,1)S(1)} %pad_maximum_fusion), channel_id=1, source_target_pairs={{0,1},{1,0},{2,3},{3,2},{4,5},{5,4},{6,7},{7,6},{8,9},{9,8},{10,11... | collective-permute-start | bytes 1277960 | tf_op jit(solution)/shard_map/ppermute | solution.py:27
  100.7 7.0 %collective-permute-start.20 = (bf16[4,4,16,384]{3,2,1,0:T(8,128)(2,1)S(1)}, bf16[4,4,16,384]{3,2,1,0:T(8,128)(2,1)S(1)}, u32[]{:S(2)}, u32[]{:S(2)}) collective-permute-start(bf16[4,4,16,384]{3,2,1,0:T(8,128)(2,1)S(1)} %fusion), channel_id=1, source_target_pairs={{0,2},{2,0},{1,3},{3,1},{4,6},{6,4},{5,7},{7,5},{8,10},{10,8},{9,1... | collective-permute-start | bytes 589832 | tf_op jit(solution)/shard_map/ppermute | solution.py:27
  101.2 20.9 %collective-permute-start.27 = (bf16[1280,128]{1,0:T(8,128)(2,1)}, bf16[1280,128]{1,0:T(8,128)(2,1)S(1)}, u32[]{:S(2)}, u32[]{:S(2)}) collective-permute-start(bf16[1280,128]{1,0:T(8,128)(2,1)} %get-tuple-element.114), channel_id=1, source_target_pairs={{0,64},{64,128},{128,192},{192,0},{1,65},{65,129},{129,193},{193,1... | collective-permute-start | bytes 983048 | tf_op jit(solution)/shard_map/ppermute | solution.py:27
  102.9 20.1 %collective-permute-start.28 = (bf16[1280,128]{1,0:T(8,128)(2,1)}, bf16[1280,128]{1,0:T(8,128)(2,1)S(1)}, u32[]{:S(2)}, u32[]{:S(2)}) collective-permute-start(bf16[1280,128]{1,0:T(8,128)(2,1)} %get-tuple-element.115), channel_id=1, source_target_pairs={{0,128},{64,192},{128,0},{192,64},{1,129},{65,193},{129,1},{193,65... | collective-permute-start | bytes 983048 | tf_op jit(solution)/shard_map/ppermute | solution.py:27
  104.9 18.1 %collective-permute-start.29 = (bf16[1280,128]{1,0:T(8,128)(2,1)}, bf16[1280,128]{1,0:T(8,128)(2,1)S(1)}, u32[]{:S(2)}, u32[]{:S(2)}) collective-permute-start(bf16[1280,128]{1,0:T(8,128)(2,1)} %get-tuple-element.116), channel_id=1, source_target_pairs={{0,192},{64,0},{128,64},{192,128},{1,193},{65,1},{129,65},{193,129... | collective-permute-start | bytes 983048 | tf_op jit(solution)/shard_map/ppermute | solution.py:27
  118.3 13.2 %collective-permute-start.21 = (bf16[768,128]{1,0:T(8,128)(2,1)}, bf16[768,128]{1,0:T(8,128)(2,1)S(1)}, u32[]{:S(2)}, u32[]{:S(2)}) collective-permute-start(bf16[768,128]{1,0:T(8,128)(2,1)} %get-tuple-element.106), channel_id=1, source_target_pairs={{0,64},{64,128},{128,192},{192,0},{1,65},{65,129},{129,193},{193,1... | collective-permute-start | bytes 589832 | tf_op jit(solution)/shard_map/ppermute | solution.py:27
  120.0 12.7 %collective-permute-start.22 = (bf16[768,128]{1,0:T(8,128)(2,1)}, bf16[768,128]{1,0:T(8,128)(2,1)S(1)}, u32[]{:S(2)}, u32[]{:S(2)}) collective-permute-start(bf16[768,128]{1,0:T(8,128)(2,1)} %get-tuple-element.107), channel_id=1, source_target_pairs={{0,128},{64,192},{128,0},{192,64},{1,129},{65,193},{129,1},{193,65... | collective-permute-start | bytes 589832 | tf_op jit(solution)/shard_map/ppermute | solution.py:27
  122.1 10.7 %collective-permute-start.23 = (bf16[768,128]{1,0:T(8,128)(2,1)}, bf16[768,128]{1,0:T(8,128)(2,1)S(1)}, u32[]{:S(2)}, u32[]{:S(2)}) collective-permute-start(bf16[768,128]{1,0:T(8,128)(2,1)} %get-tuple-element.108), channel_id=1, source_target_pairs={{0,192},{64,0},{128,64},{192,128},{1,193},{65,1},{129,65},{193,129... | collective-permute-start | bytes 589832 | tf_op jit(solution)/shard_map/ppermute | solution.py:27
  126.0 16.5 %collective-permute-start.30 = (bf16[512,128]{1,0:T(8,128)(2,1)}, bf16[512,128]{1,0:T(8,128)(2,1)S(1)}, u32[]{:S(2)}, u32[]{:S(2)}) collective-permute-start(bf16[512,128]{1,0:T(8,128)(2,1)} %get-tuple-element.118), channel_id=1, source_target_pairs={{0,12},{4,0},{8,4},{12,8},{1,13},{5,1},{9,5},{13,9},{2,14},{6,2},{... | collective-permute-start | bytes 393224 | tf_op jit(solution)/shard_map/ppermute | solution.py:27
  129.7 13.0 %collective-permute-start.31 = (bf16[512,128]{1,0:T(8,128)(2,1)}, bf16[512,128]{1,0:T(8,128)(2,1)S(1)}, u32[]{:S(2)}, u32[]{:S(2)}) collective-permute-start(bf16[512,128]{1,0:T(8,128)(2,1)} %get-tuple-element.119), channel_id=1, source_target_pairs={{0,8},{4,12},{8,0},{12,4},{1,9},{5,13},{9,1},{13,5},{2,10},{6,14},... | collective-permute-start | bytes 393224 | tf_op jit(solution)/shard_map/ppermute | solution.py:27
  131.5 14.8 %collective-permute-start.32 = (bf16[512,128]{1,0:T(8,128)(2,1)}, bf16[512,128]{1,0:T(8,128)(2,1)S(1)}, u32[]{:S(2)}, u32[]{:S(2)}) collective-permute-start(bf16[512,128]{1,0:T(8,128)(2,1)} %get-tuple-element.120), channel_id=1, source_target_pairs={{0,4},{4,8},{8,12},{12,0},{1,5},{5,9},{9,13},{13,1},{2,6},{6,10},{... | collective-permute-start | bytes 393224 | tf_op jit(solution)/shard_map/ppermute | solution.py:27
  135.5 10.7 %collective-permute-start.24 = (bf16[320,128]{1,0:T(8,128)(2,1)}, bf16[320,128]{1,0:T(8,128)(2,1)S(1)}, u32[]{:S(2)}, u32[]{:S(2)}) collective-permute-start(bf16[320,128]{1,0:T(8,128)(2,1)} %get-tuple-element.110), channel_id=1, source_target_pairs={{0,12},{4,0},{8,4},{12,8},{1,13},{5,1},{9,5},{13,9},{2,14},{6,2},{... | collective-permute-start | bytes 245768 | tf_op jit(solution)/shard_map/ppermute | solution.py:27
  138.4 11.7 %collective-permute-start.25 = (bf16[320,128]{1,0:T(8,128)(2,1)}, bf16[320,128]{1,0:T(8,128)(2,1)S(1)}, u32[]{:S(2)}, u32[]{:S(2)}) collective-permute-start(bf16[320,128]{1,0:T(8,128)(2,1)} %get-tuple-element.111), channel_id=1, source_target_pairs={{0,8},{4,12},{8,0},{12,4},{1,9},{5,13},{9,1},{13,5},{2,10},{6,14},... | collective-permute-start | bytes 245768 | tf_op jit(solution)/shard_map/ppermute | solution.py:27
  142.6 7.5 %copy-start.29 = (bf16[512,128]{1,0:T(8,128)(2,1)}, bf16[512,128]{1,0:T(8,128)(2,1)S(1)}, u32[]{:S(2)}) copy-start(bf16[512,128]{1,0:T(8,128)(2,1)S(1)} %collective-permute-done.30.h1) | copy-start | bytes 393220
  142.6 7.5 %collective-permute-start.26 = (bf16[320,128]{1,0:T(8,128)(2,1)}, bf16[320,128]{1,0:T(8,128)(2,1)S(1)}, u32[]{:S(2)}, u32[]{:S(2)}) collective-permute-start(bf16[320,128]{1,0:T(8,128)(2,1)} %get-tuple-element.112), channel_id=1, source_target_pairs={{0,4},{4,8},{8,12},{12,0},{1,5},{5,9},{9,13},{13,1},{2,6},{6,10},{... | collective-permute-start | bytes 245768 | tf_op jit(solution)/shard_map/ppermute | solution.py:27
  142.7 7.4 %copy-start.30 = (bf16[512,128]{1,0:T(8,128)(2,1)}, bf16[512,128]{1,0:T(8,128)(2,1)S(1)}, u32[]{:S(2)}) copy-start(bf16[512,128]{1,0:T(8,128)(2,1)S(1)} %collective-permute-done.31.h2) | copy-start | bytes 393220
  152.7 11.3 %collective-permute-start.35 = (bf16[320,128]{1,0:T(8,128)(2,1)}, bf16[320,128]{1,0:T(8,128)(2,1)S(1)}, u32[]{:S(2)}, u32[]{:S(2)}) collective-permute-start(bf16[320,128]{1,0:T(8,128)(2,1)} %get-tuple-element.125), channel_id=1, source_target_pairs={{0,48},{16,0},{32,16},{48,32},{1,49},{17,1},{33,17},{49,33},{2,50}... | collective-permute-start | bytes 245768 | tf_op jit(solution)/shard_map/ppermute | solution.py:27
  154.0 10.0 %collective-permute-start.34 = (bf16[320,128]{1,0:T(8,128)(2,1)}, bf16[320,128]{1,0:T(8,128)(2,1)S(1)}, u32[]{:S(2)}, u32[]{:S(2)}) collective-permute-start(bf16[320,128]{1,0:T(8,128)(2,1)} %get-tuple-element.125), channel_id=1, source_target_pairs={{0,32},{16,48},{32,0},{48,16},{1,33},{17,49},{33,1},{49,17},{2,34}... | collective-permute-start | bytes 245768 | tf_op jit(solution)/shard_map/ppermute | solution.py:27
  156.4 7.6 %collective-permute-start.33 = (bf16[320,128]{1,0:T(8,128)(2,1)}, bf16[320,128]{1,0:T(8,128)(2,1)S(1)}, u32[]{:S(2)}, u32[]{:S(2)}) collective-permute-start(bf16[320,128]{1,0:T(8,128)(2,1)} %get-tuple-element.125), channel_id=1, source_target_pairs={{0,16},{16,32},{32,48},{48,0},{1,17},{17,33},{33,49},{49,1},{2,18}... | collective-permute-start | bytes 245768 | tf_op jit(solution)/shard_map/ppermute | solution.py:27
  (29 other events, 51.7 us)

commit v3 on v2

--- a/solution.py
+++ b/solution.py
@@ -171,7 +171,7 @@
     lax.fori_loop(0, 32, body, 0)
 
 
-def product_kernel(sc, off, wid, depth, wfull, x0, x1, x2, x3, keep, send, pscr):
+def product_kernel(sc, off, wid, depth, wfull, x0, x1, x2, x3, keep0, keep1, send, ups, pscr):
     mz, mc = sc[3], sc[4]
     for s in range(4):
         n = WIN[s]
@@ -186,30 +186,30 @@
     for zr in range(2):
         zz = 2 * jnp.bitwise_xor(mz, zr)
         for r in range(2):
-            keep[zr, r] = pscr[4 * mc + zz + r]
+            (keep0, keep1)[zr][r] = pscr[4 * mc + zz + r]
             for b in range(2):
                 at = 768 * zr + 384 * b + 192 * r
                 send[at:at + 192, :] = pscr[4 * (1 - mc) + zz + r, :, 128 * b:128 * b + 128].astype(BF)
         for k, x in enumerate((x0, x1, x2, x3)):
             at = 1536 + 64 * zr + 16 * k
             send[at:at + 16, :] = x[528 + 32 * zr:544 + 32 * zr, :]
-
-
-def add_kernel(keep, rcore, x0, x1, x2, x3, out):
+            ups[64 * zr + 16 * k:64 * zr + 16 * k + 16, :] = x[512 + 32 * zr:528 + 32 * zr, :]
+
+
+def add_kernel(keep1, rcore, ups, out):
     for r in range(2):
         for b in range(2):
             at = 384 * b + 192 * r
-            v = keep[1, r, :, 128 * b:128 * b + 128] + rcore[768 + at:960 + at, :].astype(F32)
+            v = keep1[r, :, 128 * b:128 * b + 128] + rcore[768 + at:960 + at, :].astype(F32)
             out[at:at + 192, :] = v.astype(BF)
-    for k, x in enumerate((x0, x1, x2, x3)):
-        out[768 + 32 * k:784 + 32 * k, :] = x[544:560, :]
+    for k in range(4):
+        out[768 + 32 * k:784 + 32 * k, :] = ups[64 + 16 * k:80 + 16 * k, :]
         out[784 + 32 * k:800 + 32 * k, :] = rcore[1600 + 16 * k:1616 + 16 * k, :]
 
 
-def middle_kernel(sc, off, wid, keep, rcore, rzl, own, ownz, ownc, ownzc, f0, f1, f2, f3, labels,
+def middle_kernel(sc, off, wid, keep0, rcore, rzl, own, ownz, ownc, ownzc, ups, labels,
                   zout, res0, gkeep, gsend, pjs, upscr, gscr):
     q, zh, mz, mc = sc[1], sc[2], sc[3], sc[4]
-    fs = (f0, f1, f2, f3)
     for k, zr, cr, blk in blocks(sc):
         rows = pl.ds(pl.multiple_of(16 * blk, 16), 16)
         for r in range(4):
@@ -219,7 +219,7 @@
                 at = base + 16 * b
                 pjs[s, rows, 128 * b:128 * b + 128] = ((own, ownz), (ownc, ownzc))[cr][zr][at:at + 16, :]
         if zr == 0:
-            u = fs[k][512:528, :] if cr == 0 else rcore[1536 + 16 * k:1552 + 16 * k, :]
+            u = ups[16 * k:16 * k + 16, :] if cr == 0 else rcore[1536 + 16 * k:1552 + 16 * k, :]
         else:
             u = rzl[768 + 32 * k + 16 * cr:784 + 32 * k + 16 * cr, :]
         upscr[rows, :] = u.astype(F32)
@@ -239,7 +239,7 @@
     for r in range(2):
         got = [rcore[384 * b + 192 * r:384 * b + 192 * r + 192, :].astype(F32)
                + rzl[384 * b + 192 * r:384 * b + 192 * r + 192, :].astype(F32) for b in range(2)]
-        sums.append(keep[0, r] + jnp.concatenate(got, axis=1))
+        sums.append(keep0[r] + jnp.concatenate(got, axis=1))
     pre_now = jnp.stack(sums)
     pres, acts = [], []
     z = dotf(jnp.where((lane >= 3) & (lane < 6), 1.0, 0.0).astype(BF), pjs[0, :, 256:384], ((1,), (1,)))[0:1, :]
@@ -526,14 +526,14 @@
     ownz = shift(own, "zl", 1)
     ownc = shift(own, "core", 1)
     ownzc = shift(ownz, "core", 1)
-    keep, send = call(
-        product_kernel, sc, [depth, wfull, *xs], [((2, 2, NCOL, 256), F32), ((1664, 128), BF)],
+    keep0, keep1, send, ups = call(
+        product_kernel, sc, [depth, wfull, *xs], [((2, NCOL, 256), F32), ((2, NCOL, 256), F32), ((1664, 128), BF), ((128, 128), BF)],
         scratch=[((8, NCOL, 256), F32)], us=4)
     rcore = shift(send, "core", 1)
-    (zsend,) = call(add_kernel, (), [keep, rcore, *xs], [((896, 128), BF)])
+    (zsend,) = call(add_kernel, (), [keep1, rcore, ups], [((896, 128), BF)])
     rzl = shift(zsend, "zl", 1)
     zout, res0, gkeep, gsend = call(
-        middle_kernel, sc, [keep, rcore, rzl, own, ownz, ownc, ownzc, *xs, labels],
+        middle_kernel, sc, [keep0, rcore, rzl, own, ownz, ownc, ownzc, ups, labels],
         [((896, 128), BF), ((128, 128), BF), ((2, 4, 4, 16, 384), F32), ((2, 4, 4, 16, 384), BF)],
         scratch=[((4, 256, 384), BF), ((256, 128), F32), ((4, 256, 384), F32)], us=5)
 

time: 167 us -> 166 us (level)
  no operation moved by 1% of the time
where the time goes in v3:
time: 166 us
  starting transfers between devices  57.5 us (35%)
  Pallas kernels  54.7 us (33%)
  waiting for transfers between devices  38.6 us (23%)
  local copies, waits for them, and re-layouts  13 us (8%)
    ppermute x36, starting transfers between devices, shift(): return lax.ppermute(x, axis, [(i, (i + k) % n) for i in range(n)])  57.5 us
    pallas_call x15, Pallas kernels, call(): pl.pallas_call(kernel, grid_spec=pltpu.PrefetchScalarGridSpec(num_scalar_...  54.7 us
    ppermute x36, waiting for transfers between devices, shift(): return lax.ppermute(x, axis, [(i, (i + k) % n) for i in range(n)])  38.6 us
    unnamed x84, local copies, waits for them, and re-layouts  9.52 us
  transfers between devices with their start and end apart: 36, of which 17 were waited for; matrix products, arithmetic and copies ran while one was open for 4% of the time, Pallas kernels for 16%

profile of v3, /device:TPU:8, one launch (start us, length us, event | category | flops | bytes accessed | tf_op | source)
XLA Modules:
  0.0 165.7 jit_solution(7646793452511717943)
XLA Ops:
  1.3 2.3 %shard_map.153.b0 = bf16[128,128]{1,0:T(8,128)(2,1)} custom-call(s32[7]{0:T(128)} %stack.31.sc, s32[2]{0:T(128)} %off.19, s32[2]{0:T(128)} %wid.19, bf16[1,128,256]{2,1,0:T(8,128)(2,1)} %pw.1, bf16[1,9,128]{2,1,0:T(8,128)(2,1)} %dw.1, bf16[1,16,256]{2,1,0:T(8,128)(2,1)} %proj.1, f32[1,16]{1,0:T(1,128)} %pwb.1, f32[1,16]{1,0:T(1,128)} %bitcast.26), custom_call_target="tpu_custom_call" | custom-call | flops 1000000000 | bytes 3000000 | tf_op jit(solution)/shard_map/pallas_call | solution.py:482
  3.6 2.8 %collective-permute-start.2 = (bf16[128,128]{1,0:T(8,128)(2,1)}, bf16[128,128]{1,0:T(8,128)(2,1)S(1)}, u32[]{:S(2)}, u32[]{:S(2)}) collective-permute-start(bf16[128,128]{1,0:T(8,128)(2,1)} %shard_map.153.b0), channel_id=1, source_target_pairs={{0,192},{64,0},{128,64},{192,128},{1,193},{65,1},{129,65},{193,129... | collective-permute-start | bytes 98312 | tf_op jit(solution)/shard_map/ppermute | solution.py:27
  8.8 4.6 %shard_map.154 = (bf16[576,128]{1,0:T(8,128)(2,1)}, bf16[576,128]{1,0:T(8,128)(2,1)}, bf16[576,128]{1,0:T(8,128)(2,1)}, bf16[576,128]{1,0:T(8,128)(2,1)}) custom-call(s32[7]{0:T(128)} %stack.31.sc, s32[2]{0:T(128)} %off.19, s32[2]{0:T(128)} %wid.19, bf16[2,16,2,128,128]{4,3,2,1,0:T(8,128)(2,1)} %bitcast.25, bf16[2,8,16,128]{3,2,1,0:T(8,128)(2,1)} %bitcast.24), custom_call_target="tpu_custom_call" | custom-call | flops 5000000000 | bytes 15000000 | tf_op jit(solution)/shard_map/pallas_call | solution.py:482
  14.1 2.3 %shard_map.155.a0 = bf16[368,128]{1,0:T(8,128)(2,1)} custom-call(s32[7]{0:T(128)} %stack.31.sc, s32[2]{0:T(128)} %off.19, s32[2]{0:T(128)} %wid.19, bf16[128,128]{1,0:T(8,128)(2,1)} %shard_map.153.b0, bf16[128,128]{1,0:T(8,128)(2,1)} %copy-done.40, bf16[128,128]{1,0:T(8,128)(2,1)} %copy-done.39, bf16[128,128]{1,0:T(8,128)(2,1)} %copy-done.38), custom_call_target="tpu_custom_call" | custom-call | flops 1000000000 | bytes 3000000 | tf_op jit(solution)/shard_map/pallas_call | solution.py:482
  16.4 6.3 %collective-permute-start.8 = (bf16[368,128]{1,0:T(8,128)(2,1)}, bf16[368,128]{1,0:T(8,128)(2,1)S(1)}, u32[]{:S(2)}, u32[]{:S(2)}) collective-permute-start(bf16[368,128]{1,0:T(8,128)(2,1)} %shard_map.155.a0), channel_id=1, source_target_pairs={{0,12},{4,0},{8,4},{12,8},{1,13},{5,1},{9,5},{13,9},{2,14},{6,2},{... | collective-permute-start | bytes 282632 | tf_op jit(solution)/shard_map/ppermute | solution.py:27
  23.6 2.9 %collective-permute-start.6 = (bf16[368,128]{1,0:T(8,128)(2,1)}, bf16[368,128]{1,0:T(8,128)(2,1)S(1)}, u32[]{:S(2)}, u32[]{:S(2)}) collective-permute-start(bf16[368,128]{1,0:T(8,128)(2,1)} %shard_map.155.a0), channel_id=1, source_target_pairs={{0,4},{4,8},{8,12},{12,0},{1,5},{5,9},{9,13},{13,1},{2,6},{6,10},{... | collective-permute-start | bytes 282632 | tf_op jit(solution)/shard_map/ppermute | solution.py:27
  27.4 2.8 %collective-permute-done.8.a3 = bf16[368,128]{1,0:T(8,128)(2,1)S(1)} collective-permute-done((bf16[368,128]{1,0:T(8,128)(2,1)}, bf16[368,128]{1,0:T(8,128)(2,1)S(1)}, u32[]{:S(2)}, u32[]{:S(2)}) %collective-permute-start.8) | collective-permute-done | bytes 94240 | tf_op jit(solution)/shard_map/ppermute | solution.py:27
  30.2 3.5 %collective-permute-done.7.a2 = bf16[368,128]{1,0:T(8,128)(2,1)S(1)} collective-permute-done((bf16[368,128]{1,0:T(8,128)(2,1)}, bf16[368,128]{1,0:T(8,128)(2,1)S(1)}, u32[]{:S(2)}, u32[]{:S(2)}) %collective-permute-start.7) | collective-permute-done | bytes 94240 | tf_op jit(solution)/shard_map/ppermute | solution.py:27
  34.4 2.6 %collective-permute-start.10 = (bf16[1216,128]{1,0:T(8,128)(2,1)S(1)}, bf16[1216,128]{1,0:T(8,128)(2,1)S(1)}, u32[]{:S(2)}, u32[]{:S(2)}) collective-permute-start(bf16[1216,128]{1,0:T(8,128)(2,1)S(1)} %pad_maximum_fusion.1.q0), channel_id=1, source_target_pairs={{0,32},{16,48},{32,0},{48,16},{1,33},{17,49},{33,1},{49,17},{2,34}... | collective-permute-start | bytes 933896 | tf_op jit(solution)/shard_map/ppermute | solution.py:27
  36.9 1.9 %collective-permute-start.9 = (bf16[1216,128]{1,0:T(8,128)(2,1)S(1)}, bf16[1216,128]{1,0:T(8,128)(2,1)S(1)}, u32[]{:S(2)}, u32[]{:S(2)}) collective-permute-start(bf16[1216,128]{1,0:T(8,128)(2,1)S(1)} %pad_maximum_fusion.1.q0), channel_id=1, source_target_pairs={{0,16},{16,32},{32,48},{48,0},{1,17},{17,33},{33,49},{49,1},{2,18}... | collective-permute-start | bytes 933896 | tf_op jit(solution)/shard_map/ppermute | solution.py:27
  39.0 4.1 %collective-permute-start.4 = (bf16[576,128]{1,0:T(8,128)(2,1)S(1)}, bf16[576,128]{1,0:T(8,128)(2,1)S(1)}, u32[]{:S(2)}, u32[]{:S(2)}) collective-permute-start(bf16[576,128]{1,0:T(8,128)(2,1)S(1)} %copy-done.27), channel_id=1, source_target_pairs={{0,8},{4,12},{8,0},{12,4},{1,9},{5,13},{9,1},{13,5},{2,10},{6,14},... | collective-permute-start | bytes 442376 | tf_op jit(solution)/shard_map/ppermute | solution.py:27
  43.9 3.1 %collective-permute-start.5 = (bf16[576,128]{1,0:T(8,128)(2,1)S(1)}, bf16[576,128]{1,0:T(8,128)(2,1)S(1)}, u32[]{:S(2)}, u32[]{:S(2)}) collective-permute-start(bf16[576,128]{1,0:T(8,128)(2,1)S(1)} %copy-done.26), channel_id=1, source_target_pairs={{0,12},{4,0},{8,4},{12,8},{1,13},{5,1},{9,5},{13,9},{2,14},{6,2},{... | collective-permute-start | bytes 442376 | tf_op jit(solution)/shard_map/ppermute | solution.py:27
  48.9 3.2 %shard_map.156 = (bf16[768,128]{1,0:T(8,128)(2,1)}, bf16[4,4,128,256]{3,2,1,0:T(8,128)(2,1)}) custom-call(s32[7]{0:T(128)} %stack.31.sc, s32[2]{0:T(128)} %off.19, s32[2]{0:T(128)} %wid.19, bf16[1216,128]{1,0:T(8,128)(2,1)} %copy-done.2, bf16[1216,128]{1,0:T(8,128)(2,1)} %copy-done.14, bf16[1216,128]{1,0:T(8,128)(2,1)} %copy-done.13, ...), custom_call_target="tpu_custom_call" | custom-call | flops 1000000000 | bytes 3000000 | tf_op jit(solution)/shard_map/pallas_call | solution.py:482
  52.1 4.6 %collective-permute-done.5.x3 = bf16[576,128]{1,0:T(8,128)(2,1)S(1)} collective-permute-done((bf16[576,128]{1,0:T(8,128)(2,1)S(1)}, bf16[576,128]{1,0:T(8,128)(2,1)S(1)}, u32[]{:S(2)}, u32[]{:S(2)}) %collective-permute-start.5) | collective-permute-done | bytes 147488 | tf_op jit(solution)/shard_map/ppermute | solution.py:27
  57.4 6.1 %shard_map.157 = (bf16[4,8,192,128]{3,2,1,0:T(8,128)(2,1)}, f32[4,4,16,128]{3,2,1,0:T(8,128)}) custom-call(s32[7]{0:T(128)} %stack.31.sc, s32[2]{0:T(128)} %off.19, s32[2]{0:T(128)} %wid.19, bf16[576,128]{1,0:T(8,128)(2,1)} %get-tuple-element.90.x0, bf16[576,128]{1,0:T(8,128)(2,1)} %copy-done.23, bf16[576,128]{1,0:T(8,128)(2,1)} %copy-done.24, ...), custom_call_target="tpu_custom_call" | custom-call | flops 6000000000 | bytes 18000000 | tf_op jit(solution)/shard_map/pallas_call | solution.py:482
  63.6 4.3 %shard_map.158 = (f32[2,192,256]{2,1,0:T(8,128)}, f32[2,192,256]{2,1,0:T(8,128)}, bf16[1664,128]{1,0:T(8,128)(2,1)}, bf16[128,128]{1,0:T(8,128)(2,1)}) custom-call(s32[7]{0:T(128)} %stack.31.sc, s32[2]{0:T(128)} %off.19, s32[2]{0:T(128)} %wid.19, bf16[4,8,192,128]{3,2,1,0:T(8,128)(2,1)} %get-tuple-element.96.depth, ...), custom_call_target="tpu_custom_call" | custom-call | flops 4000000000 | bytes 12000000 | tf_op jit(solution)/shard_map/pallas_call | solution.py:482
  68.0 1.9 %collective-permute-done.12.rcore = bf16[1664,128]{1,0:T(8,128)(2,1)S(1)} collective-permute-done((bf16[1664,128]{1,0:T(8,128)(2,1)}, bf16[1664,128]{1,0:T(8,128)(2,1)S(1)}, u32[]{:S(2)}, u32[]{:S(2)}) %collective-permute-start.12) | collective-permute-done | bytes 426016 | tf_op jit(solution)/shard_map/ppermute | solution.py:27
  70.6 1.8 %shard_map.159 = bf16[896,128]{1,0:T(8,128)(2,1)} custom-call(f32[2,192,256]{2,1,0:T(8,128)} %get-tuple-element.99.keep1, bf16[1664,128]{1,0:T(8,128)(2,1)} %copy-done.7, bf16[128,128]{1,0:T(8,128)(2,1)} %get-tuple-element.100.ups), custom_call_target="tpu_custom_call" | custom-call | flops 1000000000 | bytes 3000000 | tf_op jit(solution)/shard_map/pallas_call | solution.py:482
  72.6 2.6 %collective-permute-done.14.ownz = bf16[768,128]{1,0:T(8,128)(2,1)S(1)} collective-permute-done((bf16[768,128]{1,0:T(8,128)(2,1)S(1)}, bf16[768,128]{1,0:T(8,128)(2,1)S(1)}, u32[]{:S(2)}, u32[]{:S(2)}) %collective-permute-start.14) | collective-permute-done | bytes 196640 | tf_op jit(solution)/shard_map/ppermute | solution.py:27
  75.2 1.4 collective-permute-done.16.ownzc
  76.6 3.7 %collective-permute-done.13.rzl = bf16[896,128]{1,0:T(8,128)(2,1)S(1)} collective-permute-done((bf16[896,128]{1,0:T(8,128)(2,1)}, bf16[896,128]{1,0:T(8,128)(2,1)S(1)}, u32[]{:S(2)}, u32[]{:S(2)}) %collective-permute-start.13) | collective-permute-done | bytes 229408 | tf_op jit(solution)/shard_map/ppermute | solution.py:27
  81.0 4.7 %shard_map.160 = (bf16[896,128]{1,0:T(8,128)(2,1)}, bf16[128,128]{1,0:T(8,128)(2,1)}, f32[2,4,4,16,384]{4,3,2,1,0:T(8,128)}, bf16[2,4,4,16,384]{4,3,2,1,0:T(8,128)(2,1)}) custom-call(s32[7]{0:T(128)} %stack.31.sc, s32[2]{0:T(128)} %off.19, s32[2]{0:T(128)} %wid.19, f32[2,192,256]{2,1,0:T(8,128)} %get-tuple-element.97.keep0, bf16[1664,128]{1,0:T(8,128)(2,1)} %copy-done.7, ...), custom_call_target="tpu_custom_call" | custom-call | flops 5000000000 | bytes 15000000 | tf_op jit(solution)/shard_map/pallas_call | solution.py:482
  86.0 1.0 slice.35
  87.7 5.0 %collective-permute-done.18.zin = bf16[896,128]{1,0:T(8,128)(2,1)S(1)} collective-permute-done((bf16[896,128]{1,0:T(8,128)(2,1)}, bf16[896,128]{1,0:T(8,128)(2,1)S(1)}, u32[]{:S(2)}, u32[]{:S(2)}) %collective-permute-start.18) | collective-permute-done | bytes 229408 | tf_op jit(solution)/shard_map/ppermute | solution.py:27
  93.0 1.6 collective-permute-done.19.cin
  95.4 4.5 %shard_map.161 = (bf16[1280,128]{1,0:T(8,128)(2,1)}, bf16[1280,128]{1,0:T(8,128)(2,1)}, bf16[1280,128]{1,0:T(8,128)(2,1)}, bf16[1280,128]{1,0:T(8,128)(2,1)}, bf16[8,192,256]{2,1,0:T(8,128)(2,1)}) custom-call(s32[7]{0:T(128)} %stack.31.sc, s32[2]{0:T(128)} %off.19, s32[2]{0:T(128)} %wid.19, bf16[4,8,192,128]{3,2,1,0:T(8,128)(2,1)} %get-tuple-element.96.depth, ...), custom_call_target="tpu_custom_call" | custom-call | flops 4000000000 | bytes 12000000 | tf_op jit(solution)/shard_map/pallas_call | solution.py:482
  100.5 1.7 %collective-permute-start.27 = (bf16[1280,128]{1,0:T(8,128)(2,1)}, bf16[1280,128]{1,0:T(8,128)(2,1)S(1)}, u32[]{:S(2)}, u32[]{:S(2)}) collective-permute-start(bf16[1280,128]{1,0:T(8,128)(2,1)} %get-tuple-element.118), channel_id=1, source_target_pairs={{0,64},{64,128},{128,192},{192,0},{1,65},{65,129},{129,193},{193,1... | collective-permute-start | bytes 983048 | tf_op jit(solution)/shard_map/ppermute | solution.py:27
  102.2 2.1 %collective-permute-start.28 = (bf16[1280,128]{1,0:T(8,128)(2,1)}, bf16[1280,128]{1,0:T(8,128)(2,1)S(1)}, u32[]{:S(2)}, u32[]{:S(2)}) collective-permute-start(bf16[1280,128]{1,0:T(8,128)(2,1)} %get-tuple-element.119), channel_id=1, source_target_pairs={{0,128},{64,192},{128,0},{192,64},{1,129},{65,193},{129,1},{193,65... | collective-permute-start | bytes 983048 | tf_op jit(solution)/shard_map/ppermute | solution.py:27
  105.2 1.8 %collective-permute-done.20 = bf16[4,4,16,384]{3,2,1,0:T(8,128)(2,1)S(1)} collective-permute-done((bf16[4,4,16,384]{3,2,1,0:T(8,128)(2,1)S(1)}, bf16[4,4,16,384]{3,2,1,0:T(8,128)(2,1)S(1)}, u32[]{:S(2)}, u32[]{:S(2)}) %collective-permute-start.20) | collective-permute-done | bytes 196640 | tf_op jit(solution)/shard_map/ppermute | solution.py:27
  107.8 9.8 %shard_map.162 = (bf16[768,128]{1,0:T(8,128)(2,1)}, bf16[768,128]{1,0:T(8,128)(2,1)}, bf16[768,128]{1,0:T(8,128)(2,1)}, bf16[768,128]{1,0:T(8,128)(2,1)}) custom-call(s32[7]{0:T(128)} %stack.31.sc, s32[2]{0:T(128)} %off.19, s32[2]{0:T(128)} %wid.19, bf16[576,128]{1,0:T(8,128)(2,1)} %get-tuple-element.90.x0, bf16[576,128]{1,0:T(8,128)(2,1)} %copy-done.23, ...), custom_call_target="tpu_custom_call" | custom-call | flops 10000000000 | bytes 30000000 | tf_op jit(solution)/shard_map/pallas_call | solution.py:482
  117.6 1.7 %collective-permute-start.21 = (bf16[768,128]{1,0:T(8,128)(2,1)}, bf16[768,128]{1,0:T(8,128)(2,1)S(1)}, u32[]{:S(2)}, u32[]{:S(2)}) collective-permute-start(bf16[768,128]{1,0:T(8,128)(2,1)} %get-tuple-element.110), channel_id=1, source_target_pairs={{0,64},{64,128},{128,192},{192,0},{1,65},{65,129},{129,193},{193,1... | collective-permute-start | bytes 589832 | tf_op jit(solution)/shard_map/ppermute | solution.py:27
  119.3 2.1 %collective-permute-start.22 = (bf16[768,128]{1,0:T(8,128)(2,1)}, bf16[768,128]{1,0:T(8,128)(2,1)S(1)}, u32[]{:S(2)}, u32[]{:S(2)}) collective-permute-start(bf16[768,128]{1,0:T(8,128)(2,1)} %get-tuple-element.111), channel_id=1, source_target_pairs={{0,128},{64,192},{128,0},{192,64},{1,129},{65,193},{129,1},{193,65... | collective-permute-start | bytes 589832 | tf_op jit(solution)/shard_map/ppermute | solution.py:27
  123.2 2.1 %shard_map.164 = (f32[256,128]{1,0:T(8,128)}, bf16[512,128]{1,0:T(8,128)(2,1)}, bf16[512,128]{1,0:T(8,128)(2,1)}, bf16[512,128]{1,0:T(8,128)(2,1)}, bf16[512,128]{1,0:T(8,128)(2,1)}) custom-call(bf16[1280,128]{1,0:T(8,128)(2,1)} %get-tuple-element.117.g0, bf16[1280,128]{1,0:T(8,128)(2,1)} %copy-done.9, bf16[1280,128]{1,0:T(8,128)(2,1)} %copy-done.10, ...), custom_call_target="tpu_custom_call" | custom-call | flops 1000000000 | bytes 3000000 | tf_op jit(solution)/shard_map/pallas_call | solution.py:482
  125.3 3.7 %collective-permute-start.30 = (bf16[512,128]{1,0:T(8,128)(2,1)}, bf16[512,128]{1,0:T(8,128)(2,1)S(1)}, u32[]{:S(2)}, u32[]{:S(2)}) collective-permute-start(bf16[512,128]{1,0:T(8,128)(2,1)} %get-tuple-element.122), channel_id=1, source_target_pairs={{0,12},{4,0},{8,4},{12,8},{1,13},{5,1},{9,5},{13,9},{2,14},{6,2},{... | collective-permute-start | bytes 393224 | tf_op jit(solution)/shard_map/ppermute | solution.py:27
  129.0 1.8 %collective-permute-start.31 = (bf16[512,128]{1,0:T(8,128)(2,1)}, bf16[512,128]{1,0:T(8,128)(2,1)S(1)}, u32[]{:S(2)}, u32[]{:S(2)}) collective-permute-start(bf16[512,128]{1,0:T(8,128)(2,1)} %get-tuple-element.123), channel_id=1, source_target_pairs={{0,8},{4,12},{8,0},{12,4},{1,9},{5,13},{9,1},{13,5},{2,10},{6,14},... | collective-permute-start | bytes 393224 | tf_op jit(solution)/shard_map/ppermute | solution.py:27
  130.8 1.2 collective-permute-start.32
  132.8 2.0 %shard_map.163 = (bf16[320,128]{1,0:T(8,128)(2,1)}, bf16[320,128]{1,0:T(8,128)(2,1)}, bf16[320,128]{1,0:T(8,128)(2,1)}, bf16[320,128]{1,0:T(8,128)(2,1)}) custom-call(bf16[768,128]{1,0:T(8,128)(2,1)} %get-tuple-element.109.v0, bf16[768,128]{1,0:T(8,128)(2,1)} %copy-done.17, bf16[768,128]{1,0:T(8,128)(2,1)} %copy-done.18, bf16[768,128]{1,0:T(8,128)(2,1)} %copy-done.19), custom_call_target="tpu_custom_call" | custom-call | flops 1000000000 | bytes 3000000 | tf_op jit(solution)/shard_map/pallas_call | solution.py:482
  134.8 2.9 %collective-permute-start.24 = (bf16[320,128]{1,0:T(8,128)(2,1)}, bf16[320,128]{1,0:T(8,128)(2,1)S(1)}, u32[]{:S(2)}, u32[]{:S(2)}) collective-permute-start(bf16[320,128]{1,0:T(8,128)(2,1)} %get-tuple-element.114), channel_id=1, source_target_pairs={{0,12},{4,0},{8,4},{12,8},{1,13},{5,1},{9,5},{13,9},{2,14},{6,2},{... | collective-permute-start | bytes 245768 | tf_op jit(solution)/shard_map/ppermute | solution.py:27
  137.7 4.2 %collective-permute-start.25 = (bf16[320,128]{1,0:T(8,128)(2,1)}, bf16[320,128]{1,0:T(8,128)(2,1)S(1)}, u32[]{:S(2)}, u32[]{:S(2)}) collective-permute-start(bf16[320,128]{1,0:T(8,128)(2,1)} %get-tuple-element.115), channel_id=1, source_target_pairs={{0,8},{4,12},{8,0},{12,4},{1,9},{5,13},{9,1},{13,5},{2,10},{6,14},... | collective-permute-start | bytes 245768 | tf_op jit(solution)/shard_map/ppermute | solution.py:27
  142.2 3.3 %collective-permute-done.32.h3 = bf16[512,128]{1,0:T(8,128)(2,1)S(1)} collective-permute-done((bf16[512,128]{1,0:T(8,128)(2,1)}, bf16[512,128]{1,0:T(8,128)(2,1)S(1)}, u32[]{:S(2)}, u32[]{:S(2)}) %collective-permute-start.32) | collective-permute-done | bytes 131104 | tf_op jit(solution)/shard_map/ppermute | solution.py:27
  145.5 3.9 %collective-permute-done.25.z2 = bf16[320,128]{1,0:T(8,128)(2,1)S(1)} collective-permute-done((bf16[320,128]{1,0:T(8,128)(2,1)}, bf16[320,128]{1,0:T(8,128)(2,1)S(1)}, u32[]{:S(2)}, u32[]{:S(2)}) %collective-permute-start.25) | collective-permute-done | bytes 81952 | tf_op jit(solution)/shard_map/ppermute | solution.py:27
  150.1 2.0 %shard_map.166 = (f32[320,128]{1,0:T(8,128)}, bf16[320,128]{1,0:T(8,128)(2,1)}) custom-call(bf16[320,128]{1,0:T(8,128)(2,1)} %get-tuple-element.113.z0, bf16[320,128]{1,0:T(8,128)(2,1)} %copy-done.32, bf16[320,128]{1,0:T(8,128)(2,1)} %copy-done.33, bf16[320,128]{1,0:T(8,128)(2,1)} %copy-done.34, f32[256,128]{1,0:T(8,128)} %get-tuple-element.127.gown, ...), custom_call_target="tpu_custom_call" | custom-call | flops 1000000000 | bytes 3000000 | tf_op jit(solution)/shard_map/pallas_call | solution.py:482
  152.1 1.1 collective-permute-start.35
  153.2 2.5 %collective-permute-start.34 = (bf16[320,128]{1,0:T(8,128)(2,1)}, bf16[320,128]{1,0:T(8,128)(2,1)S(1)}, u32[]{:S(2)}, u32[]{:S(2)}) collective-permute-start(bf16[320,128]{1,0:T(8,128)(2,1)} %get-tuple-element.129), channel_id=1, source_target_pairs={{0,32},{16,48},{32,0},{48,16},{1,33},{17,49},{33,1},{49,17},{2,34}... | collective-permute-start | bytes 245768 | tf_op jit(solution)/shard_map/ppermute | solution.py:27
  155.7 2.6 %collective-permute-start.33 = (bf16[320,128]{1,0:T(8,128)(2,1)}, bf16[320,128]{1,0:T(8,128)(2,1)S(1)}, u32[]{:S(2)}, u32[]{:S(2)}) collective-permute-start(bf16[320,128]{1,0:T(8,128)(2,1)} %get-tuple-element.129), channel_id=1, source_target_pairs={{0,16},{16,32},{32,48},{48,0},{1,17},{17,33},{33,49},{49,1},{2,18}... | collective-permute-start | bytes 245768 | tf_op jit(solution)/shard_map/ppermute | solution.py:27
  158.3 3.2 %shard_map.165 = (bf16[2,8,128,128]{3,2,1,0:T(8,128)(2,1)}, bf16[2,32,16,128]{3,2,1,0:T(8,128)(2,1)}) custom-call(s32[7]{0:T(128)} %stack.31.sc, s32[2]{0:T(128)} %off.19, s32[2]{0:T(128)} %wid.19, bf16[320,128]{1,0:T(8,128)(2,1)} %get-tuple-element.113.z0, bf16[320,128]{1,0:T(8,128)(2,1)} %copy-done.32, bf16[320,128]{1,0:T(8,128)(2,1)} %copy-done.33, ...), custom_call_target="tpu_custom_call" | custom-call | flops 3000000000 | bytes 9000000 | tf_op jit(solution)/shard_map/pallas_call | solution.py:482
  161.5 1.7 %copy.18 = bf16[16,2,32,128]{3,2,1,0:T(8,128)(2,1)} copy(bf16[16,2,32,128]{3,0,2,1:T(8,128)(2,1)} %bitcast.23) | data formatting | bytes 524288
  164.0 1.7 %shard_map.167 = (f32[9,1,128]{2,1,0:T(1,128)}, f32[1,128,256]{2,1,0:T(8,128)}, f32[1,16]{1,0:T(1,128)}, f32[1,16,256]{2,1,0:T(8,128)}, f32[1,16]{1,0:T(1,128)}) custom-call(f32[320,128]{1,0:T(8,128)} %get-tuple-element.128.own, bf16[320,128]{1,0:T(8,128)(2,1)} %copy-done.37, bf16[320,128]{1,0:T(8,128)(2,1)} %copy-done.36, bf16[320,128]{1,0:T(8,128)(2,1)} %copy-done.35), custom_call_target="tpu_custom_call" | custom-call | flops 1000000000 | bytes 3000000 | tf_op jit(solution)/shard_map/pallas_call | solution.py:482
  (138 shorter events, 19.8 us)
Async XLA Ops:
  0.6 7.4 %copy-start = (bf16[16,2,32,128]{3,2,1,0:T(8,128)(2,1)S(1)}, bf16[16,2,32,128]{3,2,1,0:T(8,128)(2,1)}, u32[]{:S(2)}) copy-start(bf16[16,2,32,128]{3,2,1,0:T(8,128)(2,1)} %param.19) | copy-start | bytes 786436
  3.6 9.9 %collective-permute-start.2 = (bf16[128,128]{1,0:T(8,128)(2,1)}, bf16[128,128]{1,0:T(8,128)(2,1)S(1)}, u32[]{:S(2)}, u32[]{:S(2)}) collective-permute-start(bf16[128,128]{1,0:T(8,128)(2,1)} %shard_map.153.b0), channel_id=1, source_target_pairs={{0,192},{64,0},{128,64},{192,128},{1,193},{65,1},{129,65},{193,129... | collective-permute-start | bytes 98312 | tf_op jit(solution)/shard_map/ppermute | solution.py:27
  6.3 7.2 %collective-permute-start.1 = (bf16[128,128]{1,0:T(8,128)(2,1)}, bf16[128,128]{1,0:T(8,128)(2,1)S(1)}, u32[]{:S(2)}, u32[]{:S(2)}) collective-permute-start(bf16[128,128]{1,0:T(8,128)(2,1)} %shard_map.153.b0), channel_id=1, source_target_pairs={{0,128},{64,192},{128,0},{192,64},{1,129},{65,193},{129,1},{193,65... | collective-permute-start | bytes 98312 | tf_op jit(solution)/shard_map/ppermute | solution.py:27
  7.1 6.4 %collective-permute-start = (bf16[128,128]{1,0:T(8,128)(2,1)}, bf16[128,128]{1,0:T(8,128)(2,1)S(1)}, u32[]{:S(2)}, u32[]{:S(2)}) collective-permute-start(bf16[128,128]{1,0:T(8,128)(2,1)} %shard_map.153.b0), channel_id=1, source_target_pairs={{0,64},{64,128},{128,192},{192,0},{1,65},{65,129},{129,193},{193,1... | collective-permute-start | bytes 98312 | tf_op jit(solution)/shard_map/ppermute | solution.py:27
  14.1 24.7 %copy-start.28 = (bf16[576,128]{1,0:T(8,128)(2,1)S(1)}, bf16[576,128]{1,0:T(8,128)(2,1)}, u32[]{:S(2)}) copy-start(bf16[576,128]{1,0:T(8,128)(2,1)} %get-tuple-element.84) | copy-start | bytes 442372
  14.1 24.8 %copy-start.27 = (bf16[576,128]{1,0:T(8,128)(2,1)S(1)}, bf16[576,128]{1,0:T(8,128)(2,1)}, u32[]{:S(2)}) copy-start(bf16[576,128]{1,0:T(8,128)(2,1)} %get-tuple-element.85) | copy-start | bytes 442372
  14.1 29.8 %copy-start.26 = (bf16[576,128]{1,0:T(8,128)(2,1)S(1)}, bf16[576,128]{1,0:T(8,128)(2,1)}, u32[]{:S(2)}) copy-start(bf16[576,128]{1,0:T(8,128)(2,1)} %get-tuple-element.86) | copy-start | bytes 442372
  16.4 13.8 %collective-permute-start.8 = (bf16[368,128]{1,0:T(8,128)(2,1)}, bf16[368,128]{1,0:T(8,128)(2,1)S(1)}, u32[]{:S(2)}, u32[]{:S(2)}) collective-permute-start(bf16[368,128]{1,0:T(8,128)(2,1)} %shard_map.155.a0), channel_id=1, source_target_pairs={{0,12},{4,0},{8,4},{12,8},{1,13},{5,1},{9,5},{13,9},{2,14},{6,2},{... | collective-permute-start | bytes 282632 | tf_op jit(solution)/shard_map/ppermute | solution.py:27
  22.7 11.1 %collective-permute-start.7 = (bf16[368,128]{1,0:T(8,128)(2,1)}, bf16[368,128]{1,0:T(8,128)(2,1)S(1)}, u32[]{:S(2)}, u32[]{:S(2)}) collective-permute-start(bf16[368,128]{1,0:T(8,128)(2,1)} %shard_map.155.a0), channel_id=1, source_target_pairs={{0,8},{4,12},{8,0},{12,4},{1,9},{5,13},{9,1},{13,5},{2,10},{6,14},... | collective-permute-start | bytes 282632 | tf_op jit(solution)/shard_map/ppermute | solution.py:27
  23.6 10.2 %collective-permute-start.6 = (bf16[368,128]{1,0:T(8,128)(2,1)}, bf16[368,128]{1,0:T(8,128)(2,1)S(1)}, u32[]{:S(2)}, u32[]{:S(2)}) collective-permute-start(bf16[368,128]{1,0:T(8,128)(2,1)} %shard_map.155.a0), channel_id=1, source_target_pairs={{0,4},{4,8},{8,12},{12,0},{1,5},{5,9},{9,13},{13,1},{2,6},{6,10},{... | collective-permute-start | bytes 282632 | tf_op jit(solution)/shard_map/ppermute | solution.py:27
  30.2 21.8 %copy-start.4 = (bf16[368,128]{1,0:T(8,128)(2,1)}, bf16[368,128]{1,0:T(8,128)(2,1)S(1)}, u32[]{:S(2)}) copy-start(bf16[368,128]{1,0:T(8,128)(2,1)S(1)} %collective-permute-done.8.a3) | copy-start | bytes 282628
  33.8 18.3 %copy-start.5 = (bf16[368,128]{1,0:T(8,128)(2,1)}, bf16[368,128]{1,0:T(8,128)(2,1)S(1)}, u32[]{:S(2)}) copy-start(bf16[368,128]{1,0:T(8,128)(2,1)S(1)} %collective-permute-done.7.a2) | copy-start | bytes 282628
  33.8 18.3 %copy-start.6 = (bf16[368,128]{1,0:T(8,128)(2,1)}, bf16[368,128]{1,0:T(8,128)(2,1)S(1)}, u32[]{:S(2)}) copy-start(bf16[368,128]{1,0:T(8,128)(2,1)S(1)} %collective-permute-done.6.a1) | copy-start | bytes 282628
  33.8 14.3 %copy-start.2 = (bf16[1216,128]{1,0:T(8,128)(2,1)}, bf16[1216,128]{1,0:T(8,128)(2,1)S(1)}, u32[]{:S(2)}) copy-start(bf16[1216,128]{1,0:T(8,128)(2,1)S(1)} %pad_maximum_fusion.1.q0) | copy-start | bytes 933892
  33.8 10.1 %collective-permute-start.11 = (bf16[1216,128]{1,0:T(8,128)(2,1)S(1)}, bf16[1216,128]{1,0:T(8,128)(2,1)S(1)}, u32[]{:S(2)}, u32[]{:S(2)}) collective-permute-start(bf16[1216,128]{1,0:T(8,128)(2,1)S(1)} %pad_maximum_fusion.1.q0), channel_id=1, source_target_pairs={{0,48},{16,0},{32,16},{48,32},{1,49},{17,1},{33,17},{49,33},{2,50}... | collective-permute-start | bytes 933896 | tf_op jit(solution)/shard_map/ppermute | solution.py:27
  34.4 12.9 %collective-permute-start.10 = (bf16[1216,128]{1,0:T(8,128)(2,1)S(1)}, bf16[1216,128]{1,0:T(8,128)(2,1)S(1)}, u32[]{:S(2)}, u32[]{:S(2)}) collective-permute-start(bf16[1216,128]{1,0:T(8,128)(2,1)S(1)} %pad_maximum_fusion.1.q0), channel_id=1, source_target_pairs={{0,32},{16,48},{32,0},{48,16},{1,33},{17,49},{33,1},{49,17},{2,34}... | collective-permute-start | bytes 933896 | tf_op jit(solution)/shard_map/ppermute | solution.py:27
  36.9 11.2 %collective-permute-start.9 = (bf16[1216,128]{1,0:T(8,128)(2,1)S(1)}, bf16[1216,128]{1,0:T(8,128)(2,1)S(1)}, u32[]{:S(2)}, u32[]{:S(2)}) collective-permute-start(bf16[1216,128]{1,0:T(8,128)(2,1)S(1)} %pad_maximum_fusion.1.q0), channel_id=1, source_target_pairs={{0,16},{16,32},{32,48},{48,0},{1,17},{17,33},{33,49},{49,1},{2,18}... | collective-permute-start | bytes 933896 | tf_op jit(solution)/shard_map/ppermute | solution.py:27
  38.8 13.3 %collective-permute-start.3 = (bf16[576,128]{1,0:T(8,128)(2,1)S(1)}, bf16[576,128]{1,0:T(8,128)(2,1)S(1)}, u32[]{:S(2)}, u32[]{:S(2)}) collective-permute-start(bf16[576,128]{1,0:T(8,128)(2,1)S(1)} %copy-done.28), channel_id=1, source_target_pairs={{0,4},{4,8},{8,12},{12,0},{1,5},{5,9},{9,13},{13,1},{2,6},{6,10},{... | collective-permute-start | bytes 442376 | tf_op jit(solution)/shard_map/ppermute | solution.py:27
  39.0 13.2 %collective-permute-start.4 = (bf16[576,128]{1,0:T(8,128)(2,1)S(1)}, bf16[576,128]{1,0:T(8,128)(2,1)S(1)}, u32[]{:S(2)}, u32[]{:S(2)}) collective-permute-start(bf16[576,128]{1,0:T(8,128)(2,1)S(1)} %copy-done.27), channel_id=1, source_target_pairs={{0,8},{4,12},{8,0},{12,4},{1,9},{5,13},{9,1},{13,5},{2,10},{6,14},... | collective-permute-start | bytes 442376 | tf_op jit(solution)/shard_map/ppermute | solution.py:27
  43.9 12.8 %collective-permute-start.5 = (bf16[576,128]{1,0:T(8,128)(2,1)S(1)}, bf16[576,128]{1,0:T(8,128)(2,1)S(1)}, u32[]{:S(2)}, u32[]{:S(2)}) collective-permute-start(bf16[576,128]{1,0:T(8,128)(2,1)S(1)} %copy-done.26), channel_id=1, source_target_pairs={{0,12},{4,0},{8,4},{12,8},{1,13},{5,1},{9,5},{13,9},{2,14},{6,2},{... | collective-permute-start | bytes 442376 | tf_op jit(solution)/shard_map/ppermute | solution.py:27
  67.9 2.0 %collective-permute-start.12 = (bf16[1664,128]{1,0:T(8,128)(2,1)}, bf16[1664,128]{1,0:T(8,128)(2,1)S(1)}, u32[]{:S(2)}, u32[]{:S(2)}) collective-permute-start(bf16[1664,128]{1,0:T(8,128)(2,1)} %get-tuple-element.98), channel_id=1, source_target_pairs={{0,1},{1,0},{2,3},{3,2},{4,5},{5,4},{6,7},{7,6},{8,9},{9,8},{10,11... | collective-permute-start | bytes 1277960 | tf_op jit(solution)/shard_map/ppermute | solution.py:27
  67.9 7.3 %collective-permute-start.14 = (bf16[768,128]{1,0:T(8,128)(2,1)S(1)}, bf16[768,128]{1,0:T(8,128)(2,1)S(1)}, u32[]{:S(2)}, u32[]{:S(2)}) collective-permute-start(bf16[768,128]{1,0:T(8,128)(2,1)S(1)} %copy-done.16), channel_id=1, source_target_pairs={{0,2},{2,0},{1,3},{3,1},{4,6},{6,4},{5,7},{7,5},{8,10},{10,8},{9,1... | collective-permute-start | bytes 589832 | tf_op jit(solution)/shard_map/ppermute | solution.py:27
  72.4 7.9 %collective-permute-start.13 = (bf16[896,128]{1,0:T(8,128)(2,1)}, bf16[896,128]{1,0:T(8,128)(2,1)S(1)}, u32[]{:S(2)}, u32[]{:S(2)}) collective-permute-start(bf16[896,128]{1,0:T(8,128)(2,1)} %shard_map.159), channel_id=1, source_target_pairs={{0,2},{2,0},{1,3},{3,1},{4,6},{6,4},{5,7},{7,5},{8,10},{10,8},{9,1... | collective-permute-start | bytes 688136 | tf_op jit(solution)/shard_map/ppermute | solution.py:27
  72.6 2.6 %collective-permute-start.15 = (bf16[768,128]{1,0:T(8,128)(2,1)S(1)}, bf16[768,128]{1,0:T(8,128)(2,1)S(1)}, u32[]{:S(2)}, u32[]{:S(2)}) collective-permute-start(bf16[768,128]{1,0:T(8,128)(2,1)S(1)} %copy-done.16), channel_id=1, source_target_pairs={{0,1},{1,0},{2,3},{3,2},{4,5},{5,4},{6,7},{7,6},{8,9},{9,8},{10,11... | collective-permute-start | bytes 589832 | tf_op jit(solution)/shard_map/ppermute | solution.py:27
  75.2 5.1 %copy-start.20 = (bf16[768,128]{1,0:T(8,128)(2,1)}, bf16[768,128]{1,0:T(8,128)(2,1)S(1)}, u32[]{:S(2)}) copy-start(bf16[768,128]{1,0:T(8,128)(2,1)S(1)} %collective-permute-done.14.ownz) | copy-start | bytes 589828
  75.2 1.4 collective-permute-start.16
  85.7 7.2 %copy-start.1 = (f32[2,4,4,16,384]{4,3,2,1,0:T(8,128)S(1)}, f32[2,4,4,16,384]{4,3,2,1,0:T(8,128)}, u32[]{:S(2)}) copy-start(f32[2,4,4,16,384]{4,3,2,1,0:T(8,128)} %get-tuple-element.102) | copy-start | bytes 2359300
  85.7 7.0 %collective-permute-start.18 = (bf16[896,128]{1,0:T(8,128)(2,1)}, bf16[896,128]{1,0:T(8,128)(2,1)S(1)}, u32[]{:S(2)}, u32[]{:S(2)}) collective-permute-start(bf16[896,128]{1,0:T(8,128)(2,1)} %get-tuple-element.104.zout), channel_id=1, source_target_pairs={{0,2},{2,0},{1,3},{3,1},{4,6},{6,4},{5,7},{7,5},{8,10},{10,8},{9,1... | collective-permute-start | bytes 688136 | tf_op jit(solution)/shard_map/ppermute | solution.py:27
  86.0 6.9 %collective-permute-start.17 = (bf16[2,4,4,16,384]{4,3,2,1,0:T(8,128)(2,1)}, bf16[2,4,4,16,384]{4,3,2,1,0:T(8,128)(2,1)S(1)}, u32[]{:S(2)}, u32[]{:S(2)}) collective-permute-start(bf16[2,4,4,16,384]{4,3,2,1,0:T(8,128)(2,1)} %get-tuple-element.103), channel_id=1, source_target_pairs={{0,1},{1,0},{2,3},{3,2},{4,5},{5,4},{6,7},{7,6},{8,9},{9,8},{10,11... | collective-permute-start | bytes 1179656 | tf_op jit(solution)/shard_map/ppermute | solution.py:27
  92.8 1.9 %collective-permute-start.19 = (bf16[1664,128]{1,0:T(8,128)(2,1)S(1)}, bf16[1664,128]{1,0:T(8,128)(2,1)S(1)}, u32[]{:S(2)}, u32[]{:S(2)}) collective-permute-start(bf16[1664,128]{1,0:T(8,128)(2,1)S(1)} %pad_maximum_fusion), channel_id=1, source_target_pairs={{0,1},{1,0},{2,3},{3,2},{4,5},{5,4},{6,7},{7,6},{8,9},{9,8},{10,11... | collective-permute-start | bytes 1277960 | tf_op jit(solution)/shard_map/ppermute | solution.py:27
  100.0 7.0 %collective-permute-start.20 = (bf16[4,4,16,384]{3,2,1,0:T(8,128)(2,1)S(1)}, bf16[4,4,16,384]{3,2,1,0:T(8,128)(2,1)S(1)}, u32[]{:S(2)}, u32[]{:S(2)}) collective-permute-start(bf16[4,4,16,384]{3,2,1,0:T(8,128)(2,1)S(1)} %fusion), channel_id=1, source_target_pairs={{0,2},{2,0},{1,3},{3,1},{4,6},{6,4},{5,7},{7,5},{8,10},{10,8},{9,1... | collective-permute-start | bytes 589832 | tf_op jit(solution)/shard_map/ppermute | solution.py:27
  100.5 20.9 %collective-permute-start.27 = (bf16[1280,128]{1,0:T(8,128)(2,1)}, bf16[1280,128]{1,0:T(8,128)(2,1)S(1)}, u32[]{:S(2)}, u32[]{:S(2)}) collective-permute-start(bf16[1280,128]{1,0:T(8,128)(2,1)} %get-tuple-element.118), channel_id=1, source_target_pairs={{0,64},{64,128},{128,192},{192,0},{1,65},{65,129},{129,193},{193,1... | collective-permute-start | bytes 983048 | tf_op jit(solution)/shard_map/ppermute | solution.py:27
  102.2 20.1 %collective-permute-start.28 = (bf16[1280,128]{1,0:T(8,128)(2,1)}, bf16[1280,128]{1,0:T(8,128)(2,1)S(1)}, u32[]{:S(2)}, u32[]{:S(2)}) collective-permute-start(bf16[1280,128]{1,0:T(8,128)(2,1)} %get-tuple-element.119), channel_id=1, source_target_pairs={{0,128},{64,192},{128,0},{192,64},{1,129},{65,193},{129,1},{193,65... | collective-permute-start | bytes 983048 | tf_op jit(solution)/shard_map/ppermute | solution.py:27
  104.3 18.0 %collective-permute-start.29 = (bf16[1280,128]{1,0:T(8,128)(2,1)}, bf16[1280,128]{1,0:T(8,128)(2,1)S(1)}, u32[]{:S(2)}, u32[]{:S(2)}) collective-permute-start(bf16[1280,128]{1,0:T(8,128)(2,1)} %get-tuple-element.120), channel_id=1, source_target_pairs={{0,192},{64,0},{128,64},{192,128},{1,193},{65,1},{129,65},{193,129... | collective-permute-start | bytes 983048 | tf_op jit(solution)/shard_map/ppermute | solution.py:27
  117.6 13.2 %collective-permute-start.21 = (bf16[768,128]{1,0:T(8,128)(2,1)}, bf16[768,128]{1,0:T(8,128)(2,1)S(1)}, u32[]{:S(2)}, u32[]{:S(2)}) collective-permute-start(bf16[768,128]{1,0:T(8,128)(2,1)} %get-tuple-element.110), channel_id=1, source_target_pairs={{0,64},{64,128},{128,192},{192,0},{1,65},{65,129},{129,193},{193,1... | collective-permute-start | bytes 589832 | tf_op jit(solution)/shard_map/ppermute | solution.py:27
  119.3 12.7 %collective-permute-start.22 = (bf16[768,128]{1,0:T(8,128)(2,1)}, bf16[768,128]{1,0:T(8,128)(2,1)S(1)}, u32[]{:S(2)}, u32[]{:S(2)}) collective-permute-start(bf16[768,128]{1,0:T(8,128)(2,1)} %get-tuple-element.111), channel_id=1, source_target_pairs={{0,128},{64,192},{128,0},{192,64},{1,129},{65,193},{129,1},{193,65... | collective-permute-start | bytes 589832 | tf_op jit(solution)/shard_map/ppermute | solution.py:27
  121.4 10.6 %collective-permute-start.23 = (bf16[768,128]{1,0:T(8,128)(2,1)}, bf16[768,128]{1,0:T(8,128)(2,1)S(1)}, u32[]{:S(2)}, u32[]{:S(2)}) collective-permute-start(bf16[768,128]{1,0:T(8,128)(2,1)} %get-tuple-element.112), channel_id=1, source_target_pairs={{0,192},{64,0},{128,64},{192,128},{1,193},{65,1},{129,65},{193,129... | collective-permute-start | bytes 589832 | tf_op jit(solution)/shard_map/ppermute | solution.py:27
  125.3 16.6 %collective-permute-start.30 = (bf16[512,128]{1,0:T(8,128)(2,1)}, bf16[512,128]{1,0:T(8,128)(2,1)S(1)}, u32[]{:S(2)}, u32[]{:S(2)}) collective-permute-start(bf16[512,128]{1,0:T(8,128)(2,1)} %get-tuple-element.122), channel_id=1, source_target_pairs={{0,12},{4,0},{8,4},{12,8},{1,13},{5,1},{9,5},{13,9},{2,14},{6,2},{... | collective-permute-start | bytes 393224 | tf_op jit(solution)/shard_map/ppermute | solution.py:27
  129.0 13.2 %collective-permute-start.31 = (bf16[512,128]{1,0:T(8,128)(2,1)}, bf16[512,128]{1,0:T(8,128)(2,1)S(1)}, u32[]{:S(2)}, u32[]{:S(2)}) collective-permute-start(bf16[512,128]{1,0:T(8,128)(2,1)} %get-tuple-element.123), channel_id=1, source_target_pairs={{0,8},{4,12},{8,0},{12,4},{1,9},{5,13},{9,1},{13,5},{2,10},{6,14},... | collective-permute-start | bytes 393224 | tf_op jit(solution)/shard_map/ppermute | solution.py:27
  130.8 14.7 %collective-permute-start.32 = (bf16[512,128]{1,0:T(8,128)(2,1)}, bf16[512,128]{1,0:T(8,128)(2,1)S(1)}, u32[]{:S(2)}, u32[]{:S(2)}) collective-permute-start(bf16[512,128]{1,0:T(8,128)(2,1)} %get-tuple-element.124), channel_id=1, source_target_pairs={{0,4},{4,8},{8,12},{12,0},{1,5},{5,9},{9,13},{13,1},{2,6},{6,10},{... | collective-permute-start | bytes 393224 | tf_op jit(solution)/shard_map/ppermute | solution.py:27
  134.8 10.7 %collective-permute-start.24 = (bf16[320,128]{1,0:T(8,128)(2,1)}, bf16[320,128]{1,0:T(8,128)(2,1)S(1)}, u32[]{:S(2)}, u32[]{:S(2)}) collective-permute-start(bf16[320,128]{1,0:T(8,128)(2,1)} %get-tuple-element.114), channel_id=1, source_target_pairs={{0,12},{4,0},{8,4},{12,8},{1,13},{5,1},{9,5},{13,9},{2,14},{6,2},{... | collective-permute-start | bytes 245768 | tf_op jit(solution)/shard_map/ppermute | solution.py:27
  137.7 11.7 %collective-permute-start.25 = (bf16[320,128]{1,0:T(8,128)(2,1)}, bf16[320,128]{1,0:T(8,128)(2,1)S(1)}, u32[]{:S(2)}, u32[]{:S(2)}) collective-permute-start(bf16[320,128]{1,0:T(8,128)(2,1)} %get-tuple-element.115), channel_id=1, source_target_pairs={{0,8},{4,12},{8,0},{12,4},{1,9},{5,13},{9,1},{13,5},{2,10},{6,14},... | collective-permute-start | bytes 245768 | tf_op jit(solution)/shard_map/ppermute | solution.py:27
  141.9 7.6 %copy-start.29 = (bf16[512,128]{1,0:T(8,128)(2,1)}, bf16[512,128]{1,0:T(8,128)(2,1)S(1)}, u32[]{:S(2)}) copy-start(bf16[512,128]{1,0:T(8,128)(2,1)S(1)} %collective-permute-done.30.h1) | copy-start | bytes 393220
  141.9 7.6 %collective-permute-start.26 = (bf16[320,128]{1,0:T(8,128)(2,1)}, bf16[320,128]{1,0:T(8,128)(2,1)S(1)}, u32[]{:S(2)}, u32[]{:S(2)}) collective-permute-start(bf16[320,128]{1,0:T(8,128)(2,1)} %get-tuple-element.116), channel_id=1, source_target_pairs={{0,4},{4,8},{8,12},{12,0},{1,5},{5,9},{9,13},{13,1},{2,6},{6,10},{... | collective-permute-start | bytes 245768 | tf_op jit(solution)/shard_map/ppermute | solution.py:27
  142.2 7.2 %copy-start.30 = (bf16[512,128]{1,0:T(8,128)(2,1)}, bf16[512,128]{1,0:T(8,128)(2,1)S(1)}, u32[]{:S(2)}) copy-start(bf16[512,128]{1,0:T(8,128)(2,1)S(1)} %collective-permute-done.31.h2) | copy-start | bytes 393220
  152.1 11.2 %collective-permute-start.35 = (bf16[320,128]{1,0:T(8,128)(2,1)}, bf16[320,128]{1,0:T(8,128)(2,1)S(1)}, u32[]{:S(2)}, u32[]{:S(2)}) collective-permute-start(bf16[320,128]{1,0:T(8,128)(2,1)} %get-tuple-element.129), channel_id=1, source_target_pairs={{0,48},{16,0},{32,16},{48,32},{1,49},{17,1},{33,17},{49,33},{2,50}... | collective-permute-start | bytes 245768 | tf_op jit(solution)/shard_map/ppermute | solution.py:27
  153.2 10.1 %collective-permute-start.34 = (bf16[320,128]{1,0:T(8,128)(2,1)}, bf16[320,128]{1,0:T(8,128)(2,1)S(1)}, u32[]{:S(2)}, u32[]{:S(2)}) collective-permute-start(bf16[320,128]{1,0:T(8,128)(2,1)} %get-tuple-element.129), channel_id=1, source_target_pairs={{0,32},{16,48},{32,0},{48,16},{1,33},{17,49},{33,1},{49,17},{2,34}... | collective-permute-start | bytes 245768 | tf_op jit(solution)/shard_map/ppermute | solution.py:27
  155.7 7.6 %collective-permute-start.33 = (bf16[320,128]{1,0:T(8,128)(2,1)}, bf16[320,128]{1,0:T(8,128)(2,1)S(1)}, u32[]{:S(2)}, u32[]{:S(2)}) collective-permute-start(bf16[320,128]{1,0:T(8,128)(2,1)} %get-tuple-element.129), channel_id=1, source_target_pairs={{0,16},{16,32},{32,48},{48,0},{1,17},{17,33},{33,49},{49,1},{2,18}... | collective-permute-start | bytes 245768 | tf_op jit(solution)/shard_map/ppermute | solution.py:27
  (29 other events, 51.1 us)
